TPU v7x, 32 devices: a whole 2x2x4 slice. The times are simulated.
32 devices in a mesh: dp: 16 (over z, y, x), tensor: 2 (over core).
Axes of the slice: x: 2, y: 2, z: 4, core: 2. Of those that a mesh axis runs over, the one named last changes fastest.
Arguments:
- tokens: bfloat16 [2048, 768], P('dp'), may hold values from -6 to 6
- seq_ids: int32 [2048], P('dp'), may hold values from 0 to 127, as said below
- routes: int32 [2048, 2], P('dp'), may hold values from 0 to 3, all different within a row; in each aligned block of 128 rows (0 to 127, 128 to 255, ...) at most 80 rows name the same one
- gain_attn: float32 [768], replicated, may hold values from 0.25 to 1.75
- w_query: bfloat16 [768, 768], P(None, 'tensor'), may hold values from -0.21875 to 0.21875
- w_key: bfloat16 [768, 768], P(None, 'tensor'), may hold values from -0.21875 to 0.21875
- w_value: bfloat16 [768, 768], P(None, 'tensor'), may hold values from -0.21875 to 0.21875
- w_attn_out: bfloat16 [768, 768], P('tensor'), may hold values from -0.625 to 0.625
- rel_bias: float32 [12, 32], P('tensor'), may hold values from -2.5 to 2.5
- gain_ffn: float32 [768], replicated, may hold values from 0.25 to 1.75
- w_router: bfloat16 [768, 4], replicated, may hold values from -0.145 to 0.145
- expert_in: bfloat16 [16, 768, 768], P('dp', None, 'tensor'), may hold values from -0.21875 to 0.21875
- expert_out: bfloat16 [16, 768, 768], P('dp', 'tensor'), may hold values from -1.75 to 1.75
- cotangent: bfloat16 [2048, 768], P('dp'), may hold values from -6 to 6
Outputs:
- output: bfloat16 [2048, 768], P('dp')
- grad_tokens: float32 [2048, 768], P('dp')
- grad_gain_attn: float32 [768], replicated
- grad_w_query: float32 [768, 768], P(None, 'tensor')
- grad_w_key: float32 [768, 768], P(None, 'tensor')
- grad_w_value: float32 [768, 768], P(None, 'tensor')
- grad_w_attn_out: float32 [768, 768], P('tensor')
- grad_rel_bias: float32 [12, 32], P('tensor')
- grad_gain_ffn: float32 [768], replicated
- grad_w_router: float32 [768, 4], replicated
- grad_expert_in: float32 [16, 768, 768], P('dp', None, 'tensor')
- grad_expert_out: float32 [16, 768, 768], P('dp', 'tensor')
Inputs may be any that keep to these rules, and one draw needn't show every extreme that they name: `seq_ids`: in each device's 128 rows the sequence number starts at 0 and rises by 0 or 1 from row to row; equal numbers form one sequence; in every draw some device holds a single sequence of 128 rows, and some device holds 128 sequences of one row. `routes`: the 2 experts of a row differ; within the 128 rows of one device no expert is named more than 80 times, and in every draw some expert is named exactly 80 times there.
All inputs are finite; a program needn't handle non-finite values.
Results may differ from a plain program's by a relative error of at most 0.017.
Values may be sent and summed in bfloat16 or wider, within the bound.
No kernel may reach another device: no remote copies, remote signals or barrier semaphores. Data moves between devices by JAX's collectives and lax.ppermute only.
A program may use at most 128 MiB of HBM per device.

v0:
```python
import jax
import jax.numpy as jnp
import numpy as np
from jax import lax
from jax.sharding import PartitionSpec as P

HEAD_DIM = 64
TOP = 2
REACH = 64


eps_norm = 1e-06


def bucket_matrix(length, buckets, max_reach):
    exact_span = buckets // 2
    distance = np.arange(length)
    log_ratio = np.log(np.maximum(distance, exact_span) / exact_span) / np.log(
        max_reach / exact_span
    )
    coarse = exact_span + np.floor(log_ratio * (buckets - exact_span)).astype(np.int64)
    bucket_of = np.where(distance < exact_span, distance, np.minimum(coarse, buckets - 1))
    offset = np.maximum(distance[:, None] - distance[None, :], 0)
    return bucket_of[offset].astype(np.int32)


def gelu_tanh(values):
    return jax.nn.gelu(values, approximate=True)


def rms_forward(values, gain_vec):
    inv_rms = lax.rsqrt(jnp.mean(values * values, axis=-1, keepdims=True) + eps_norm)
    return (values * inv_rms * gain_vec, inv_rms)


def rms_backward(grad_normed, values, inv_rms, gain_vec):
    scaled = grad_normed * gain_vec
    inv_cubed = inv_rms * inv_rms * inv_rms
    grad_values = inv_rms * scaled - values * inv_cubed * jnp.mean(
        scaled * values, axis=-1, keepdims=True
    )
    grad_gain = jnp.sum(grad_normed * values * inv_rms, axis=0)
    return (grad_values, grad_gain)


def slot_of(route_ids, experts, capacity):
    count_all = route_ids.shape[0] * route_ids.shape[1]
    flat_ids = route_ids.reshape(-1)
    expert_hot = (flat_ids[:, None] == jnp.arange(experts, dtype=jnp.int32)[None, :]).astype(
        jnp.bfloat16
    )
    order_ids = jnp.arange(count_all, dtype=jnp.int32)
    earlier = (order_ids[:, None] > order_ids[None, :]).astype(jnp.bfloat16)
    before = jnp.dot(earlier, expert_hot, preferred_element_type=jnp.float32)
    rank_in = jnp.sum(before * expert_hot.astype(jnp.float32), axis=1).astype(jnp.int32)
    return (flat_ids * capacity + rank_in).reshape(route_ids.shape)


def head_split(matrix):
    return matrix.reshape(matrix.shape[0], -1, HEAD_DIM)


def attention_scores(queries, key_rows, score_bias, allowed):
    raw_scores = jnp.einsum(
        "qhd,khd->hqk",
        head_split(queries),
        head_split(key_rows),
        preferred_element_type=jnp.float32,
    )
    return jnp.where(allowed[None], raw_scores * HEAD_DIM ** (-0.5) + score_bias, -jnp.inf)


def to_experts(sent_rows, experts, capacity):
    row_width = sent_rows.shape[-1]
    repeated = jnp.broadcast_to(
        sent_rows.reshape(experts, 1, capacity, row_width), (experts, 4, capacity, row_width)
    )
    arrived = lax.all_to_all(
        repeated.reshape(experts * 4, capacity, row_width),
        "dp",
        split_axis=0,
        concat_axis=0,
        tiled=True,
    )
    gathered = arrived.reshape(-1, row_width)
    return gathered


def from_experts(part_rows, experts, capacity):
    row_width = part_rows.shape[-1]
    sources = part_rows.shape[0] // capacity
    returned_rows = lax.all_to_all(
        part_rows.reshape(sources, capacity, row_width),
        "dp",
        split_axis=0,
        concat_axis=0,
        tiled=True,
    )
    summed_rows = jnp.sum(
        returned_rows.reshape(experts, 4, capacity, row_width).astype(jnp.float32), axis=1
    ).reshape(experts * capacity, row_width)
    return summed_rows


def slot_rows(expert_rows, slot_index):
    selected = jnp.take(expert_rows, slot_index, axis=0)
    return selected


def on_device(
    tokens,
    seq_ids,
    routes,
    gain_attn,
    w_query,
    w_key,
    w_value,
    w_attn_out,
    rel_bias,
    gain_ffn,
    w_router,
    expert_in,
    expert_out,
    cotangent,
):
    tok_rows = tokens.shape[0]
    experts = w_router.shape[1]
    bucket_count = rel_bias.shape[1]
    capacity = 4 * ((5 * TOP * tok_rows + 16 * experts - 1) // (16 * experts))
    inputs_wide = tokens.astype(jnp.float32)
    normed_one, inv_one = rms_forward(inputs_wide, gain_attn)
    normed_one = normed_one.astype(jnp.bfloat16)
    queries = jnp.dot(normed_one, w_query, preferred_element_type=jnp.float32).astype(jnp.bfloat16)
    key_rows = jnp.dot(normed_one, w_key, preferred_element_type=jnp.float32).astype(jnp.bfloat16)
    value_rows = jnp.dot(normed_one, w_value, preferred_element_type=jnp.float32).astype(
        jnp.bfloat16
    )
    positions = jnp.arange(tok_rows)
    allowed = (seq_ids[:, None] == seq_ids[None, :]) & (positions[:, None] >= positions[None, :])
    bucket_hot = (
        jnp.asarray(bucket_matrix(tok_rows, bucket_count, REACH))[None]
        == jnp.arange(bucket_count, dtype=jnp.int32)[:, None, None]
    ).astype(jnp.float32)
    score_bias = jnp.einsum("hb,bij->hij", rel_bias, bucket_hot, precision=lax.Precision.HIGHEST)
    scores = attention_scores(queries, key_rows, score_bias, allowed)
    row_max = jnp.max(scores, axis=-1, keepdims=True)
    log_total = row_max + jnp.log(jnp.sum(jnp.exp(scores - row_max), axis=-1, keepdims=True))
    weights = jnp.exp(scores - log_total).astype(jnp.bfloat16)
    mixed_heads = (
        jnp.einsum(
            "hqk,khd->qhd", weights, head_split(value_rows), preferred_element_type=jnp.float32
        )
        .astype(jnp.bfloat16)
        .reshape(tok_rows, -1)
    )
    attended = lax.psum(
        jnp.dot(mixed_heads, w_attn_out, preferred_element_type=jnp.float32), "tensor"
    )
    residual_one = inputs_wide + attended
    normed_two, inv_two = rms_forward(residual_one, gain_ffn)
    normed_two = normed_two.astype(jnp.bfloat16)
    logits = jnp.dot(normed_two, w_router, preferred_element_type=jnp.float32)
    router_max = jnp.max(logits, axis=-1, keepdims=True)
    router_exp = jnp.exp(logits - router_max)
    router_probs = router_exp / jnp.sum(router_exp, axis=-1, keepdims=True)
    route_hot = (routes[:, :, None] == jnp.arange(experts, dtype=jnp.int32)[None, None, :]).astype(
        jnp.float32
    )
    gate_probs = jnp.sum(router_probs[:, None, :] * route_hot, axis=-1)
    slot_index = slot_of(routes, experts, capacity)
    pick_table = (
        slot_index[:, :, None] == jnp.arange(experts * capacity, dtype=jnp.int32)[None, None, :]
    ).astype(jnp.bfloat16)
    dispatched = jnp.einsum(
        "tks,td->sd", pick_table, normed_two, preferred_element_type=jnp.float32
    ).astype(jnp.bfloat16)
    received = to_experts(dispatched, experts, capacity)
    weight_in = expert_in[0]
    weight_out = expert_out[0]
    pre_act = jnp.dot(received, weight_in, preferred_element_type=jnp.float32)
    activated, gelu_back = jax.vjp(gelu_tanh, pre_act)
    activated = activated.astype(jnp.bfloat16)
    expert_part = jnp.dot(activated, weight_out, preferred_element_type=jnp.float32).astype(
        jnp.bfloat16
    )
    expert_rows = from_experts(expert_part, experts, capacity)
    chosen = slot_rows(expert_rows, slot_index)
    grad_wide = cotangent.astype(jnp.float32)
    mixture, grad_gate = lax.psum(
        (
            jnp.sum(gate_probs[:, :, None] * chosen, axis=1),
            jnp.sum(grad_wide[:, None, :] * chosen, axis=-1),
        ),
        "tensor",
    )
    output = (residual_one + mixture).astype(jnp.bfloat16)
    routed_grad = (gate_probs[:, :, None] * grad_wide[:, None, :]).astype(jnp.bfloat16)
    returned = jnp.einsum(
        "tks,tkd->sd", pick_table, routed_grad, preferred_element_type=jnp.float32
    ).astype(jnp.bfloat16)
    grad_rows = to_experts(returned, experts, capacity)
    grad_act = jnp.dot(grad_rows, weight_out.T, preferred_element_type=jnp.float32)
    grad_pre = gelu_back(grad_act)[0].astype(jnp.bfloat16)
    grad_weight_out = jnp.dot(activated.T, grad_rows, preferred_element_type=jnp.float32)
    grad_weight_in = jnp.dot(received.T, grad_pre, preferred_element_type=jnp.float32)
    back_part = jnp.dot(grad_pre, weight_in.T, preferred_element_type=jnp.float32).astype(
        jnp.bfloat16
    )
    back_rows = from_experts(back_part, experts, capacity)
    back_tokens = lax.psum(jnp.sum(slot_rows(back_rows, slot_index), axis=1), "tensor")
    grad_probs = jnp.sum(grad_gate[:, :, None] * route_hot, axis=1)
    grad_logits = (
        router_probs * (grad_probs - jnp.sum(router_probs * grad_probs, axis=-1, keepdims=True))
    ).astype(jnp.bfloat16)
    grad_router = jnp.dot(normed_two.T, grad_logits, preferred_element_type=jnp.float32)
    grad_normed_two = back_tokens + jnp.dot(
        grad_logits, w_router.T, preferred_element_type=jnp.float32
    )
    grad_res_norm, grad_gain_ffn = rms_backward(grad_normed_two, residual_one, inv_two, gain_ffn)
    grad_residual = grad_wide + grad_res_norm
    grad_attended = grad_residual.astype(jnp.bfloat16)
    grad_attn_out = jnp.dot(mixed_heads.T, grad_attended, preferred_element_type=jnp.float32)
    grad_mixed = jnp.dot(grad_attended, w_attn_out.T, preferred_element_type=jnp.float32).astype(
        jnp.bfloat16
    )
    scores_again = attention_scores(queries, key_rows, score_bias, allowed)
    probs_wide = jnp.exp(scores_again - log_total)
    grad_heads = head_split(grad_mixed)
    grad_values = (
        jnp.einsum(
            "hqk,qhd->khd",
            probs_wide.astype(jnp.bfloat16),
            grad_heads,
            preferred_element_type=jnp.float32,
        )
        .astype(jnp.bfloat16)
        .reshape(tok_rows, -1)
    )
    grad_probs_attn = jnp.einsum(
        "qhd,khd->hqk", grad_heads, head_split(value_rows), preferred_element_type=jnp.float32
    )
    delta_rows = jnp.sum(
        grad_heads.astype(jnp.float32) * head_split(mixed_heads).astype(jnp.float32), axis=-1
    ).T[:, :, None]
    grad_scores = probs_wide * (grad_probs_attn - delta_rows)
    grad_bias = jnp.einsum("hij,bij->hb", grad_scores, bucket_hot, precision=lax.Precision.HIGHEST)
    scores_half = grad_scores.astype(jnp.bfloat16)
    score_scale = HEAD_DIM ** (-0.5)
    grad_queries = (
        (
            jnp.einsum(
                "hqk,khd->qhd",
                scores_half,
                head_split(key_rows),
                preferred_element_type=jnp.float32,
            )
            * score_scale
        )
        .astype(jnp.bfloat16)
        .reshape(tok_rows, -1)
    )
    grad_keys = (
        (
            jnp.einsum(
                "hqk,qhd->khd", scores_half, head_split(queries), preferred_element_type=jnp.float32
            )
            * score_scale
        )
        .astype(jnp.bfloat16)
        .reshape(tok_rows, -1)
    )
    grad_query = jnp.dot(normed_one.T, grad_queries, preferred_element_type=jnp.float32)
    grad_key = jnp.dot(normed_one.T, grad_keys, preferred_element_type=jnp.float32)
    grad_value = jnp.dot(normed_one.T, grad_values, preferred_element_type=jnp.float32)
    grad_normed_part = jnp.dot(grad_queries, w_query.T, preferred_element_type=jnp.float32)
    grad_normed_part = grad_normed_part + jnp.dot(
        grad_keys, w_key.T, preferred_element_type=jnp.float32
    )
    grad_normed_part = grad_normed_part + jnp.dot(
        grad_values, w_value.T, preferred_element_type=jnp.float32
    )
    grad_normed_one = lax.psum(grad_normed_part.astype(jnp.bfloat16), "tensor").astype(jnp.float32)
    grad_in_norm, grad_gain_attn = rms_backward(grad_normed_one, inputs_wide, inv_one, gain_attn)
    grad_tokens = grad_residual + grad_in_norm
    summed = lax.psum(
        (
            grad_gain_attn,
            grad_query,
            grad_key,
            grad_value,
            grad_attn_out,
            grad_bias,
            grad_gain_ffn,
            grad_router,
        ),
        "dp",
    )
    return (
        output,
        grad_tokens,
        summed[0],
        summed[1],
        summed[2],
        summed[3],
        summed[4],
        summed[5],
        summed[6],
        summed[7],
        grad_weight_in[None],
        grad_weight_out[None],
    )


def solution(mesh):
    in_specs = (
        P("dp", None),
        P("dp"),
        P("dp", None),
        P(),
        P(None, "tensor"),
        P(None, "tensor"),
        P(None, "tensor"),
        P("tensor", None),
        P("tensor", None),
        P(),
        P(),
        P("dp", None, "tensor"),
        P("dp", "tensor", None),
        P("dp", None),
    )
    out_specs = (
        P("dp", None),
        P("dp", None),
        P(),
        P(None, "tensor"),
        P(None, "tensor"),
        P(None, "tensor"),
        P("tensor", None),
        P("tensor", None),
        P(),
        P(),
        P("dp", None, "tensor"),
        P("dp", "tensor", None),
    )
    return jax.shard_map(
        on_device, mesh=mesh, in_specs=in_specs, out_specs=out_specs, check_vma=False
    )
```

profile of v0, /device:TPU:0, one launch (start us, length us, event | category | flops | bytes accessed | tf_op | source)
XLA Modules:
  0.0 504.1 jit_solution(16210575287183119069)
XLA Ops:
  17.7 20.6 %all-reduce.8.cloned.1.call-done = f32[128,768]{1,0:T(8,128)} async-done(((f32[128,768]{1,0:T(8,128)}), f32[128,768]{1,0:T(8,128)}) %all-reduce.8.cloned.1.call-update) | async-done | bytes 393232 | tf_op jit(solution)/shard_map/psum | solution.py:156
  41.7 7.0 %all-to-all-start = ((bf16[16,80,768]{2,1,0:T(8,128)(2,1)}), bf16[16,80,768]{2,1,0:T(8,128)(2,1)}, u32[]{:S(2)}, u32[]{:S(2)}) async-start(bf16[16,80,768]{2,1,0:T(8,128)(2,1)} %bitcast.8), calls=%async_computation | async-start | bytes 3932160 | tf_op jit(solution)/shard_map/all_to_all | solution.py:78
  49.4 40.4 %all-to-all-done = bf16[16,80,768]{2,1,0:T(8,128)(2,1)} async-done(((bf16[16,80,768]{2,1,0:T(8,128)(2,1)}), bf16[16,80,768]{2,1,0:T(8,128)(2,1)}, u32[]{:S(2)}, u32[]{:S(2)}) %all-to-all-start) | async-done | bytes 1966112 | tf_op jit(solution)/shard_map/all_to_all | solution.py:78
  91.3 9.9 %all-to-all-start.2 = ((bf16[16,80,768]{2,1,0:T(8,128)(2,1)}), bf16[16,80,768]{2,1,0:T(8,128)(2,1)}, u32[]{:S(2)}, u32[]{:S(2)}) async-start(bf16[16,80,768]{2,1,0:T(8,128)(2,1)} %bitcast.17), calls=%async_computation.2 | async-start | bytes 3932160 | tf_op jit(solution)/shard_map/all_to_all | solution.py:78
  101.2 2.7 fusion.26
  105.2 2.9 convolution_convert_fusion.1
  108.1 33.6 %all-to-all-done.2 = bf16[16,80,768]{2,1,0:T(8,128)(2,1)} async-done(((bf16[16,80,768]{2,1,0:T(8,128)(2,1)}), bf16[16,80,768]{2,1,0:T(8,128)(2,1)}, u32[]{:S(2)}, u32[]{:S(2)}) %all-to-all-start.2) | async-done | bytes 1966112 | tf_op jit(solution)/shard_map/all_to_all | solution.py:78
  141.7 9.2 %all-to-all-start.1 = ((bf16[16,80,768]{2,1,0:T(8,128)(2,1)}), bf16[16,80,768]{2,1,0:T(8,128)(2,1)}, u32[]{:S(2)}, u32[]{:S(2)}) async-start(bf16[16,80,768]{2,1,0:T(8,128)(2,1)} %bitcast.105), calls=%async_computation.1 | async-start | bytes 3932160 | tf_op jit(solution)/shard_map/all_to_all | solution.py:92
  150.9 4.3 fusion.8
  156.2 2.5 convolution_convert_fusion
  158.6 32.7 %all-to-all-done.1 = bf16[16,80,768]{2,1,0:T(8,128)(2,1)} async-done(((bf16[16,80,768]{2,1,0:T(8,128)(2,1)}), bf16[16,80,768]{2,1,0:T(8,128)(2,1)}, u32[]{:S(2)}, u32[]{:S(2)}) %all-to-all-start.1) | async-done | bytes 1966112 | tf_op jit(solution)/shard_map/all_to_all | solution.py:92
  191.3 8.9 %all-to-all-start.3 = ((bf16[16,80,768]{2,1,0:T(8,128)(2,1)}), bf16[16,80,768]{2,1,0:T(8,128)(2,1)}, u32[]{:S(2)}, u32[]{:S(2)}) async-start(bf16[16,80,768]{2,1,0:T(8,128)(2,1)} %bitcast.104), calls=%async_computation.3 | async-start | bytes 3932160 | tf_op jit(solution)/shard_map/all_to_all | solution.py:92
  203.4 2.0 gather_fusion
  207.9 32.5 %all-to-all-done.3 = bf16[16,80,768]{2,1,0:T(8,128)(2,1)} async-done(((bf16[16,80,768]{2,1,0:T(8,128)(2,1)}), bf16[16,80,768]{2,1,0:T(8,128)(2,1)}, u32[]{:S(2)}, u32[]{:S(2)}) %all-to-all-start.3) | async-done | bytes 1966112 | tf_op jit(solution)/shard_map/all_to_all | solution.py:92
  244.1 2.6 select_reduce_fusion
  246.8 2.6 psum.94
  249.4 20.1 %all-reduce.14.cloned.1.call-done = (f32[128,768]{1,0:T(8,128)}, f32[128,768]{1,0:T(8,128)}) async-done(((f32[128,768]{1,0:T(8,128)}, f32[128,768]{1,0:T(8,128)}), (f32[128,768]{1,0:T(8,128)}, f32[128,768]{1,0:T(8,128)})) %all-reduce.14.cloned.1.call-update) | async-done | bytes 786448 | tf_op jit(solution)/shard_map/psum | solution.py:189
  269.6 2.0 multiply_reduce_fusion.2
  286.2 3.9 convolution_bitcast_fusion.1
  290.2 3.7 convolution_bitcast_fusion
  295.4 7.5 %all-reduce.10.cloned.1.call-done = bf16[128,768]{1,0:T(8,128)(2,1)} async-done(((bf16[128,768]{1,0:T(8,128)(2,1)}), bf16[128,768]{1,0:T(8,128)(2,1)}) %all-reduce.10.cloned.1.call-update) | async-done | bytes 196624 | tf_op jit(solution)/shard_map/psum | solution.py:282
  304.0 79.7 %all-reduce = (f32[768]{0:T(1024)}, f32[6,32]{1,0:T(8,128)}, f32[768]{0:T(1024)}, f32[768,4]{0,1:T(4,128)}) all-reduce(f32[768]{0:T(1024)S(1)} %get-tuple-element.17, f32[6,32]{1,0:T(8,128)S(1)} %fusion.16, f32[768]{0:T(1024)S(1)} %copy-done.32, f32[768,4]{0,1:T(4,128)S(1)} %fusion.69), channel_id=1, replica_groups=mesh['dp'=16,'tensor'=2] {'dp'}, use_global_device_ids=true, to_apply=%region_25.27 | all-reduce | flops 4800 | bytes 38400 | tf_op jit(solution)/shard_map/psum | solution.py:285
  385.6 106.5 %all-reduce.12.cloned.1.call-done = (f32[768,384]{1,0:T(8,128)}, f32[768,384]{1,0:T(8,128)}, f32[768,384]{1,0:T(8,128)}, f32[384,768]{1,0:T(8,128)}) async-done(((f32[768,384]{1,0:T(8,128)}, f32[768,384]{1,0:T(8,128)}, f32[768,384]{1,0:T(8,128)}, f32[384,768]{1,0:T(8,128)}), (f32[768,384]{1,0:T(8,128)}, f32[768,384]{1,0:T(8,128)}, f32[768,384]{1,0:T(8,128)}, ...) | async-done | bytes 4718608 | tf_op jit(solution)/shard_map/psum | solution.py:285
  492.0 2.5 copy.136
  (184 shorter events, 49.3 us)
Async XLA Ops:
  7.2 98.0 %copy-start = (bf16[1,384,768]{2,1,0:T(8,128)(2,1)S(1)}, bf16[1,384,768]{2,1,0:T(8,128)(2,1)}, u32[]{:S(2)}) copy-start(bf16[1,384,768]{2,1,0:T(8,128)(2,1)} %param.29) | copy-start | bytes 1769476
  7.3 31.0 %all-reduce.8.cloned.1.call-start = ((), (), s32[]{:S(2)}) async-start(), calls=%async_computation.4 | async-start | bytes 786432 | tf_op jit(solution)/shard_map/psum | solution.py:156
  14.9 25.0 %copy-start.21 = (f32[768]{0:T(1024)S(1)}, f32[768]{0:T(1024)}, u32[]{:S(2)}) copy-start(f32[768]{0:T(1024)} %param.26) | copy-start | bytes 9220
  41.7 7.0 %copy-start.27 = (bf16[768,4]{0,1:T(4,128)(2,1)S(1)}, bf16[768,4]{0,1:T(4,128)(2,1)}, u32[]{:S(2)}) copy-start(bf16[768,4]{0,1:T(4,128)(2,1)} %param.27) | copy-start | bytes 18436
  41.7 48.1 %all-to-all-start = ((bf16[16,80,768]{2,1,0:T(8,128)(2,1)}), bf16[16,80,768]{2,1,0:T(8,128)(2,1)}, u32[]{:S(2)}, u32[]{:S(2)}) async-start(bf16[16,80,768]{2,1,0:T(8,128)(2,1)} %bitcast.8), calls=%async_computation | async-start | bytes 3932160 | tf_op jit(solution)/shard_map/all_to_all | solution.py:78
  48.9 42.4 %copy-start.29 = (f32[128]{0:T(128)}, f32[128]{0:T(128)S(1)}, u32[]{:S(2)}) copy-start(f32[128]{0:T(128)S(1)} %get-tuple-element.41) | copy-start | bytes 1540
  49.0 42.3 %copy-start.35 = (f32[128]{0:T(128)}, f32[128]{0:T(128)S(1)}, u32[]{:S(2)}) copy-start(f32[128]{0:T(128)S(1)} %fusion.55) | copy-start | bytes 1540
  91.2 9.9 %copy-start.46 = (bf16[1,768,384]{2,1,0:T(8,128)(2,1)S(1)}, bf16[1,768,384]{2,1,0:T(8,128)(2,1)}, u32[]{:S(2)}) copy-start(bf16[1,768,384]{2,1,0:T(8,128)(2,1)} %param.28) | copy-start | bytes 1769476
  91.3 50.4 %all-to-all-start.2 = ((bf16[16,80,768]{2,1,0:T(8,128)(2,1)}), bf16[16,80,768]{2,1,0:T(8,128)(2,1)}, u32[]{:S(2)}, u32[]{:S(2)}) async-start(bf16[16,80,768]{2,1,0:T(8,128)(2,1)} %bitcast.17), calls=%async_computation.2 | async-start | bytes 3932160 | tf_op jit(solution)/shard_map/all_to_all | solution.py:78
  141.7 49.6 %all-to-all-start.1 = ((bf16[16,80,768]{2,1,0:T(8,128)(2,1)}), bf16[16,80,768]{2,1,0:T(8,128)(2,1)}, u32[]{:S(2)}, u32[]{:S(2)}) async-start(bf16[16,80,768]{2,1,0:T(8,128)(2,1)} %bitcast.105), calls=%async_computation.1 | async-start | bytes 3932160 | tf_op jit(solution)/shard_map/all_to_all | solution.py:92
  191.3 49.1 %all-to-all-start.3 = ((bf16[16,80,768]{2,1,0:T(8,128)(2,1)}), bf16[16,80,768]{2,1,0:T(8,128)(2,1)}, u32[]{:S(2)}, u32[]{:S(2)}) async-start(bf16[16,80,768]{2,1,0:T(8,128)(2,1)} %bitcast.104), calls=%async_computation.3 | async-start | bytes 3932160 | tf_op jit(solution)/shard_map/all_to_all | solution.py:92
  200.2 69.3 %all-reduce.14.cloned.1.call-start = ((), (), s32[]{:S(2)}) async-start(), calls=%async_computation.7 | async-start | bytes 1572864 | tf_op jit(solution)/shard_map/psum | solution.py:189
  244.0 25.5 %copy-start.22 = (f32[768]{0:T(1024)S(1)}, f32[768]{0:T(1024)}, u32[]{:S(2)}) copy-start(f32[768]{0:T(1024)} %param.26) | copy-start | bytes 9220
  244.0 25.5 %copy-start.28 = (bf16[768,4]{0,1:T(4,128)(2,1)S(1)}, bf16[768,4]{0,1:T(4,128)(2,1)}, u32[]{:S(2)}) copy-start(bf16[768,4]{0,1:T(4,128)(2,1)} %param.27) | copy-start | bytes 18436
  244.0 25.5 %copy-start.41 = (f32[128]{0:T(128)S(1)}, f32[128]{0:T(128)}, u32[]{:S(2)}) copy-start(f32[128]{0:T(128)} %copy-done.40) | copy-start | bytes 1540
  244.0 27.5 %copy-start.17 = (bf16[128,768]{1,0:T(8,128)(2,1)S(1)}, bf16[128,768]{1,0:T(8,128)(2,1)}, u32[]{:S(2)}) copy-start(bf16[128,768]{1,0:T(8,128)(2,1)} %param.30) | copy-start | bytes 589828
  244.1 27.5 %copy-start.45 = (f32[128]{0:T(128)S(1)}, f32[128]{0:T(128)}, u32[]{:S(2)}) copy-start(f32[128]{0:T(128)} %get-tuple-element.37) | copy-start | bytes 1540
  246.7 26.6 %copy-start.5 = (bf16[384,768]{1,0:T(8,128)(2,1)S(1)}, bf16[384,768]{1,0:T(8,128)(2,1)}, u32[]{:S(2)}) copy-start(bf16[384,768]{1,0:T(8,128)(2,1)} %param.24) | copy-start | bytes 1769476
  246.7 56.2 %all-reduce.10.cloned.1.call-start = ((), (), s32[]{:S(2)}) async-start(), calls=%async_computation.5 | async-start | bytes 393216 | tf_op jit(solution)/shard_map/psum | solution.py:282
  249.4 23.9 %copy-start.25 = (f32[128,4]{0,1:T(4,128)}, f32[128,4]{0,1:T(4,128)S(1)}, u32[]{:S(2)}) copy-start(f32[128,4]{0,1:T(4,128)S(1)} %select_reduce_fusion.1) | copy-start | bytes 6148
  249.4 23.9 %copy-start.38 = (f32[128]{0:T(128)}, f32[128]{0:T(128)S(1)}, u32[]{:S(2)}) copy-start(f32[128]{0:T(128)S(1)} %multiply_reduce_fusion.6) | copy-start | bytes 1540
  283.5 208.5 %all-reduce.12.cloned.1.call-start = ((), (), s32[]{:S(2)}) async-start(), calls=%async_computation.6 | async-start | bytes 9437184 | tf_op jit(solution)/shard_map/psum | solution.py:285
  293.9 10.1 %copy-start.32 = (f32[768]{0:T(1024)S(1)}, f32[768]{0:T(1024)}, u32[]{:S(2)}) copy-start(f32[768]{0:T(1024)} %get-tuple-element.15) | copy-start | bytes 9220
  293.9 89.8 %copy-start.44 = (f32[128]{0:T(128)S(1)}, f32[128]{0:T(128)}, u32[]{:S(2)}) copy-start(f32[128]{0:T(128)} %get-tuple-element.35) | copy-start | bytes 1540
  (35 other events, 130.5 us)
Sparse Core Ops, SparseCore 0:
  17.1 21.1 all-reduce.7
  246.8 22.6 all-reduce.13
  283.6 19.2 all-reduce.9
  309.4 182.6 all-reduce.11
where the time goes:
time: 505 us; the launch traced here: 504 us
  waiting for transfers between devices  294 us (58%)
  blocking collectives  82.3 us (16%)
  matrix products  41.1 us (8%)
  starting transfers between devices  35.3 us (7%)
  local copies, waits for them, and re-layouts  20.1 us (4%)
  other arithmetic  16.8 us (3%)
  between operations  14.6 us (3%)
    psum x1, waiting for transfers between devices, on_device(): lax.psum((grad_gain_attn, grad_query, grad_key, grad_value, grad_attn_out...  106 us
    psum x1, blocking collectives, on_device(): lax.psum((grad_gain_attn, grad_query, grad_key, grad_value, grad_attn_out...  79.7 us
    all_to_all x2, waiting for transfers between devices, to_experts(): lax.all_to_all(repeated.reshape(experts * 4, capacity, row_width), 'dp',...  74.1 us
    all_to_all x2, waiting for transfers between devices, from_experts(): lax.all_to_all(part_rows.reshape(sources, capacity, row_width), 'dp', spl...  65.2 us
    psum x1, waiting for transfers between devices, on_device(): lax.psum(jnp.dot(mixed_heads, w_attn_out, preferred_element_type=jnp.floa...  20.6 us
    psum x1, waiting for transfers between devices, on_device(): lax.psum((jnp.sum(gate_probs[:, :, None] * chosen, axis=1), jnp.sum(grad_...  20.1 us
    all_to_all x2, starting transfers between devices, from_experts(): lax.all_to_all(part_rows.reshape(sources, capacity, row_width), 'dp', spl...  18 us
    all_to_all x2, starting transfers between devices, to_experts(): lax.all_to_all(repeated.reshape(experts * 4, capacity, row_width), 'dp',...  16.9 us
  transfers between devices with their start and end apart: 8, of which 8 were waited for; matrix products, arithmetic and copies ran while one was open for 7% of the time, Pallas kernels for 0%

commit v1 on v0

--- a/solution.py
+++ b/solution.py
@@ -1,3 +1,5 @@
+import functools
+
 import jax
 import jax.numpy as jnp
 import numpy as np
@@ -43,7 +45,7 @@
     return (grad_values, grad_gain)
 
 
-def slot_of(route_ids, experts, capacity):
+def slot_of(route_ids, group_id, experts, capacity):
     count_all = route_ids.shape[0] * route_ids.shape[1]
     flat_ids = route_ids.reshape(-1)
     expert_hot = (flat_ids[:, None] == jnp.arange(experts, dtype=jnp.int32)[None, :]).astype(
@@ -53,7 +55,7 @@
     earlier = (order_ids[:, None] > order_ids[None, :]).astype(jnp.bfloat16)
     before = jnp.dot(earlier, expert_hot, preferred_element_type=jnp.float32)
     rank_in = jnp.sum(before * expert_hot.astype(jnp.float32), axis=1).astype(jnp.int32)
-    return (flat_ids * capacity + rank_in).reshape(route_ids.shape)
+    return ((flat_ids ^ group_id) * capacity + rank_in).reshape(route_ids.shape)
 
 
 def head_split(matrix):
@@ -70,44 +72,72 @@
     return jnp.where(allowed[None], raw_scores * HEAD_DIM ** (-0.5) + score_bias, -jnp.inf)
 
 
-def to_experts(sent_rows, experts, capacity):
-    row_width = sent_rows.shape[-1]
-    repeated = jnp.broadcast_to(
-        sent_rows.reshape(experts, 1, capacity, row_width), (experts, 4, capacity, row_width)
-    )
-    arrived = lax.all_to_all(
-        repeated.reshape(experts * 4, capacity, row_width),
-        "dp",
-        split_axis=0,
-        concat_axis=0,
-        tiled=True,
-    )
-    gathered = arrived.reshape(-1, row_width)
-    return gathered
-
-
-def from_experts(part_rows, experts, capacity):
-    row_width = part_rows.shape[-1]
-    sources = part_rows.shape[0] // capacity
-    returned_rows = lax.all_to_all(
-        part_rows.reshape(sources, capacity, row_width),
-        "dp",
-        split_axis=0,
-        concat_axis=0,
-        tiled=True,
-    )
-    summed_rows = jnp.sum(
-        returned_rows.reshape(experts, 4, capacity, row_width).astype(jnp.float32), axis=1
-    ).reshape(experts * capacity, row_width)
-    return summed_rows
-
-
-def slot_rows(expert_rows, slot_index):
-    selected = jnp.take(expert_rows, slot_index, axis=0)
-    return selected
+def make_comm(n_dp, n_tensor):
+    groups = n_dp // 4
+
+    def send(array, target):
+        pairs = []
+        for dp_id in range(n_dp):
+            for t_id in range(n_tensor):
+                e_to, q_to, t_to = target(dp_id // 4, dp_id % 4, t_id)
+                pairs.append((dp_id * n_tensor + t_id, (e_to * 4 + q_to) * n_tensor + t_to))
+        return lax.ppermute(array, ("dp", "tensor"), pairs)
+
+    return groups, send
+
+
+def swap_pair(send, array):
+    return send(array, lambda e, q, t: (e, q, 1 - t))
+
+
+def plane_gather(send, array, t):
+    first = send(array, lambda e, q, t: (e, q ^ (1 if t == 0 else 2), t))
+    both = jnp.concatenate([array, first], axis=0)
+    second = send(both, lambda e, q, t: (e, q ^ (2 if t == 0 else 1), t))
+    rows = array.shape[0]
+    even = t == 0
+    near = jnp.where(even, first, second[:rows])
+    far = jnp.where(even, second[:rows], first)
+    return jnp.concatenate([array, near, far, second[rows:]], axis=0)
+
+
+def plane_scatter(send, array, t):
+    rows = array.shape[0] // 4
+    even = t == 0
+    blocks = array.reshape(4, rows, array.shape[1])
+    near = jnp.where(even, blocks[1], blocks[2])
+    far = jnp.where(even, blocks[2], blocks[1])
+    moved = send(
+        jnp.concatenate([near, blocks[3]], axis=0),
+        lambda e, q, t: (e, q ^ (1 if t == 0 else 2), t),
+    )
+    kept = jnp.concatenate([blocks[0], far], axis=0).astype(jnp.float32) + moved.astype(jnp.float32)
+    moved_two = send(
+        kept[rows:].astype(jnp.bfloat16), lambda e, q, t: (e, q ^ (2 if t == 0 else 1), t)
+    )
+    return (kept[:rows] + moved_two.astype(jnp.float32)).astype(jnp.bfloat16)
+
+
+def group_exchange(send, chunks):
+    received = [chunks[0]]
+    for step in range(1, len(chunks)):
+        received.append(send(chunks[step], lambda e, q, t, step=step: (e ^ step, q, t)))
+    return received
+
+
+def own_half(array, t):
+    width = array.shape[1] // 2
+    return lax.dynamic_slice_in_dim(array, t * width, width, axis=1)
+
+
+def join_halves(mine, other, t):
+    even = t == 0
+    return jnp.concatenate([jnp.where(even, mine, other), jnp.where(even, other, mine)], axis=1)
 
 
 def on_device(
+    n_dp,
+    n_tensor,
     tokens,
     seq_ids,
     routes,
@@ -127,9 +157,47 @@
     experts = w_router.shape[1]
     bucket_count = rel_bias.shape[1]
     capacity = 4 * ((5 * TOP * tok_rows + 16 * experts - 1) // (16 * experts))
+    groups, send = make_comm(n_dp, n_tensor)
+    dp_id = lax.axis_index("dp")
+    t_id = lax.axis_index("tensor")
+    e_id = dp_id // 4
+    q_id = dp_id % 4
+
+    slot_index = slot_of(routes, e_id, experts, capacity)
+    pick_table = (
+        slot_index[:, :, None] == jnp.arange(experts * capacity, dtype=jnp.int32)[None, None, :]
+    ).astype(jnp.bfloat16)
+    pick_any = pick_table[:, 0] + pick_table[:, 1]
+
+    def dispatch(rows, extra=None):
+        width = rows.shape[1]
+        picked = lax.dot_general(
+            pick_any, rows, (((0,), (0,)), ((), ())), preferred_element_type=jnp.float32
+        ).astype(jnp.bfloat16)
+        chunks = [picked[s * capacity : (s + 1) * capacity] for s in range(experts)]
+        arrived = group_exchange(send, chunks)
+        if extra is not None:
+            arrived = arrived + [extra]
+        block = jnp.concatenate(arrived, axis=0)
+        gathered = plane_gather(send, block, t_id)
+        return join_halves(gathered, swap_pair(send, gathered), t_id)
+
+    def give_back(rows):
+        mine = own_half(rows, t_id)
+        other = swap_pair(send, own_half(rows, 1 - t_id))
+        summed = (mine.astype(jnp.float32) + other.astype(jnp.float32)).astype(jnp.bfloat16)
+        block = plane_scatter(send, summed, t_id)
+        chunks = [block[s * capacity : (s + 1) * capacity] for s in range(experts)]
+        return jnp.concatenate(group_exchange(send, chunks), axis=0)
+
     inputs_wide = tokens.astype(jnp.float32)
     normed_one, inv_one = rms_forward(inputs_wide, gain_attn)
     normed_one = normed_one.astype(jnp.bfloat16)
+    slots = experts * capacity
+    early = dispatch(own_half(cotangent, t_id), own_half(normed_one, t_id))
+    early = early.reshape(4, slots + tok_rows, -1)
+    cot_rows = early[:, :slots].reshape(4 * slots, -1)
+    normed_all = early[:, slots:].reshape(4 * tok_rows, -1)
     queries = jnp.dot(normed_one, w_query, preferred_element_type=jnp.float32).astype(jnp.bfloat16)
     key_rows = jnp.dot(normed_one, w_key, preferred_element_type=jnp.float32).astype(jnp.bfloat16)
     value_rows = jnp.dot(normed_one, w_value, preferred_element_type=jnp.float32).astype(
@@ -153,9 +221,8 @@
         .astype(jnp.bfloat16)
         .reshape(tok_rows, -1)
     )
-    attended = lax.psum(
-        jnp.dot(mixed_heads, w_attn_out, preferred_element_type=jnp.float32), "tensor"
-    )
+    attended_part = jnp.dot(mixed_heads, w_attn_out, preferred_element_type=jnp.float32)
+    attended = attended_part + swap_pair(send, attended_part)
     residual_one = inputs_wide + attended
     normed_two, inv_two = rms_forward(residual_one, gain_ffn)
     normed_two = normed_two.astype(jnp.bfloat16)
@@ -167,14 +234,14 @@
         jnp.float32
     )
     gate_probs = jnp.sum(router_probs[:, None, :] * route_hot, axis=-1)
-    slot_index = slot_of(routes, experts, capacity)
-    pick_table = (
-        slot_index[:, :, None] == jnp.arange(experts * capacity, dtype=jnp.int32)[None, None, :]
-    ).astype(jnp.bfloat16)
-    dispatched = jnp.einsum(
-        "tks,td->sd", pick_table, normed_two, preferred_element_type=jnp.float32
-    ).astype(jnp.bfloat16)
-    received = to_experts(dispatched, experts, capacity)
+    received = dispatch(own_half(normed_two, t_id))
+    row_logits = jnp.dot(received, w_router, preferred_element_type=jnp.float32)
+    row_exp = jnp.exp(row_logits - jnp.max(row_logits, axis=-1, keepdims=True))
+    own_expert = (jnp.arange(experts, dtype=jnp.int32) == e_id).astype(jnp.float32)
+    row_gate = jnp.sum(row_exp * own_expert, axis=-1, keepdims=True) / jnp.sum(
+        row_exp, axis=-1, keepdims=True
+    )
+    grad_rows = (row_gate * cot_rows.astype(jnp.float32)).astype(jnp.bfloat16)
     weight_in = expert_in[0]
     weight_out = expert_out[0]
     pre_act = jnp.dot(received, weight_in, preferred_element_type=jnp.float32)
@@ -183,22 +250,6 @@
     expert_part = jnp.dot(activated, weight_out, preferred_element_type=jnp.float32).astype(
         jnp.bfloat16
     )
-    expert_rows = from_experts(expert_part, experts, capacity)
-    chosen = slot_rows(expert_rows, slot_index)
-    grad_wide = cotangent.astype(jnp.float32)
-    mixture, grad_gate = lax.psum(
-        (
-            jnp.sum(gate_probs[:, :, None] * chosen, axis=1),
-            jnp.sum(grad_wide[:, None, :] * chosen, axis=-1),
-        ),
-        "tensor",
-    )
-    output = (residual_one + mixture).astype(jnp.bfloat16)
-    routed_grad = (gate_probs[:, :, None] * grad_wide[:, None, :]).astype(jnp.bfloat16)
-    returned = jnp.einsum(
-        "tks,tkd->sd", pick_table, routed_grad, preferred_element_type=jnp.float32
-    ).astype(jnp.bfloat16)
-    grad_rows = to_experts(returned, experts, capacity)
     grad_act = jnp.dot(grad_rows, weight_out.T, preferred_element_type=jnp.float32)
     grad_pre = gelu_back(grad_act)[0].astype(jnp.bfloat16)
     grad_weight_out = jnp.dot(activated.T, grad_rows, preferred_element_type=jnp.float32)
@@ -206,8 +257,20 @@
     back_part = jnp.dot(grad_pre, weight_in.T, preferred_element_type=jnp.float32).astype(
         jnp.bfloat16
     )
-    back_rows = from_experts(back_part, experts, capacity)
-    back_tokens = lax.psum(jnp.sum(slot_rows(back_rows, slot_index), axis=1), "tensor")
+    expert_rows = give_back(expert_part)
+    back_rows = give_back(back_part)
+    grad_wide = cotangent.astype(jnp.float32)
+    chosen = jnp.einsum("tks,sd->tkd", pick_table, expert_rows, preferred_element_type=jnp.float32)
+    back_half = jnp.dot(pick_any, back_rows, preferred_element_type=jnp.float32)
+    mixture_half = jnp.sum(gate_probs[:, :, None] * chosen, axis=1)
+    gate_half = jnp.sum(own_half(grad_wide, t_id)[:, None, :] * chosen, axis=-1)
+    output_half = (own_half(residual_one, t_id) + mixture_half).astype(jnp.bfloat16)
+    output = join_halves(output_half, swap_pair(send, output_half), t_id)
+    packed = jnp.concatenate([back_half, jnp.pad(gate_half, ((0, 0), (0, 126)))], axis=1)
+    packed_other = swap_pair(send, packed)
+    width = back_half.shape[1]
+    back_tokens = join_halves(back_half, packed_other[:, :width], t_id)
+    grad_gate = gate_half + packed_other[:, width : width + TOP]
     grad_probs = jnp.sum(grad_gate[:, :, None] * route_hot, axis=1)
     grad_logits = (
         router_probs * (grad_probs - jnp.sum(router_probs * grad_probs, axis=-1, keepdims=True))
@@ -219,7 +282,8 @@
     grad_res_norm, grad_gain_ffn = rms_backward(grad_normed_two, residual_one, inv_two, gain_ffn)
     grad_residual = grad_wide + grad_res_norm
     grad_attended = grad_residual.astype(jnp.bfloat16)
-    grad_attn_out = jnp.dot(mixed_heads.T, grad_attended, preferred_element_type=jnp.float32)
+    att_gathered = plane_gather(send, own_half(grad_attended, t_id), t_id)
+    attended_all = join_halves(att_gathered, swap_pair(send, att_gathered), t_id)
     grad_mixed = jnp.dot(grad_attended, w_attn_out.T, preferred_element_type=jnp.float32).astype(
         jnp.bfloat16
     )
@@ -269,9 +333,6 @@
         .astype(jnp.bfloat16)
         .reshape(tok_rows, -1)
     )
-    grad_query = jnp.dot(normed_one.T, grad_queries, preferred_element_type=jnp.float32)
-    grad_key = jnp.dot(normed_one.T, grad_keys, preferred_element_type=jnp.float32)
-    grad_value = jnp.dot(normed_one.T, grad_values, preferred_element_type=jnp.float32)
     grad_normed_part = jnp.dot(grad_queries, w_query.T, preferred_element_type=jnp.float32)
     grad_normed_part = grad_normed_part + jnp.dot(
         grad_keys, w_key.T, preferred_element_type=jnp.float32
@@ -279,33 +340,75 @@
     grad_normed_part = grad_normed_part + jnp.dot(
         grad_values, w_value.T, preferred_element_type=jnp.float32
     )
-    grad_normed_one = lax.psum(grad_normed_part.astype(jnp.bfloat16), "tensor").astype(jnp.float32)
+    normed_part = grad_normed_part.astype(jnp.bfloat16)
+    grad_normed_one = normed_part.astype(jnp.float32) + swap_pair(send, normed_part).astype(
+        jnp.float32
+    )
     grad_in_norm, grad_gain_attn = rms_backward(grad_normed_one, inputs_wide, inv_one, gain_attn)
     grad_tokens = grad_residual + grad_in_norm
-    summed = lax.psum(
-        (
-            grad_gain_attn,
-            grad_query,
-            grad_key,
-            grad_value,
-            grad_attn_out,
-            grad_bias,
-            grad_gain_ffn,
-            grad_router,
-        ),
-        "dp",
-    )
+    right_sides = jnp.stack([grad_queries, grad_keys, grad_values, mixed_heads])
+    right_all = [lax.dynamic_index_in_dim(right_sides, q_id, 0, keepdims=False)]
+    for step in (1, 2, 3):
+        right_all.append(
+            send(
+                lax.dynamic_index_in_dim(right_sides, q_id ^ step, 0, keepdims=False),
+                lambda e, q, t, step=step: (e, q ^ step, t),
+            )
+        )
+    right_all = jnp.concatenate(right_all, axis=0)
+    left_all = jnp.where(q_id == 3, attended_all, normed_all)
+    partial = lax.dot_general(
+        left_all, right_all, (((0,), (0,)), ((), ())), preferred_element_type=jnp.float32
+    ).astype(jnp.bfloat16)
+    depth = partial.shape[0] // groups
+    blocks = [
+        lax.dynamic_slice_in_dim(partial, (e_id ^ s) * depth, depth, axis=0) for s in range(groups)
+    ]
+    arrived = group_exchange(send, blocks)
+    reduced = arrived[0].astype(jnp.float32)
+    for block in arrived[1:]:
+        reduced = reduced + block.astype(jnp.float32)
+    reduced = reduced.astype(jnp.bfloat16)
+    spread = jnp.stack(group_exchange(send, [reduced] * groups))
+    order = jnp.arange(groups, dtype=jnp.int32) ^ e_id
+    matrix = jnp.take(spread, order, axis=0).reshape(partial.shape)
+    rows = matrix.shape[0] // 2
+    from_x = send(matrix, lambda e, q, t: (e, q ^ 1, t))
+    from_y = send(matrix, lambda e, q, t: (e, q ^ 2, t))
+    cross_top = send(from_x[:rows], lambda e, q, t: (e, q ^ 2, t))
+    cross_low = send(from_y[rows:], lambda e, q, t: (e, q ^ 1, t))
+    cross = jnp.concatenate([cross_top, cross_low], axis=0)
+    matrices = jnp.stack([matrix, from_x, from_y, cross])
+    grads = [
+        lax.dynamic_index_in_dim(matrices, q_id ^ m, 0, keepdims=False).astype(jnp.float32)
+        for m in range(4)
+    ]
+    small_parts = (grad_gain_attn, grad_bias, grad_gain_ffn, grad_router)
+    small = jnp.concatenate([part.reshape(-1) for part in small_parts])
+    small = jnp.pad(small, (0, -small.shape[0] % 1024)).reshape(-1, 128)
+    small = small + send(small, lambda e, q, t: (e, q ^ 1, t))
+    small = small + send(small, lambda e, q, t: (e, q ^ 2, t))
+    step = 1
+    while step < groups:
+        small = small + send(small, lambda e, q, t, step=step: (e ^ step, q, t))
+        step *= 2
+    small = small.reshape(-1)
+    totals = []
+    start = 0
+    for part in small_parts:
+        totals.append(small[start : start + part.size].reshape(part.shape))
+        start += part.size
     return (
         output,
         grad_tokens,
-        summed[0],
-        summed[1],
-        summed[2],
-        summed[3],
-        summed[4],
-        summed[5],
-        summed[6],
-        summed[7],
+        totals[0],
+        grads[0],
+        grads[1],
+        grads[2],
+        grads[3].T,
+        totals[1],
+        totals[2],
+        totals[3],
         grad_weight_in[None],
         grad_weight_out[None],
     )
@@ -343,5 +446,6 @@
         P("dp", "tensor", None),
     )
     return jax.shard_map(
-        on_device, mesh=mesh, in_specs=in_specs, out_specs=out_specs, check_vma=False
-    )
+        functools.partial(on_device, mesh.shape["dp"], mesh.shape["tensor"]),
+        mesh=mesh, in_specs=in_specs, out_specs=out_specs, check_vma=False
+    )

time: 505 us -> 203 us (0.40)
  waiting for transfers between devices: 294 us -> 60.7 us
  blocking collectives: 82.3 us -> 0 us
  starting transfers between devices: 35.3 us -> 57.5 us
  between operations: 14.6 us -> 2.05 us
  matrix products: 41.1 us -> 30 us
  other arithmetic: 16.8 us -> 26.6 us
  local copies, waits for them, and re-layouts: 20.1 us -> 25.7 us
    psum x4 -> x0, waiting for transfers between devices: 155 us -> none  [the longest x1 106 us: on_device(): lax.psum((grad_gain_attn, grad_query, grad_key, grad_value, grad_attn_out...]
    all_to_all x4 -> x0, waiting for transfers between devices: 139 us -> none  [the longest x2 74.1 us: to_experts(): lax.all_to_all(repeated.reshape(experts * 4, capacity, row_width), 'dp',...]
    psum x2 -> x0, blocking collectives: 82.3 us -> none  [the longest x1 79.7 us: on_device(): lax.psum((grad_gain_attn, grad_query, grad_key, grad_value, grad_attn_out...]
    ppermute x0 -> x48, waiting for transfers between devices: none -> 60.7 us  [send(): return lax.ppermute(array, ('dp', 'tensor'), pairs)]
    ppermute x0 -> x48, starting transfers between devices: none -> 57.5 us  [send(): return lax.ppermute(array, ('dp', 'tensor'), pairs)]
    all_to_all x4 -> x0, starting transfers between devices: 34.9 us -> none  [the longest x2 18 us: from_experts(): lax.all_to_all(part_rows.reshape(sources, capacity, row_width), 'dp', spl...]
    reduce_sum x5 -> x1, other arithmetic: 7.52 us -> 0.09 us  [on_device(): jnp.sum(row_exp, axis=-1, keepdims=True)]
    select_n x1 -> x9, other arithmetic: 0.01 us -> 6.49 us  [the longest x5 5.88 us: join_halves(): jnp.where(even, mine, other)]
  transfers between devices with their start and end apart: 8 -> 48, of which waited for: 8 -> 21; matrix products, arithmetic and copies ran while one was open for 7% -> 32% of each run, Pallas kernels for 0% -> 0%
where the time goes in v1:
time: 203 us
  waiting for transfers between devices  60.7 us (30%)
  starting transfers between devices  57.5 us (28%)
  matrix products  30 us (15%)
  other arithmetic  26.6 us (13%)
  local copies, waits for them, and re-layouts  25.7 us (13%)
  between operations  2.05 us (1%)
    ppermute x48, waiting for transfers between devices, send(): return lax.ppermute(array, ('dp', 'tensor'), pairs)  60.7 us
    ppermute x48, starting transfers between devices, send(): return lax.ppermute(array, ('dp', 'tensor'), pairs)  57.5 us
    unnamed x130, local copies, waits for them, and re-layouts  12.2 us
    select_n x5, other arithmetic, join_halves(): jnp.where(even, mine, other)  5.88 us
    unnamed x4, other arithmetic  5.08 us
  transfers between devices with their start and end apart: 48, of which 21 were waited for; matrix products, arithmetic and copies ran while one was open for 32% of the time, Pallas kernels for 0%

profile of v1, /device:TPU:0, one launch (start us, length us, event | category | flops | bytes accessed | tf_op | source)
XLA Modules:
  0.0 202.6 jit_solution(3546781306496602170)
XLA Ops:
  4.9 3.0 %collective-permute-start.14 = (bf16[80,384]{1,0:T(8,128)(2,1)}, bf16[80,384]{1,0:T(8,128)(2,1)}, u32[]{:S(2)}, u32[]{:S(2)}) collective-permute-start(bf16[80,384]{1,0:T(8,128)(2,1)} %get-tuple-element.109), channel_id=1, source_target_pairs={{0,8},{1,9},{2,10},{3,11},{4,12},{5,13},{6,14},{7,15},{8,0},{9,1},... | collective-permute-start | bytes 184328 | tf_op jit(solution)/shard_map/ppermute | solution.py:84
  7.9 2.6 %collective-permute-start.15 = (bf16[80,384]{1,0:T(8,128)(2,1)}, bf16[80,384]{1,0:T(8,128)(2,1)}, u32[]{:S(2)}, u32[]{:S(2)}) collective-permute-start(bf16[80,384]{1,0:T(8,128)(2,1)} %get-tuple-element.108), channel_id=1, source_target_pairs={{0,16},{1,17},{2,18},{3,19},{4,20},{5,21},{6,22},{7,23},{8,24},{9,... | collective-permute-start | bytes 184328 | tf_op jit(solution)/shard_map/ppermute | solution.py:84
  25.1 3.5 %collective-permute-start.2 = (bf16[80,384]{1,0:T(8,128)(2,1)S(1)}, bf16[80,384]{1,0:T(8,128)(2,1)S(1)}, u32[]{:S(2)}, u32[]{:S(2)}) collective-permute-start(bf16[80,384]{1,0:T(8,128)(2,1)S(1)} %get-tuple-element.118), channel_id=1, source_target_pairs={{0,16},{1,17},{2,18},{3,19},{4,20},{5,21},{6,22},{7,23},{8,24},{9,... | collective-permute-start | bytes 184328 | tf_op jit(solution)/shard_map/ppermute | solution.py:84
  38.2 2.7 %collective-permute-done.4 = bf16[320,384]{1,0:T(8,128)(2,1)S(1)} collective-permute-done((bf16[320,384]{1,0:T(8,128)(2,1)S(1)}, bf16[320,384]{1,0:T(8,128)(2,1)S(1)}, u32[]{:S(2)}, u32[]{:S(2)}) %collective-permute-start.4) | collective-permute-done | bytes 245792 | tf_op jit(solution)/shard_map/ppermute | solution.py:84
  46.2 4.7 %collective-permute-done.5 = bf16[640,384]{1,0:T(8,128)(2,1)} collective-permute-done((bf16[640,384]{1,0:T(8,128)(2,1)}, bf16[640,384]{1,0:T(8,128)(2,1)}, u32[]{:S(2)}, u32[]{:S(2)}) %collective-permute-start.5) | collective-permute-done | bytes 491552 | tf_op jit(solution)/shard_map/ppermute | solution.py:84
  55.9 2.2 %collective-permute-done.18 = bf16[896,384]{1,0:T(8,128)(2,1)S(1)} collective-permute-done((bf16[896,384]{1,0:T(8,128)(2,1)}, bf16[896,384]{1,0:T(8,128)(2,1)S(1)}, u32[]{:S(2)}, u32[]{:S(2)}) %collective-permute-start.18) | collective-permute-done | bytes 688160 | tf_op jit(solution)/shard_map/ppermute | solution.py:84
  60.6 2.7 %broadcast_select_fusion.3 = (bf16[1280,384]{1,0:T(8,128)(2,1)}, bf16[1280,384]{1,0:T(8,128)(2,1)}) fusion(bf16[1280,384]{1,0:T(8,128)(2,1)} %slice_dynamic-update-slice_fusion.1, bf16[1280,384]{1,0:T(8,128)(2,1)S(1)} %collective-permute-done.6, pred[]{:T(512)S(6)} %eq.100), kind=kLoop, calls=%fused_computation.59 | loop fusion | flops 983040 | bytes 3932161 | tf_op jit(solution)/shard_map/jit(_where)/select_n | solution.py:135
  63.2 2.2 %fusion.103 = (f32[1280]{0:T(1024)S(1)}, f32[1280,4]{0,1:T(4,128)S(1)}) fusion(bf16[768,4]{0,1:T(4,128)(2,1)S(1)} %copy-done.40, bf16[1280,384]{1,0:T(8,128)(2,1)} %get-tuple-element.79, bf16[1280,384]{1,0:T(8,128)(2,1)} %get-tuple-element.78), kind=kOutput, calls=%fused_computation.260 | convolution fusion | flops 11800320 | bytes 1997824 | tf_op jit(solution)/shard_map/dot_general | solution.py:238
  65.6 2.8 %fusion.29 = f32[1280,384]{1,0:T(8,128)S(1)} fusion(bf16[1,768,384]{2,1,0:T(8,128)(2,1)} %param.26, bf16[1280,384]{1,0:T(8,128)(2,1)} %get-tuple-element.79, bf16[1280,384]{1,0:T(8,128)(2,1)} %get-tuple-element.78), kind=kOutput, calls=%fused_computation.81 | convolution fusion | flops 758906880 | bytes 4521984 | tf_op jit(solution)/shard_map/dot_general | solution.py:247
  73.3 2.2 %fusion.9 = bf16[1280,384]{1,0:T(8,128)(2,1)S(1)} fusion(f32[1280,384]{1,0:T(8,128)S(1)} %fusion.29, bf16[1280,768]{1,0:T(8,128)(2,1)S(1)} %bitcast.152, bf16[1,384,768]{2,1,0:T(8,128)(2,1)S(1)} %copy-done), kind=kOutput, calls=%fused_computation.19 | convolution fusion | flops 764805120 | bytes 5505024 | tf_op jit(solution)/shard_map/dot_general | solution.py:253
  81.7 5.4 %collective-permute-done.8 = bf16[640,384]{1,0:T(8,128)(2,1)S(1)} collective-permute-done((bf16[640,384]{1,0:T(8,128)(2,1)S(1)}, bf16[640,384]{1,0:T(8,128)(2,1)S(1)}, u32[]{:S(2)}, u32[]{:S(2)}) %collective-permute-start.8) | collective-permute-done | bytes 491552 | tf_op jit(solution)/shard_map/ppermute | solution.py:84
  90.9 3.6 %collective-permute-done.9 = bf16[320,384]{1,0:T(8,128)(2,1)S(1)} collective-permute-done((bf16[320,384]{1,0:T(8,128)(2,1)S(1)}, bf16[320,384]{1,0:T(8,128)(2,1)S(1)}, u32[]{:S(2)}, u32[]{:S(2)}) %collective-permute-start.9) | collective-permute-done | bytes 245792 | tf_op jit(solution)/shard_map/ppermute | solution.py:84
  100.8 3.7 %convolution_bitcast_fusion.1 = f32[1,768,384]{2,1,0:T(8,128)} fusion(bf16[1280,384]{1,0:T(8,128)(2,1)S(1)} %fusion.9, bf16[1280,384]{1,0:T(8,128)(2,1)} %get-tuple-element.79, bf16[1280,384]{1,0:T(8,128)(2,1)} %get-tuple-element.78), kind=kOutput, calls=%fused_computation.26 | convolution fusion | flops 758906880 | bytes 4128768 | tf_op jit(solution)/shard_map/dot_general | solution.py:256
  106.2 2.8 %collective-permute-start.24 = (bf16[80,384]{1,0:T(8,128)(2,1)S(1)}, bf16[80,384]{1,0:T(8,128)(2,1)S(1)}, u32[]{:S(2)}, u32[]{:S(2)}) collective-permute-start(bf16[80,384]{1,0:T(8,128)(2,1)S(1)} %get-tuple-element.103), channel_id=1, source_target_pairs={{0,16},{1,17},{2,18},{3,19},{4,20},{5,21},{6,22},{7,23},{8,24},{9,... | collective-permute-start | bytes 184328 | tf_op jit(solution)/shard_map/ppermute | solution.py:84
  112.2 2.9 %collective-permute-done.25 = bf16[80,384]{1,0:T(8,128)(2,1)S(1)} collective-permute-done((bf16[80,384]{1,0:T(8,128)(2,1)S(1)}, bf16[80,384]{1,0:T(8,128)(2,1)S(1)}, u32[]{:S(2)}, u32[]{:S(2)}) %collective-permute-start.25) | collective-permute-done | bytes 61472 | tf_op jit(solution)/shard_map/ppermute | solution.py:84
  133.2 4.8 %collective-permute-done.33 = bf16[256,384]{1,0:T(8,128)(2,1)S(1)} collective-permute-done((bf16[256,384]{1,0:T(8,128)(2,1)S(1)}, bf16[256,384]{1,0:T(8,128)(2,1)S(1)}, u32[]{:S(2)}, u32[]{:S(2)}) %collective-permute-start.33) | collective-permute-done | bytes 196640 | tf_op jit(solution)/shard_map/ppermute | solution.py:84
  145.4 2.3 %collective-permute-start.40 = (bf16[192,384]{1,0:T(8,128)(2,1)S(1)}, bf16[192,384]{1,0:T(8,128)(2,1)S(1)}, u32[]{:S(2)}, u32[]{:S(2)}) collective-permute-start(bf16[192,384]{1,0:T(8,128)(2,1)S(1)} %get-tuple-element.91), channel_id=1, source_target_pairs={{0,24},{1,25},{2,26},{3,27},{4,28},{5,29},{6,30},{7,31},{8,16},{9,... | collective-permute-start | bytes 442376 | tf_op jit(solution)/shard_map/ppermute | solution.py:84
  151.1 6.3 %collective-permute-done.39 = bf16[192,384]{1,0:T(8,128)(2,1)S(1)} collective-permute-done((bf16[192,384]{1,0:T(8,128)(2,1)S(1)}, bf16[192,384]{1,0:T(8,128)(2,1)S(1)}, u32[]{:S(2)}, u32[]{:S(2)}) %collective-permute-start.39) | collective-permute-done | bytes 147488 | tf_op jit(solution)/shard_map/ppermute | solution.py:84
  157.5 2.9 %collective-permute-start.41 = (bf16[192,384]{1,0:T(8,128)(2,1)S(1)}, bf16[192,384]{1,0:T(8,128)(2,1)S(1)}, u32[]{:S(2)}, u32[]{:S(2)}) collective-permute-start(bf16[192,384]{1,0:T(8,128)(2,1)S(1)} %add_convert_fusion.2), channel_id=1, source_target_pairs={{0,8},{1,9},{2,10},{3,11},{4,12},{5,13},{6,14},{7,15},{8,0},{9,1},... | collective-permute-start | bytes 442376 | tf_op jit(solution)/shard_map/ppermute | solution.py:84
  160.5 2.3 %collective-permute-start.43 = (bf16[192,384]{1,0:T(8,128)(2,1)S(1)}, bf16[192,384]{1,0:T(8,128)(2,1)S(1)}, u32[]{:S(2)}, u32[]{:S(2)}) collective-permute-start(bf16[192,384]{1,0:T(8,128)(2,1)S(1)} %add_convert_fusion.2), channel_id=1, source_target_pairs={{0,24},{1,25},{2,26},{3,27},{4,28},{5,29},{6,30},{7,31},{8,16},{9,... | collective-permute-start | bytes 442376 | tf_op jit(solution)/shard_map/ppermute | solution.py:84
  164.7 8.8 %collective-permute-done.42 = bf16[192,384]{1,0:T(8,128)(2,1)S(1)} collective-permute-done((bf16[192,384]{1,0:T(8,128)(2,1)S(1)}, bf16[192,384]{1,0:T(8,128)(2,1)S(1)}, u32[]{:S(2)}, u32[]{:S(2)}) %collective-permute-start.42) | collective-permute-done | bytes 147488 | tf_op jit(solution)/shard_map/ppermute | solution.py:84
  176.8 2.6 %collective-permute-start.30 = (f32[40,128]{1,0:T(8,128)S(1)}, f32[40,128]{1,0:T(8,128)S(1)}, u32[]{:S(2)}, u32[]{:S(2)}) collective-permute-start(f32[40,128]{1,0:T(8,128)S(1)} %fusion.143), channel_id=1, source_target_pairs={{0,8},{1,9},{2,10},{3,11},{4,12},{5,13},{6,14},{7,15},{8,0},{9,1},... | collective-permute-start | bytes 61448 | tf_op jit(solution)/shard_map/ppermute | solution.py:84
  188.2 2.7 %collective-permute-done.45 = bf16[768,384]{1,0:T(8,128)(2,1)S(1)} collective-permute-done((bf16[768,384]{1,0:T(8,128)(2,1)S(1)}, bf16[768,384]{1,0:T(8,128)(2,1)S(1)}, u32[]{:S(2)}, u32[]{:S(2)}) %collective-permute-start.45) | collective-permute-done | bytes 589856 | tf_op jit(solution)/shard_map/ppermute | solution.py:84
  195.1 2.7 %collective-permute-done.47 = bf16[384,384]{1,0:T(8,128)(2,1)} collective-permute-done((bf16[384,384]{1,0:T(8,128)(2,1)S(1)}, bf16[384,384]{1,0:T(8,128)(2,1)}, u32[]{:S(2)}, u32[]{:S(2)}) %collective-permute-start.47) | collective-permute-done | bytes 294944 | tf_op jit(solution)/shard_map/ppermute | solution.py:84
  (349 shorter events, 118.2 us)
Async XLA Ops:
  4.9 13.1 %collective-permute-start.14 = (bf16[80,384]{1,0:T(8,128)(2,1)}, bf16[80,384]{1,0:T(8,128)(2,1)}, u32[]{:S(2)}, u32[]{:S(2)}) collective-permute-start(bf16[80,384]{1,0:T(8,128)(2,1)} %get-tuple-element.109), channel_id=1, source_target_pairs={{0,8},{1,9},{2,10},{3,11},{4,12},{5,13},{6,14},{7,15},{8,0},{9,1},... | collective-permute-start | bytes 184328 | tf_op jit(solution)/shard_map/ppermute | solution.py:84
  7.9 11.6 %collective-permute-start.15 = (bf16[80,384]{1,0:T(8,128)(2,1)}, bf16[80,384]{1,0:T(8,128)(2,1)}, u32[]{:S(2)}, u32[]{:S(2)}) collective-permute-start(bf16[80,384]{1,0:T(8,128)(2,1)} %get-tuple-element.108), channel_id=1, source_target_pairs={{0,16},{1,17},{2,18},{3,19},{4,20},{5,21},{6,22},{7,23},{8,24},{9,... | collective-permute-start | bytes 184328 | tf_op jit(solution)/shard_map/ppermute | solution.py:84
  10.5 10.5 %collective-permute-start.16 = (bf16[80,384]{1,0:T(8,128)(2,1)}, bf16[80,384]{1,0:T(8,128)(2,1)}, u32[]{:S(2)}, u32[]{:S(2)}) collective-permute-start(bf16[80,384]{1,0:T(8,128)(2,1)} %get-tuple-element.107), channel_id=1, source_target_pairs={{0,24},{1,25},{2,26},{3,27},{4,28},{5,29},{6,30},{7,31},{8,16},{9,... | collective-permute-start | bytes 184328 | tf_op jit(solution)/shard_map/ppermute | solution.py:84
  29.3 15.6 %collective-permute-start.17 = (bf16[448,384]{1,0:T(8,128)(2,1)}, bf16[448,384]{1,0:T(8,128)(2,1)S(1)}, u32[]{:S(2)}, u32[]{:S(2)}) collective-permute-start(bf16[448,384]{1,0:T(8,128)(2,1)} %get-tuple-element.124), channel_id=1, source_target_pairs={{0,2},{1,5},{2,0},{3,7},{4,6},{5,1},{6,4},{7,3},{8,10},{9,13},{10,... | collective-permute-start | bytes 1032200 | tf_op jit(solution)/shard_map/ppermute | solution.py:84
  41.7 9.1 %collective-permute-start.5 = (bf16[640,384]{1,0:T(8,128)(2,1)}, bf16[640,384]{1,0:T(8,128)(2,1)}, u32[]{:S(2)}, u32[]{:S(2)}) collective-permute-start(bf16[640,384]{1,0:T(8,128)(2,1)} %constant_dynamic-update-slice_fusion), channel_id=1, source_target_pairs={{0,4},{1,3},{2,6},{3,1},{4,0},{5,7},{6,2},{7,5},{8,12},{9,11},{10,... | collective-permute-start | bytes 1474568 | tf_op jit(solution)/shard_map/ppermute | solution.py:84
  45.7 12.4 %collective-permute-start.18 = (bf16[896,384]{1,0:T(8,128)(2,1)}, bf16[896,384]{1,0:T(8,128)(2,1)S(1)}, u32[]{:S(2)}, u32[]{:S(2)}) collective-permute-start(bf16[896,384]{1,0:T(8,128)(2,1)} %constant_dynamic-update-slice_fusion.13), channel_id=1, source_target_pairs={{0,4},{1,3},{2,6},{3,1},{4,0},{5,7},{6,2},{7,5},{8,12},{9,11},{10,... | collective-permute-start | bytes 2064392 | tf_op jit(solution)/shard_map/ppermute | solution.py:84
  60.6 10.1 %collective-permute-start.19 = (bf16[1792,384]{1,0:T(8,128)(2,1)}, bf16[1792,384]{1,0:T(8,128)(2,1)}, u32[]{:S(2)}, u32[]{:S(2)}) collective-permute-start(bf16[1792,384]{1,0:T(8,128)(2,1)} %slice_dynamic-update-slice_fusion), channel_id=1, source_target_pairs={{0,1},{1,0},{2,3},{3,2},{4,5},{5,4},{6,7},{7,6},{8,9},{9,8},{10,11... | collective-permute-start | bytes 4128776 | tf_op jit(solution)/shard_map/ppermute | solution.py:84
  78.2 8.9 %collective-permute-start.8 = (bf16[640,384]{1,0:T(8,128)(2,1)S(1)}, bf16[640,384]{1,0:T(8,128)(2,1)S(1)}, u32[]{:S(2)}, u32[]{:S(2)}) collective-permute-start(bf16[640,384]{1,0:T(8,128)(2,1)S(1)} %pad_maximum_fusion.7), channel_id=1, source_target_pairs={{0,2},{1,5},{2,0},{3,7},{4,6},{5,1},{6,4},{7,3},{8,10},{9,13},{10,... | collective-permute-start | bytes 1474568 | tf_op jit(solution)/shard_map/ppermute | solution.py:84
  80.2 18.9 %collective-permute-start.21 = (bf16[640,384]{1,0:T(8,128)(2,1)S(1)}, bf16[640,384]{1,0:T(8,128)(2,1)S(1)}, u32[]{:S(2)}, u32[]{:S(2)}) collective-permute-start(bf16[640,384]{1,0:T(8,128)(2,1)S(1)} %pad_maximum_fusion.8), channel_id=1, source_target_pairs={{0,2},{1,5},{2,0},{3,7},{4,6},{5,1},{6,4},{7,3},{8,10},{9,13},{10,... | collective-permute-start | bytes 1474568 | tf_op jit(solution)/shard_map/ppermute | solution.py:84
  94.6 10.9 %collective-permute-start.10 = (bf16[80,384]{1,0:T(8,128)(2,1)S(1)}, bf16[80,384]{1,0:T(8,128)(2,1)S(1)}, u32[]{:S(2)}, u32[]{:S(2)}) collective-permute-start(bf16[80,384]{1,0:T(8,128)(2,1)S(1)} %get-tuple-element.114), channel_id=1, source_target_pairs={{0,8},{1,9},{2,10},{3,11},{4,12},{5,13},{6,14},{7,15},{8,0},{9,1},... | collective-permute-start | bytes 184328 | tf_op jit(solution)/shard_map/ppermute | solution.py:84
  95.5 10.0 %collective-permute-start.11 = (bf16[80,384]{1,0:T(8,128)(2,1)S(1)}, bf16[80,384]{1,0:T(8,128)(2,1)S(1)}, u32[]{:S(2)}, u32[]{:S(2)}) collective-permute-start(bf16[80,384]{1,0:T(8,128)(2,1)S(1)} %get-tuple-element.113), channel_id=1, source_target_pairs={{0,16},{1,17},{2,18},{3,19},{4,20},{5,21},{6,22},{7,23},{8,24},{9,... | collective-permute-start | bytes 184328 | tf_op jit(solution)/shard_map/ppermute | solution.py:84
  123.7 8.1 %collective-permute-start.32 = (bf16[128,384]{1,0:T(8,128)(2,1)S(1)}, bf16[128,384]{1,0:T(8,128)(2,1)S(1)}, u32[]{:S(2)}, u32[]{:S(2)}) collective-permute-start(bf16[128,384]{1,0:T(8,128)(2,1)S(1)} %constant_dynamic-slice_fusion.3), channel_id=1, source_target_pairs={{0,2},{1,5},{2,0},{3,7},{4,6},{5,1},{6,4},{7,3},{8,10},{9,13},{10,... | collective-permute-start | bytes 294920 | tf_op jit(solution)/shard_map/ppermute | solution.py:84
  128.0 13.5 %collective-permute-start.35 = (bf16[128,384]{0,1:T(8,128)(2,1)}, bf16[128,384]{0,1:T(8,128)(2,1)}, u32[]{:S(2)}, u32[]{:S(2)}) collective-permute-start(bf16[128,384]{0,1:T(8,128)(2,1)} %get-tuple-element.98), channel_id=1, source_target_pairs={{0,2},{1,3},{2,0},{3,1},{4,6},{5,7},{6,4},{7,5},{8,10},{9,11},{10,... | collective-permute-start | bytes 294920 | tf_op jit(solution)/shard_map/ppermute | solution.py:84
  128.6 12.9 %collective-permute-start.36 = (bf16[128,384]{0,1:T(8,128)(2,1)}, bf16[128,384]{0,1:T(8,128)(2,1)}, u32[]{:S(2)}, u32[]{:S(2)}) collective-permute-start(bf16[128,384]{0,1:T(8,128)(2,1)} %get-tuple-element.97), channel_id=1, source_target_pairs={{0,4},{1,5},{2,6},{3,7},{4,0},{5,1},{6,2},{7,3},{8,12},{9,13},{10,... | collective-permute-start | bytes 294920 | tf_op jit(solution)/shard_map/ppermute | solution.py:84
  129.7 11.8 %collective-permute-start.37 = (bf16[128,384]{0,1:T(8,128)(2,1)}, bf16[128,384]{0,1:T(8,128)(2,1)}, u32[]{:S(2)}, u32[]{:S(2)}) collective-permute-start(bf16[128,384]{0,1:T(8,128)(2,1)} %get-tuple-element.96), channel_id=1, source_target_pairs={{0,6},{1,7},{2,4},{3,5},{4,2},{5,3},{6,0},{7,1},{8,14},{9,15},{10,... | collective-permute-start | bytes 294920 | tf_op jit(solution)/shard_map/ppermute | solution.py:84
  138.6 9.1 %collective-permute-start.27 = (bf16[128,768]{1,0:T(8,128)(2,1)S(1)}, bf16[128,768]{1,0:T(8,128)(2,1)S(1)}, u32[]{:S(2)}, u32[]{:S(2)}) collective-permute-start(bf16[128,768]{1,0:T(8,128)(2,1)S(1)} %fusion.13), channel_id=1, source_target_pairs={{0,1},{1,0},{2,3},{3,2},{4,5},{5,4},{6,7},{7,6},{8,9},{9,8},{10,11... | collective-permute-start | bytes 589832 | tf_op jit(solution)/shard_map/ppermute | solution.py:84
  143.3 14.0 %collective-permute-start.39 = (bf16[192,384]{1,0:T(8,128)(2,1)S(1)}, bf16[192,384]{1,0:T(8,128)(2,1)S(1)}, u32[]{:S(2)}, u32[]{:S(2)}) collective-permute-start(bf16[192,384]{1,0:T(8,128)(2,1)S(1)} %get-tuple-element.92), channel_id=1, source_target_pairs={{0,16},{1,17},{2,18},{3,19},{4,20},{5,21},{6,22},{7,23},{8,24},{9,... | collective-permute-start | bytes 442376 | tf_op jit(solution)/shard_map/ppermute | solution.py:84
  145.4 12.0 %collective-permute-start.40 = (bf16[192,384]{1,0:T(8,128)(2,1)S(1)}, bf16[192,384]{1,0:T(8,128)(2,1)S(1)}, u32[]{:S(2)}, u32[]{:S(2)}) collective-permute-start(bf16[192,384]{1,0:T(8,128)(2,1)S(1)} %get-tuple-element.91), channel_id=1, source_target_pairs={{0,24},{1,25},{2,26},{3,27},{4,28},{5,29},{6,30},{7,31},{8,16},{9,... | collective-permute-start | bytes 442376 | tf_op jit(solution)/shard_map/ppermute | solution.py:84
  148.0 14.8 %collective-permute-start.28 = (f32[40,128]{1,0:T(8,128)S(1)}, f32[40,128]{1,0:T(8,128)S(1)}, u32[]{:S(2)}, u32[]{:S(2)}) collective-permute-start(f32[40,128]{1,0:T(8,128)S(1)} %pad_bitcast_fusion), channel_id=1, source_target_pairs={{0,2},{1,3},{2,0},{3,1},{4,6},{5,7},{6,4},{7,5},{8,10},{9,11},{10,... | collective-permute-start | bytes 61448 | tf_op jit(solution)/shard_map/ppermute | solution.py:84
  160.4 13.1 %collective-permute-start.42 = (bf16[192,384]{1,0:T(8,128)(2,1)S(1)}, bf16[192,384]{1,0:T(8,128)(2,1)S(1)}, u32[]{:S(2)}, u32[]{:S(2)}) collective-permute-start(bf16[192,384]{1,0:T(8,128)(2,1)S(1)} %add_convert_fusion.2), channel_id=1, source_target_pairs={{0,16},{1,17},{2,18},{3,19},{4,20},{5,21},{6,22},{7,23},{8,24},{9,... | collective-permute-start | bytes 442376 | tf_op jit(solution)/shard_map/ppermute | solution.py:84
  160.5 12.9 %collective-permute-start.43 = (bf16[192,384]{1,0:T(8,128)(2,1)S(1)}, bf16[192,384]{1,0:T(8,128)(2,1)S(1)}, u32[]{:S(2)}, u32[]{:S(2)}) collective-permute-start(bf16[192,384]{1,0:T(8,128)(2,1)S(1)} %add_convert_fusion.2), channel_id=1, source_target_pairs={{0,24},{1,25},{2,26},{3,27},{4,28},{5,29},{6,30},{7,31},{8,16},{9,... | collective-permute-start | bytes 442376 | tf_op jit(solution)/shard_map/ppermute | solution.py:84
  162.8 14.0 %collective-permute-start.29 = (f32[40,128]{1,0:T(8,128)S(1)}, f32[40,128]{1,0:T(8,128)S(1)}, u32[]{:S(2)}, u32[]{:S(2)}) collective-permute-start(f32[40,128]{1,0:T(8,128)S(1)} %fusion.92), channel_id=1, source_target_pairs={{0,4},{1,5},{2,6},{3,7},{4,0},{5,1},{6,2},{7,3},{8,12},{9,13},{10,... | collective-permute-start | bytes 61448 | tf_op jit(solution)/shard_map/ppermute | solution.py:84
  174.7 12.5 %collective-permute-start.44 = (bf16[768,384]{1,0:T(8,128)(2,1)S(1)}, bf16[768,384]{1,0:T(8,128)(2,1)S(1)}, u32[]{:S(2)}, u32[]{:S(2)}) collective-permute-start(bf16[768,384]{1,0:T(8,128)(2,1)S(1)} %bitcast_select_fusion), channel_id=1, source_target_pairs={{0,2},{1,3},{2,0},{3,1},{4,6},{5,7},{6,4},{7,5},{8,10},{9,11},{10,... | collective-permute-start | bytes 1769480 | tf_op jit(solution)/shard_map/ppermute | solution.py:84
  175.6 15.3 %collective-permute-start.45 = (bf16[768,384]{1,0:T(8,128)(2,1)S(1)}, bf16[768,384]{1,0:T(8,128)(2,1)S(1)}, u32[]{:S(2)}, u32[]{:S(2)}) collective-permute-start(bf16[768,384]{1,0:T(8,128)(2,1)S(1)} %bitcast_select_fusion), channel_id=1, source_target_pairs={{0,4},{1,5},{2,6},{3,7},{4,0},{5,1},{6,2},{7,3},{8,12},{9,13},{10,... | collective-permute-start | bytes 1769480 | tf_op jit(solution)/shard_map/ppermute | solution.py:84
  (83 other events, 678.9 us)

commit v2 on v0

v2 whole, which is shorter than its diff:
```python
import functools

import jax
import jax.numpy as jnp
import numpy as np
from jax import lax
from jax.experimental import pallas as pl
from jax.experimental.pallas import tpu as pltpu
from jax.sharding import PartitionSpec as P

HEAD_DIM = 64
TOP = 2
REACH = 64
LANES = 128

eps_norm = 1e-06
gelu_scale = float(np.sqrt(2.0 / np.pi))
microseconds = {"front": 5, "route": 1.9, "expert": 4.4, "expert_back": 5.4, "expert_grads": 4.0, "combine": 1.9, "attend_back": 2.5, "partial": 1.2, "final": 3.9, "tokens_back": 1.5, "small": 1.4}
f32 = jnp.float32
bf16 = jnp.bfloat16


def bucket_of_distance(length, buckets, max_reach):
    exact_span = buckets // 2
    distance = np.arange(length)
    log_ratio = np.log(np.maximum(distance, exact_span) / exact_span) / np.log(
        max_reach / exact_span
    )
    coarse = exact_span + np.floor(log_ratio * (buckets - exact_span)).astype(np.int64)
    return np.where(distance < exact_span, distance, np.minimum(coarse, buckets - 1))


def nn(left, right, precision=None):
    return lax.dot_general(
        left, right, (((1,), (0,)), ((), ())), precision=precision, preferred_element_type=f32
    )


def nt(left, right):
    return lax.dot_general(left, right, (((1,), (1,)), ((), ())), preferred_element_type=f32)


def tn(left, right):
    return lax.dot_general(left, right, (((0,), (0,)), ((), ())), preferred_element_type=f32)


def iota(shape, axis):
    return lax.broadcasted_iota(jnp.int32, shape, axis)


def call(body, name, ids, outs, *args, scratch=(), limit=24, far=()):
    shapes = [jax.ShapeDtypeStruct(shape, dtype) for shape, dtype in outs]
    return pl.pallas_call(
        body,
        out_shape=shapes,
        in_specs=[pl.BlockSpec(memory_space=pltpu.SMEM)]
        + [
            pl.BlockSpec(memory_space=pltpu.HBM if i in far else pltpu.VMEM)
            for i in range(len(args))
        ],
        out_specs=[pl.BlockSpec(memory_space=pltpu.VMEM)] * len(outs),
        scratch_shapes=list(scratch),
        compiler_params=pltpu.CompilerParams(vmem_limit_bytes=limit << 20),
        cost_estimate=pl.CostEstimate(
            flops=0, transcendentals=0, bytes_accessed=int(microseconds.get(name, 0.8) * 3.6e6)
        ),
        name=name,
    )(
        ids,
        *[
            pltpu.with_memory_space_constraint(a, pltpu.HBM) if i in far else a
            for i, a in enumerate(args)
        ],
    )


def halves(value, t):
    width = value.shape[1] // 2
    low, high = value[:, :width], value[:, width:]
    even = t == 0
    return jnp.where(even, low, high), jnp.where(even, high, low)


def row_halves(value, t):
    width = value.shape[0] // 2
    low, high = value[:width], value[width:]
    even = t == 0
    return jnp.where(even, low, high), jnp.where(even, high, low)


def columns_of(row):
    length = row.shape[1]
    return jnp.broadcast_to(row.astype(f32), (length, length)).T


def sums_by_distance(square):
    length = square.shape[0]
    rows = length // 2
    while rows >= 1:
        square = square[:rows] + pltpu.roll(square[rows:], length - rows, 1)
        rows //= 2
    return square


def fetch(sources, targets, sems):
    copies = [
        pltpu.make_async_copy(source, target, sems.at[i])
        for i, (source, target) in enumerate(zip(sources, targets))
    ]
    for copy in copies:
        copy.start()
    return copies


def route_body(experts, stride, ids, routes_far, cot_far, slots, *refs):
    chunks, (routes, cot, sems) = refs[:experts], refs[experts:]
    copies = fetch((routes_far, cot_far), (routes, cot), sems)
    copies[0].wait()
    e, t = ids[0], ids[2]
    length = routes.shape[1]
    expert_row = iota((experts, length), 0)
    first = (expert_row == routes[0:1, :]).astype(f32)
    second = (expert_row == routes[1:2, :]).astype(f32)
    earlier = (iota((length, length), 0) < iota((length, length), 1)).astype(bf16)
    before = nn((first + second).astype(bf16), earlier)
    rank0 = jnp.sum(before * first, axis=0, keepdims=True).astype(jnp.int32)
    rank1 = jnp.sum(before * second, axis=0, keepdims=True).astype(jnp.int32)
    slot0 = (routes[0:1, :] ^ e) * stride + rank0
    slot1 = (routes[1:2, :] ^ e) * stride + rank1
    slots[0:1, :] = slot0
    slots[1:2, :] = slot1
    copies[1].wait()
    mine, _ = halves(cot[...], t)
    for s in range(experts):
        place = iota((stride, length), 0) + s * stride
        pick = ((place == slot0) | (place == slot1)).astype(bf16)
        chunks[s][...] = nn(pick, mine).astype(bf16)


def front_body(ids, *refs):
    sources = refs[:9]
    early, part, q_out, k_out, v_out, probs = refs[9:15]
    targets, sems = refs[15:-1], refs[-1]
    tokens, gain, wq, wk, wv, rel, hot, seq, wo = targets
    copies = fetch(sources, targets, sems)
    t = ids[2]
    length = tokens.shape[0]
    mixed_out = early.at[pl.ds(length, length), :]
    copies[0].wait()
    copies[1].wait()
    wide = tokens[...].astype(f32)
    inv = lax.rsqrt(jnp.mean(wide * wide, axis=-1, keepdims=True) + eps_norm)
    value = (wide * inv * gain[...][None, :]).astype(bf16)
    early[pl.ds(0, length), :] = halves(value, t)[0]
    rows = length
    copies[2].wait()
    queries = nn(value, wq[...]).astype(bf16)
    copies[3].wait()
    keys = nn(value, wk[...]).astype(bf16)
    copies[4].wait()
    values = nn(value, wv[...]).astype(bf16)
    q_out[...] = queries
    k_out[...] = keys
    v_out[...] = values
    for copy in copies[5:8]:
        copy.wait()
    seq_cols = jnp.broadcast_to(seq[...].astype(f32), (rows, rows))
    allowed = (seq_cols == seq_cols.T) & (iota((rows, rows), 0) >= iota((rows, rows), 1))
    table = nn(rel[...], hot[...], lax.Precision.HIGHEST)
    lane = iota((rows, LANES), 1)
    for pair in range(queries.shape[1] // LANES):
        span = slice(pair * LANES, (pair + 1) * LANES)
        q, k, v = queries[:, span], keys[:, span], values[:, span]
        mixed = []
        for side in range(2):
            head = pair * 2 + side
            mine = (lane < HEAD_DIM) if side == 0 else (lane >= HEAD_DIM)
            raw = nt(jnp.where(mine, q, jnp.zeros_like(q)), k)
            bias = pltpu.roll(
                jnp.broadcast_to(table[head : head + 1, :], (rows, rows)),
                0,
                1,
                stride=1,
                stride_axis=0,
            )
            scores = jnp.where(allowed, raw * HEAD_DIM ** (-0.5) + bias, -1e30)
            top = jnp.max(scores, axis=-1, keepdims=True)
            raised = jnp.exp(scores - top)
            weight = raised / jnp.sum(raised, axis=-1, keepdims=True)
            probs[head] = weight
            mixed.append(nn(weight.astype(bf16), v))
        mixed_out[:, span] = jnp.where(lane < HEAD_DIM, mixed[0], mixed[1]).astype(bf16)
    copies[8].wait()
    part[...] = nn(mixed_out[...], wo[...])


def router_of(normed, weights_row):
    logits = nt(normed, weights_row)
    raised = jnp.exp(logits - jnp.max(logits, axis=-1, keepdims=True))
    return raised / jnp.sum(raised, axis=-1, keepdims=True)


def middle_body(experts, stride, ids, own, other, tokens, gain, router, slots, residual, normed, probs, *chunks):
    t = ids[2]
    wide = tokens[...].astype(f32) + (own[...] + other[...])
    residual[...] = wide
    inv = lax.rsqrt(jnp.mean(wide * wide, axis=-1, keepdims=True) + eps_norm)
    value = (wide * inv * gain[...][None, :]).astype(bf16)
    normed[...] = value
    mine, _ = halves(value, t)
    length = slots.shape[1]
    for s in range(experts):
        place = iota((stride, length), 0) + s * stride
        pick = ((place == slots[0:1, :]) | (place == slots[1:2, :])).astype(bf16)
        chunks[s][...] = nn(pick, mine).astype(bf16)
    probs[...] = router_of(value, router[...])


def join_body(ids, *refs):
    out = refs[-1]
    start = 0
    for ref in refs[:-1]:
        out[pl.ds(start, ref.shape[0]), :] = ref[...]
        start += ref.shape[0]


def expert_body(rows, ids, *refs):
    own, other = refs[:4], refs[4:8]
    w_in, w_out, act, slope, part_mine, part_other = refs[8:]
    t = ids[2]
    in_mine, in_other = row_halves(w_in[0], t)
    out_mine, out_other = halves(w_out[0], t)
    for p in range(4):
        span = pl.ds(p * rows, rows)
        pre = nn(own[p][...], in_mine) + nn(other[p][...], in_other)
        square = pre * pre
        bent = jnp.tanh(gelu_scale * (pre + 0.044715 * pre * square))
        half = 0.5 * (1.0 + bent)
        value = (pre * half).astype(bf16)
        act[span, :] = value
        slope[span, :] = half + 0.5 * pre * (1.0 - bent * bent) * (
            gelu_scale * (1.0 + 3 * 0.044715 * square)
        )
        part_mine[span, :] = nn(value, out_mine).astype(bf16)
        part_other[span, :] = nn(value, out_other).astype(bf16)


def expert_back_body(rows, experts, ids, *refs):
    own, other, cot_own, cot_other = refs[:4], refs[4:8], refs[8:12], refs[12:16]
    w_in, w_out, router, slope, grad_pre, grad_mine, grad_other, back_mine, back_other = refs[16:]
    e, t = ids[0], ids[2]
    in_mine, in_other = row_halves(w_in[0], t)
    out_mine, out_other = halves(w_out[0], t)
    router_mine, router_other = halves(router[...], t)
    for p in range(4):
        span = pl.ds(p * rows, rows)
        logits = nt(own[p][...], router_mine) + nt(other[p][...], router_other)
        raised = jnp.exp(logits - jnp.max(logits, axis=-1, keepdims=True))
        chosen = jnp.where(iota(raised.shape, 1) == e, raised, 0.0)
        gate = jnp.sum(chosen, axis=-1, keepdims=True) / jnp.sum(raised, axis=-1, keepdims=True)
        first = (gate * cot_own[p][pl.ds(0, rows), :].astype(f32)).astype(bf16)
        second = (gate * cot_other[p][pl.ds(0, rows), :].astype(f32)).astype(bf16)
        grad_mine[span, :] = first
        grad_other[span, :] = second
        grad_act = nt(first, out_mine) + nt(second, out_other)
        value = (grad_act * slope[span, :]).astype(bf16)
        grad_pre[span, :] = value
        back_mine[span, :] = nt(value, in_mine).astype(bf16)
        back_other[span, :] = nt(value, in_other).astype(bf16)


def expert_grads_body(rows, ids, *refs):
    own, other = refs[:4], refs[4:8]
    act, grad_pre, grad_mine, grad_other, out_in, out_out = refs[8:]
    even = ids[2] == 0
    low = jnp.where(even, grad_mine[...], grad_other[...])
    high = jnp.where(even, grad_other[...], grad_mine[...])
    width = low.shape[1]
    left = act[...]
    out_out[0, :, :width] = tn(left, low)
    out_out[0, :, width:] = tn(left, high)
    first = jnp.concatenate([jnp.where(even, own[p][...], other[p][...]) for p in range(4)], axis=0)
    second = jnp.concatenate([jnp.where(even, other[p][...], own[p][...]) for p in range(4)], axis=0)
    right = grad_pre[...]
    out_in[0, :width, :] = tn(first, right)
    out_in[0, width:, :] = tn(second, right)


def pair_sum_body(ids, mine, received, keep, send):
    rows = mine.shape[0] // 4

    def block(p):
        q = (0, 2, 1, 3)[p]
        left = mine[pl.ds(p * rows, rows), :].astype(f32)
        return (left + received[pl.ds(q * rows, rows), :].astype(f32)).astype(bf16)

    keep[pl.ds(0, rows), :] = block(0)
    keep[pl.ds(rows, rows), :] = block(2)
    send[pl.ds(0, rows), :] = block(1)
    send[pl.ds(rows, rows), :] = block(3)


def plane_sum_body(ids, keep, received, kept, send):
    rows = keep.shape[0] // 2
    total = keep[...].astype(f32) + received[...].astype(f32)
    kept[...] = total[:rows]
    send[...] = total[rows:].astype(bf16)


def last_sum_body(experts, stride, ids, kept, received, kept_back, received_back, *chunks):
    first = (kept[...] + received[...].astype(f32)).astype(bf16)
    second = (kept_back[...] + received_back[...].astype(f32)).astype(bf16)
    for s in range(experts):
        chunks[s][pl.ds(0, stride), :] = first[s * stride : (s + 1) * stride]
        chunks[s][pl.ds(stride, stride), :] = second[s * stride : (s + 1) * stride]


def combine_body(experts, stride, ids, *refs):
    chunks = refs[:experts]
    slots, routes, probs, cot, residual, packed = refs[experts:]
    t = ids[2]
    length = slots.shape[1]
    probs_all = probs[...]
    choice = iota(probs_all.shape, 1)
    cot_mine = halves(cot[...], t)[0].astype(f32)
    mixture = None
    back = None
    lanes = iota((length, LANES), 1)
    dots = jnp.zeros((length, LANES), f32)
    for k in range(TOP):
        slot = columns_of(slots[k : k + 1, :])
        route = columns_of(routes[k : k + 1, :])[:, : probs_all.shape[1]]
        gate = jnp.sum(
            jnp.where(choice.astype(f32) == route, probs_all, 0.0), axis=-1, keepdims=True
        )
        chosen = None
        for s in range(experts):
            place = (iota((length, stride), 1) + s * stride).astype(f32)
            pick = (place == slot[:, :1]).astype(bf16)
            value = nn(pick, chunks[s][pl.ds(0, stride), :])
            grad = nn(pick, chunks[s][pl.ds(stride, stride), :])
            chosen = value if chosen is None else chosen + value
            back = grad if back is None else back + grad
        mixture = gate * chosen if mixture is None else mixture + gate * chosen
        dots = jnp.where(lanes == k, jnp.sum(cot_mine * chosen, axis=-1, keepdims=True), dots)
    width = back.shape[1]
    packed[:, :width] = back
    packed[:, width : 2 * width] = halves(residual[...], t)[0] + mixture
    packed[:, 2 * width :] = dots


def norm_back_body(
    experts, ids, own, other, normed, probs, residual, routes, cot, gain, router, output, grad_out, att, small
):
    even = ids[2] == 0
    width = residual.shape[1] // 2
    first, last = slice(0, width), slice(width, 2 * width)
    low = jnp.where(even, own[:, first], other[:, first])
    high = jnp.where(even, other[:, first], own[:, first])
    back = jnp.concatenate([low, high], axis=1)
    output[:, first] = jnp.where(even, own[:, last], other[:, last]).astype(bf16)
    output[:, last] = jnp.where(even, other[:, last], own[:, last]).astype(bf16)
    dots = own[:, 2 * width :] + other[:, 2 * width :]
    probs_all = probs[...]
    choice = iota(probs_all.shape, 1).astype(f32)
    grad_probs = jnp.zeros_like(probs_all)
    for k in range(TOP):
        route = columns_of(routes[k : k + 1, :])[:, : probs_all.shape[1]]
        grad_probs = grad_probs + jnp.where(choice == route, dots[:, k : k + 1], 0.0)
    inner = jnp.sum(probs_all * grad_probs, axis=-1, keepdims=True)
    grad_logits = (probs_all * (grad_probs - inner)).astype(bf16)
    grad_normed = back + nn(grad_logits, router[...])
    wide = residual[...]
    inv = lax.rsqrt(jnp.mean(wide * wide, axis=-1, keepdims=True) + eps_norm)
    scaled = grad_normed * gain[...][None, :]
    grad = (
        cot[...].astype(f32)
        + inv * scaled
        - wide * (inv * inv * inv) * jnp.mean(scaled * wide, axis=-1, keepdims=True)
    )
    grad_out[...] = grad
    att[...] = grad.astype(bf16)
    small[0:1, :] = jnp.sum(grad_normed * wide * inv, axis=0, keepdims=True)
    small[pl.ds(1, experts), :] = tn(grad_logits, normed[...])


def attend_back_body(
    ids, att, wo, q_in, k_in, v_in, mixed_in, probs, wq, wk, wv, r0, r1, r2, r3, normed_part, bias, stack
):
    q_id, t = ids[1], ids[2]
    grad = att[...]
    rows = grad.shape[0]
    lane = iota((rows, LANES), 1)
    scale = HEAD_DIM ** (-0.5)
    for pair in range(q_in.shape[1] // LANES):
        span = slice(pair * LANES, (pair + 1) * LANES)
        grad_mixed = nt(grad, wo[span, :]).astype(bf16)
        q, k, v = q_in[:, span], k_in[:, span], v_in[:, span]
        mixed = mixed_in[pl.ds(rows, rows), span].astype(f32)
        dq, dk, dv = [], [], []
        for side in range(2):
            head = pair * 2 + side
            mine = (lane < HEAD_DIM) if side == 0 else (lane >= HEAD_DIM)
            part = jnp.where(mine, grad_mixed, jnp.zeros_like(grad_mixed))
            weight = probs[head]
            dv.append(tn(weight.astype(bf16), grad_mixed))
            delta = jnp.sum(part.astype(f32) * mixed, axis=-1, keepdims=True)
            scores = weight * (nt(part, v) - delta)
            bias[0:1, head * rows : (head + 1) * rows] = sums_by_distance(scores)
            scores = scores.astype(bf16)
            dq.append(nn(scores, k))
            dk.append(tn(scores, q))
        first = lane < HEAD_DIM
        stack[0, :, span] = (jnp.where(first, dq[0], dq[1]) * scale).astype(bf16)
        stack[1, :, span] = (jnp.where(first, dk[0], dk[1]) * scale).astype(bf16)
        stack[2, :, span] = jnp.where(first, dv[0], dv[1]).astype(bf16)
    stack[3] = halves(grad, t)[0]
    r0[...] = stack[q_id]
    r1[...] = stack[q_id ^ (1 + t)]
    r2[...] = stack[q_id ^ (2 - t)]
    r3[...] = stack[q_id ^ 3]
    total = nt(stack[0], wq[...]) + nt(stack[1], wk[...]) + nt(stack[2], wv[...])
    normed_part[...] = total.astype(bf16)


def tokens_back_body(experts, ids, own, other, tokens, gain, grad_res, small_ffn, bias, out, small):
    wide = tokens[...].astype(f32)
    inv = lax.rsqrt(jnp.mean(wide * wide, axis=-1, keepdims=True) + eps_norm)
    grad_normed = own[...].astype(f32) + other[...].astype(f32)
    scaled = grad_normed * gain[...][None, :]
    out[...] = (
        grad_res[...]
        + inv * scaled
        - wide * (inv * inv * inv) * jnp.mean(scaled * wide, axis=-1, keepdims=True)
    )
    small[...] = jnp.zeros_like(small)
    small[0:1, :] = jnp.sum(grad_normed * wide * inv, axis=0, keepdims=True)
    small[1:2, :] = bias[...]
    small[pl.ds(2, 1 + experts), :] = small_ffn[...]


def encode(value):
    width = value.shape[1] // 2
    tall = jnp.concatenate([value[:, :width], value[:, width:]], axis=0)
    lead = tall.astype(bf16)
    return lead, (tall - lead.astype(f32)).astype(bf16)


def decode(ref, start, rows):
    lead = ref[pl.ds(start, 2 * rows), :].astype(f32)
    return lead + ref[pl.ds(start + 2 * rows, 2 * rows), :].astype(f32)


def widen(tall):
    rows = tall.shape[0] // 2
    return jnp.concatenate([tall[:rows], tall[rows:]], axis=1)


def partial_body(groups, ids, *refs):
    early_own, early_other = refs[:4], refs[4:8]
    right, right_pair, small = refs[8:12], refs[12:16], refs[16]
    blocks, total = refs[17:-1], refs[-1]
    e, q, t = ids[0], ids[1], ids[2]
    even = t == 0
    is_last = q == 3
    tokens = right[0].shape[0]
    rows = early_own[0].shape[0]
    width = early_own[0].shape[1]
    low, high, rights = [], [], []
    normed, mixed = pl.ds(rows - 2 * tokens, tokens), pl.ds(rows - tokens, tokens)
    for p in range(4):
        mine = jnp.where(is_last, right[p][...], early_own[p][normed, :])
        other = jnp.where(is_last, right_pair[p][...], early_other[p][normed, :])
        low.append(jnp.where(even, mine, other))
        high.append(jnp.where(even, other, mine))
        rights.append(jnp.where(is_last, early_own[p][mixed, :], right[p][...]))
    rights = jnp.concatenate(rights, axis=0)
    total[:width, :] = tn(jnp.concatenate(low, axis=0), rights)
    total[width:, :] = tn(jnp.concatenate(high, axis=0), rights)
    depth = total.shape[0] // groups
    lead, rest = encode(small[...])
    for s in range(groups):
        start = pl.multiple_of((e ^ s) * depth, 8)
        blocks[s][pl.ds(0, depth), :] = total[pl.ds(start, depth), :].astype(bf16)
        blocks[s][pl.ds(depth, lead.shape[0]), :] = lead
        blocks[s][pl.ds(depth + lead.shape[0], lead.shape[0]), :] = rest


def reduce_body(groups, rows, ids, *refs):
    arrived, outs = refs[:groups], refs[groups:]
    depth = outs[0].shape[0]
    total = arrived[0][pl.ds(0, depth), :].astype(f32)
    for ref in arrived[1:]:
        total = total + ref[pl.ds(0, depth), :].astype(f32)
    outs[0][...] = total.astype(bf16)
    code, stack = outs[1:]
    for s in range(groups):
        stack[s] = decode(arrived[s], depth, rows)
    small = stack[ids[0]]
    for k in range(1, groups):
        small = small + stack[ids[0] ^ k]
    lead = small.astype(bf16)
    code[pl.ds(0, 2 * rows), :] = lead
    code[pl.ds(2 * rows, 2 * rows), :] = (small - lead.astype(f32)).astype(bf16)


def final_body(groups, experts, rows, ids, *refs):
    pieces, hot, outs = refs[:8], refs[8], refs[9:13]
    gain_attn, bias, gain_ffn, router = refs[13:17]
    stack, square, small = refs[17:]
    e, q, t = ids[0], ids[1], ids[2]
    depth = stack.shape[2]
    per = groups // 2

    def place_of(chip):
        away = q ^ chip
        return jnp.where((t == 1) & ((away == 1) | (away == 2)), 3 - away, away)

    for p in range(4):
        for s in range(groups):
            piece = pieces[s // per * 4 + p]
            stack[p, s] = piece[pl.ds(s % per * depth, depth), :].astype(f32)
        small[p] = decode(pieces[p], per * depth, rows)
    for m in range(4):
        place = place_of(m)
        for k in range(groups):
            block = stack[place, k ^ e]
            span = pl.ds(k * depth, depth)
            if m < 3:
                outs[m][span, :] = block
            else:
                square[span, :] = block
    outs[3][...] = square[...].T
    total = widen(small[place_of(0)] + small[place_of(1)] + small[place_of(2)] + small[place_of(3)])
    gain_attn[...] = total[0]
    gain_ffn[...] = total[2]
    router[...] = total[3 : 3 + experts]
    length = hot.shape[1]
    for head in range(bias.shape[0]):
        line = jnp.broadcast_to(total[1:2, head * length : (head + 1) * length], (8, length))
        value = lax.dot_general(
            line,
            hot[...],
            (((1,), (1,)), ((), ())),
            precision=lax.Precision.HIGHEST,
            preferred_element_type=f32,
        )
        bias[head : head + 1, :] = value[0:1]


def on_device(
    n_dp,
    n_tensor,
    tokens,
    seq_ids,
    routes,
    gain_attn,
    w_query,
    w_key,
    w_value,
    w_attn_out,
    rel_bias,
    gain_ffn,
    w_router,
    expert_in,
    expert_out,
    cotangent,
):
    groups = n_dp // 4
    length, width = tokens.shape
    half = width // 2
    experts = w_router.shape[1]
    bucket_count = rel_bias.shape[1]
    heads = rel_bias.shape[0]
    local = w_query.shape[1]
    capacity = 4 * ((5 * TOP * length + 16 * experts - 1) // (16 * experts))
    stride = -(-capacity // 16) * 16
    slot_count = experts * stride
    dp_id = lax.axis_index("dp")
    t_id = lax.axis_index("tensor")
    ids = jnp.stack([dp_id // 4, dp_id % 4, t_id]).astype(jnp.int32)

    def send(array, target, only=None):
        pairs = []
        for dp in range(n_dp):
            for t in range(n_tensor):
                e_to, q_to, t_to = target(dp // 4, dp % 4, t)
                if only is None or q_to == only:
                    pairs.append((dp * n_tensor + t, (e_to * 4 + q_to) * n_tensor + t_to))
        return lax.ppermute(array, ("dp", "tensor"), pairs)

    def to_pair(e, q, t):
        return e, q, 1 - t

    def to_first(e, q, t):
        return e, q ^ (1 + t), t

    def to_second(e, q, t):
        return e, q ^ (2 - t), t

    def to_far(e, q, t):
        return e, q ^ 3, t

    def to_group(step):
        return lambda e, q, t: (e ^ step, q, t)

    def exchange(chunks):
        return [chunks[0]] + [send(chunks[s], to_group(s)) for s in range(1, len(chunks))]

    def join(arrays):
        rows = sum(a.shape[0] for a in arrays)
        return call(join_body, "join", ids, [((rows, arrays[0].shape[1]), arrays[0].dtype)], *arrays)[0]

    def spread_first(block):
        return block, send(block, to_first), send(block, to_second)

    def spread_rest(block, first, second):
        own = [block, first, second, send(first, to_second)]
        other = [send(piece, to_pair) for piece in own]
        return own, [other[0], other[2], other[1], other[3]]

    routes_t = routes.T
    gain_one, gain_two = gain_attn, gain_ffn
    router_t = w_router.T
    distance_bucket = bucket_of_distance(length, bucket_count, REACH)
    hot = (
        distance_bucket[(-np.arange(length)) % length][None, :] == np.arange(bucket_count)[:, None]
    ).astype(np.float32)
    hot = jnp.asarray(hot)

    chunk = ((stride, half), bf16)
    local_out = ((length, local), bf16)
    slots, *cot_chunks = call(
        functools.partial(route_body, experts, stride),
        "route",
        ids,
        [((TOP, length), jnp.int32)] + [chunk] * experts,
        routes_t,
        cotangent,
        scratch=[
            pltpu.VMEM((TOP, length), jnp.int32),
            pltpu.VMEM((length, width), bf16),
            pltpu.SemaphoreType.DMA((2,)),
        ],
        far=(0, 1),
    )
    cot_arrived = exchange(cot_chunks)
    early, att_part, queries, keys, values, probs = call(
        front_body,
        "front",
        ids,
        [((2 * length, half), bf16), ((length, width), f32)]
        + [local_out] * 3
        + [((heads, length, length), f32)],
        tokens,
        gain_one,
        w_query,
        w_key,
        w_value,
        rel_bias,
        hot,
        seq_ids.reshape(1, length),
        w_attn_out,
        scratch=[pltpu.VMEM((length, width), bf16), pltpu.VMEM((width,), f32)]
        + [pltpu.VMEM((width, local), bf16)] * 3
        + [
            pltpu.VMEM(rel_bias.shape, f32),
            pltpu.VMEM(hot.shape, f32),
            pltpu.VMEM((1, length), jnp.int32),
            pltpu.VMEM((local, width), bf16),
            pltpu.SemaphoreType.DMA((9,)),
        ],
        far=range(9),
    )
    att_part, *cot_arrived = lax.optimization_barrier((att_part, *cot_arrived))
    cot_near = spread_first(join(cot_arrived + [early]))
    att_other = send(att_part, to_pair)
    residual, normed_two, router_probs, *row_chunks = call(
        functools.partial(middle_body, experts, stride),
        "middle",
        ids,
        [((length, width), f32), ((length, width), bf16), ((length, experts), f32)]
        + [chunk] * experts,
        att_part,
        att_other,
        tokens,
        gain_two,
        router_t,
        slots,
    )
    *row_arrived, near, next_near = lax.optimization_barrier((*exchange(row_chunks), *cot_near[1:]))
    row_own, row_other = spread_rest(*spread_first(join(row_arrived)))
    cot_own, cot_other = spread_rest(cot_near[0], near, next_near)

    all_rows = 4 * slot_count
    rows_half = ((all_rows, half), bf16)
    units = expert_in.shape[2]
    act, slope, part_mine, part_other = call(
        functools.partial(expert_body, slot_count),
        "expert",
        ids,
        [((all_rows, units), bf16), ((all_rows, units), f32), rows_half, rows_half],
        *row_own,
        *row_other,
        expert_in,
        expert_out,
        limit=40,
    )
    two = ((2 * slot_count, half), bf16)
    one = ((slot_count, half), bf16)
    one_wide = ((slot_count, half), f32)

    keep, go = call(pair_sum_body, "pair_sum", ids, [two, two], part_mine, send(part_other, to_pair))
    part_kept, go = call(
        plane_sum_body, "plane_sum", ids, [one_wide, one], keep, send(go, to_first)
    )
    part_last = send(go, to_second)
    grad_pre, grad_mine, grad_other, back_mine, back_other = call(
        functools.partial(expert_back_body, slot_count, experts),
        "expert_back",
        ids,
        [((all_rows, units), bf16), rows_half, rows_half, rows_half, rows_half],
        *row_own,
        *row_other,
        *cot_own,
        *cot_other,
        expert_in,
        expert_out,
        router_t,
        slope,
        limit=40,
    )
    keep, go = call(pair_sum_body, "pair_sum", ids, [two, two], back_mine, send(back_other, to_pair))
    back_kept, go = call(
        plane_sum_body, "plane_sum", ids, [one_wide, one], keep, send(go, to_first)
    )
    back_last = send(go, to_second)
    grad_in, grad_out = call(
        functools.partial(expert_grads_body, slot_count),
        "expert_grads",
        ids,
        [(expert_in.shape, f32), (expert_out.shape, f32)],
        *row_own,
        *row_other,
        act,
        grad_pre,
        grad_mine,
        grad_other,
        limit=40,
    )
    part_last, back_last, grad_in, grad_out = lax.optimization_barrier(
        (part_last, back_last, grad_in, grad_out)
    )
    chunks = call(
        functools.partial(last_sum_body, experts, stride),
        "last_sum",
        ids,
        [((2 * stride, half), bf16)] * experts,
        part_kept,
        part_last,
        back_kept,
        back_last,
    )
    returned = exchange(chunks)
    packed = call(
        functools.partial(combine_body, experts, stride),
        "combine",
        ids,
        [((length, width + LANES), f32)],
        *returned,
        slots,
        routes_t,
        router_probs,
        cotangent,
        residual,
    )[0]
    output, grad_residual, grad_att, small_ffn = call(
        functools.partial(norm_back_body, experts),
        "norm_back",
        ids,
        [
            ((length, width), bf16),
            ((length, width), f32),
            ((length, width), bf16),
            ((1 + experts, width), f32),
        ],
        packed,
        send(packed, to_pair),
        normed_two,
        router_probs,
        residual,
        routes_t,
        cotangent,
        gain_two,
        router_t,
    )
    right0, right1, right2, right3, normed_part, bias = call(
        attend_back_body,
        "attend_back",
        ids,
        [local_out] * 4 + [((length, width), bf16), ((1, heads * length), f32)],
        grad_att,
        w_attn_out,
        queries,
        keys,
        values,
        early,
        probs,
        w_query,
        w_key,
        w_value,
        scratch=[pltpu.VMEM((4, length, local), bf16)],
    )
    right_all = [right0, send(right1, to_first), send(right2, to_second), send(right3, to_far)]
    small_rows = -(-(3 + experts) // 8) * 8
    grad_tokens, small = call(
        functools.partial(tokens_back_body, experts),
        "tokens_back",
        ids,
        [((length, width), f32), ((small_rows, width), f32)],
        normed_part,
        send(normed_part, to_pair),
        tokens,
        gain_one,
        grad_residual,
        small_ffn,
        bias,
    )
    right_all[1], small = lax.optimization_barrier((right_all[1], small))
    right_pair = [send(right_all[p], to_pair) for p in (0, 2, 1, 3)]
    depth = width // groups
    blocks = call(
        functools.partial(partial_body, groups),
        "partial",
        ids,
        [((depth + 4 * small_rows, local), bf16)] * groups,
        *cot_own,
        *cot_other,
        *right_all,
        *right_pair,
        small,
        scratch=[pltpu.VMEM((width, local), f32)],
    )
    reduced, code = call(
        functools.partial(reduce_body, groups, small_rows),
        "reduce",
        ids,
        [((depth, local), bf16), ((4 * small_rows, local), bf16)],
        *exchange(blocks),
        scratch=[pltpu.VMEM((groups, 2 * small_rows, local), f32)],
    )
    spread = exchange([reduced] * groups)
    near, rest = spread[: groups // 2], spread[groups // 2 :]
    matrix = join(near + [code])
    first, second = send(matrix, to_first), send(matrix, to_second)
    *rest, first, second = lax.optimization_barrier((*rest, first, second))
    far = send(first, to_second)
    matrix_two = join(list(rest))
    first_two, second_two = send(matrix_two, to_first), send(matrix_two, to_second)
    far_two = send(second_two, to_first)
    grads = call(
        functools.partial(final_body, groups, experts, small_rows),
        "final",
        ids,
        [((width, local), f32)] * 3
        + [((local, width), f32), ((width,), f32), ((heads, bucket_count), f32)]
        + [((width,), f32), ((experts, width), f32)],
        matrix,
        first,
        second,
        far,
        matrix_two,
        first_two,
        second_two,
        far_two,
        hot,
        scratch=[
            pltpu.VMEM((4, groups, depth, local), f32),
            pltpu.VMEM((width, local), f32),
            pltpu.VMEM((4, 2 * small_rows, local), f32),
        ],
        limit=40,
    )
    return (
        output,
        grad_tokens,
        grads[4],
        grads[0],
        grads[1],
        grads[2],
        grads[3],
        grads[5],
        grads[6],
        grads[7].T,
        grad_in,
        grad_out,
    )


def solution(mesh):
    in_specs = (
        P("dp", None),
        P("dp"),
        P("dp", None),
        P(),
        P(None, "tensor"),
        P(None, "tensor"),
        P(None, "tensor"),
        P("tensor", None),
        P("tensor", None),
        P(),
        P(),
        P("dp", None, "tensor"),
        P("dp", "tensor", None),
        P("dp", None),
    )
    out_specs = (
        P("dp", None),
        P("dp", None),
        P(),
        P(None, "tensor"),
        P(None, "tensor"),
        P(None, "tensor"),
        P("tensor", None),
        P("tensor", None),
        P(),
        P(),
        P("dp", None, "tensor"),
        P("dp", "tensor", None),
    )
    return jax.shard_map(
        functools.partial(on_device, mesh.shape["dp"], mesh.shape["tensor"]),
        mesh=mesh,
        in_specs=in_specs,
        out_specs=out_specs,
        check_vma=False,
    )
```

time: 505 us -> 171 us (0.34)
  waiting for transfers between devices: 294 us -> 78.6 us
  blocking collectives: 82.3 us -> 0 us
  matrix products: 41.1 us -> 0 us
  Pallas kernels: 0 us -> 39.7 us
  local copies, waits for them, and re-layouts: 20.1 us -> 0.06 us
  other arithmetic: 16.8 us -> 0.08 us
  starting transfers between devices: 35.3 us -> 51.5 us
  between operations: 14.6 us -> 0.97 us
    psum x4 -> x0, waiting for transfers between devices: 155 us -> none  [the longest x1 106 us: on_device(): lax.psum((grad_gain_attn, grad_query, grad_key, grad_value, grad_attn_out...]
    all_to_all x4 -> x0, waiting for transfers between devices: 139 us -> none  [the longest x2 74.1 us: to_experts(): lax.all_to_all(repeated.reshape(experts * 4, capacity, row_width), 'dp',...]
    psum x2 -> x0, blocking collectives: 82.3 us -> none  [the longest x1 79.7 us: on_device(): lax.psum((grad_gain_attn, grad_query, grad_key, grad_value, grad_attn_out...]
    ppermute x0 -> x51, waiting for transfers between devices: none -> 78.6 us  [send(): return lax.ppermute(array, ('dp', 'tensor'), pairs)]
    ppermute x0 -> x51, starting transfers between devices: none -> 51.5 us  [send(): return lax.ppermute(array, ('dp', 'tensor'), pairs)]
    dot_general x32 -> x0, matrix products: 41.1 us -> none  [the longest x1 4.33 us: on_device(): jnp.dot(grad_rows, weight_out.T, preferred_element_type=jnp.float32)]
    pallas_call x0 -> x22, Pallas kernels: none -> 39.7 us  [call(): pl.pallas_call(body, out_shape=shapes, in_specs=[pl.BlockSpec(memory_spac...]
    all_to_all x4 -> x0, starting transfers between devices: 34.9 us -> none  [the longest x2 18 us: from_experts(): lax.all_to_all(part_rows.reshape(sources, capacity, row_width), 'dp', spl...]
  transfers between devices with their start and end apart: 8 -> 51, of which waited for: 8 -> 26; matrix products, arithmetic and copies ran while one was open for 7% -> 0% of each run, Pallas kernels for 0% -> 14%
where the time goes in v2:
time: 171 us
  waiting for transfers between devices  78.6 us (46%)
  starting transfers between devices  51.5 us (30%)
  Pallas kernels  39.7 us (23%)
    ppermute x51, waiting for transfers between devices, send(): return lax.ppermute(array, ('dp', 'tensor'), pairs)  78.6 us
    ppermute x51, starting transfers between devices, send(): return lax.ppermute(array, ('dp', 'tensor'), pairs)  51.5 us
    pallas_call x22, Pallas kernels, call(): pl.pallas_call(body, out_shape=shapes, in_specs=[pl.BlockSpec(memory_spac...  39.7 us
  transfers between devices with their start and end apart: 51, of which 26 were waited for; matrix products, arithmetic and copies ran while one was open for 0% of the time, Pallas kernels for 14%

profile of v2, /device:TPU:0, one launch (start us, length us, event | category | flops | bytes accessed | tf_op | source)
XLA Modules:
  0.0 170.9 jit_solution(5309690249467130758)
XLA Ops:
  2.5 3.1 %collective-permute-start = (bf16[80,384]{1,0:T(8,128)(2,1)S(1)}, bf16[80,384]{1,0:T(8,128)(2,1)S(1)}, u32[]{:S(2)}, u32[]{:S(2)}) collective-permute-start(bf16[80,384]{1,0:T(8,128)(2,1)S(1)} %get-tuple-element.102), channel_id=1, source_target_pairs={{0,8},{1,9},{2,10},{3,11},{4,12},{5,13},{6,14},{7,15},{8,0},{9,1},... | collective-permute-start | bytes 184328 | tf_op jit(solution)/shard_map/ppermute | solution.py:590
  5.6 2.6 %collective-permute-start.1 = (bf16[80,384]{1,0:T(8,128)(2,1)S(1)}, bf16[80,384]{1,0:T(8,128)(2,1)S(1)}, u32[]{:S(2)}, u32[]{:S(2)}) collective-permute-start(bf16[80,384]{1,0:T(8,128)(2,1)S(1)} %get-tuple-element.103), channel_id=1, source_target_pairs={{0,16},{1,17},{2,18},{3,19},{4,20},{5,21},{6,22},{7,23},{8,24},{9,... | collective-permute-start | bytes 184328 | tf_op jit(solution)/shard_map/ppermute | solution.py:590
  8.2 4.8 %front.1 = (bf16[256,384]{1,0:T(8,128)(2,1)S(1)}, f32[128,768]{1,0:T(8,128)S(1)}, bf16[128,384]{1,0:T(8,128)(2,1)S(1)}, bf16[128,384]{1,0:T(8,128)(2,1)S(1)}, bf...) custom-call(s32[3]{0:T(128)S(1)} %pad_add_fusion.ids, bf16[128,768]{1,0:T(8,128)(2,1)} %tokens.3, f32[768]{0:T(1024)} %gain.5, ...), custom_call_target="tpu_custom_call" | custom-call | bytes 18000000 | tf_op jit(solution)/shard_map/front/pallas_call | solution.py:53
  19.1 3.3 %collective-permute-start.5 = (bf16[80,384]{1,0:T(8,128)(2,1)S(1)}, bf16[80,384]{1,0:T(8,128)(2,1)S(1)}, u32[]{:S(2)}, u32[]{:S(2)}) collective-permute-start(bf16[80,384]{1,0:T(8,128)(2,1)S(1)} %get-tuple-element.109), channel_id=1, source_target_pairs={{0,16},{1,17},{2,18},{3,19},{4,20},{5,21},{6,22},{7,23},{8,24},{9,... | collective-permute-start | bytes 184328 | tf_op jit(solution)/shard_map/ppermute | solution.py:590
  23.5 3.7 %collective-permute-done.7.refs_9_.refs_1_ = bf16[576,384]{1,0:T(8,128)(2,1)S(1)} collective-permute-done((bf16[576,384]{1,0:T(8,128)(2,1)S(1)}, bf16[576,384]{1,0:T(8,128)(2,1)S(1)}, u32[]{:S(2)}, u32[]{:S(2)}) %collective-permute-start.7) | collective-permute-done | bytes 442400 | tf_op jit(solution)/shard_map/ppermute | solution.py:590
  31.6 6.2 %collective-permute-done.9.refs_1_ = bf16[320,384]{1,0:T(8,128)(2,1)S(1)} collective-permute-done((bf16[320,384]{1,0:T(8,128)(2,1)S(1)}, bf16[320,384]{1,0:T(8,128)(2,1)S(1)}, u32[]{:S(2)}, u32[]{:S(2)}) %collective-permute-start.9) | collective-permute-done | bytes 245792 | tf_op jit(solution)/shard_map/ppermute | solution.py:590
  46.9 4.3 %expert.1 = (bf16[1280,384]{1,0:T(8,128)(2,1)S(1)}, f32[1280,384]{1,0:T(8,128)S(1)}, bf16[1280,384]{1,0:T(8,128)(2,1)S(1)}, bf16[1280,384]{1,0:T(8,128)(2,1)S(1)}) custom-call(s32[3]{0:T(128)S(1)} %pad_add_fusion.ids, bf16[320,384]{1,0:T(8,128)(2,1)S(1)} %join.5.refs_0_, bf16[320,384]{1,0:T(8,128)(2,1)S(1)} %collective-permute-done.9.refs_1_, ...), custom_call_target="tpu_custom_call" | custom-call | bytes 15840000 | tf_op jit(solution)/shard_map/expert/pallas_call | solution.py:53
  51.6 5.4 %expert_back.1 = (bf16[1280,384]{1,0:T(8,128)(2,1)S(1)}, bf16[1280,384]{1,0:T(8,128)(2,1)S(1)}, bf16[1280,384]{1,0:T(8,128)(2,1)S(1)}, bf16[1280,384]{1,0:T(8,128)(2,1)S(1)}, bf16[1280,384]{1,0:T(8,128)(2,1)S(1)}) custom-call(s32[3]{0:T(128)S(1)} %pad_add_fusion.ids, bf16[320,384]{1,0:T(8,128)(2,1)S(1)} %join.5.refs_0_, ...), custom_call_target="tpu_custom_call" | custom-call | bytes 19440000 | tf_op jit(solution)/shard_map/expert_back/pallas_call | solution.py:53
  61.7 5.4 %collective-permute-done.17.received = bf16[640,384]{1,0:T(8,128)(2,1)S(1)} collective-permute-done((bf16[640,384]{1,0:T(8,128)(2,1)S(1)}, bf16[640,384]{1,0:T(8,128)(2,1)S(1)}, u32[]{:S(2)}, u32[]{:S(2)}) %collective-permute-start.17) | collective-permute-done | bytes 491552 | tf_op jit(solution)/shard_map/ppermute | solution.py:590
  68.8 5.9 %collective-permute-done.25.received = bf16[640,384]{1,0:T(8,128)(2,1)S(1)} collective-permute-done((bf16[640,384]{1,0:T(8,128)(2,1)S(1)}, bf16[640,384]{1,0:T(8,128)(2,1)S(1)}, u32[]{:S(2)}, u32[]{:S(2)}) %collective-permute-start.25) | collective-permute-done | bytes 491552 | tf_op jit(solution)/shard_map/ppermute | solution.py:590
  76.4 3.9 %expert_grads.1 = (f32[1,768,384]{2,1,0:T(8,128)}, f32[1,384,768]{2,1,0:T(8,128)}) custom-call(s32[3]{0:T(128)S(1)} %pad_add_fusion.ids, bf16[320,384]{1,0:T(8,128)(2,1)S(1)} %join.5.refs_0_, bf16[320,384]{1,0:T(8,128)(2,1)S(1)} %collective-permute-done.9.refs_1_, bf16[320,384]{1,0:T(8,128)(2,1)S(1)} %collective-permute-done.10.refs_2_, ...), custom_call_target="tpu_custom_call" | custom-call | bytes 14400000 | tf_op jit(solution)/shard_map/expert_grads/pallas_call | solution.py:53
  82.4 2.9 %collective-permute-start.28 = (bf16[160,384]{1,0:T(8,128)(2,1)S(1)}, bf16[160,384]{1,0:T(8,128)(2,1)S(1)}, u32[]{:S(2)}, u32[]{:S(2)}) collective-permute-start(bf16[160,384]{1,0:T(8,128)(2,1)S(1)} %get-tuple-element.145), channel_id=1, source_target_pairs={{0,16},{1,17},{2,18},{3,19},{4,20},{5,21},{6,22},{7,23},{8,24},{9,... | collective-permute-start | bytes 368648 | tf_op jit(solution)/shard_map/ppermute | solution.py:590
  86.8 2.3 %collective-permute-done.27.refs_1_ = bf16[160,384]{1,0:T(8,128)(2,1)S(1)} collective-permute-done((bf16[160,384]{1,0:T(8,128)(2,1)S(1)}, bf16[160,384]{1,0:T(8,128)(2,1)S(1)}, u32[]{:S(2)}, u32[]{:S(2)}) %collective-permute-start.27) | collective-permute-done | bytes 122912 | tf_op jit(solution)/shard_map/ppermute | solution.py:590
  97.2 2.4 %attend_back.1 = (bf16[128,384]{1,0:T(8,128)(2,1)S(1)}, bf16[128,384]{1,0:T(8,128)(2,1)S(1)}, bf16[128,384]{1,0:T(8,128)(2,1)S(1)}, bf16[128,384]{1,0:T(8,128)(2...) custom-call(s32[3]{0:T(128)S(1)} %pad_add_fusion.ids, bf16[128,768]{1,0:T(8,128)(2,1)S(1)} %get-tuple-element.151.att, ...), custom_call_target="tpu_custom_call" | custom-call | bytes 9000000 | tf_op jit(solution)/shard_map/attend_back/pallas_call | solution.py:53
  104.4 2.6 %collective-permute-done.34.refs_11_ = bf16[128,384]{1,0:T(8,128)(2,1)S(1)} collective-permute-done((bf16[128,384]{1,0:T(8,128)(2,1)S(1)}, bf16[128,384]{1,0:T(8,128)(2,1)S(1)}, u32[]{:S(2)}, u32[]{:S(2)}) %collective-permute-start.34) | collective-permute-done | bytes 98336 | tf_op jit(solution)/shard_map/ppermute | solution.py:590
  115.8 5.4 %collective-permute-done.39.refs_1_ = bf16[224,384]{1,0:T(8,128)(2,1)S(1)} collective-permute-done((bf16[224,384]{1,0:T(8,128)(2,1)S(1)}, bf16[224,384]{1,0:T(8,128)(2,1)S(1)}, u32[]{:S(2)}, u32[]{:S(2)}) %collective-permute-start.39) | collective-permute-done | bytes 172064 | tf_op jit(solution)/shard_map/ppermute | solution.py:590
  121.2 7.0 %collective-permute-done.40.refs_2_ = bf16[224,384]{1,0:T(8,128)(2,1)S(1)} collective-permute-done((bf16[224,384]{1,0:T(8,128)(2,1)S(1)}, bf16[224,384]{1,0:T(8,128)(2,1)S(1)}, u32[]{:S(2)}, u32[]{:S(2)}) %collective-permute-start.40) | collective-permute-done | bytes 172064 | tf_op jit(solution)/shard_map/ppermute | solution.py:590
  128.9 3.4 %collective-permute-start.42 = (bf16[192,384]{1,0:T(8,128)(2,1)S(1)}, bf16[192,384]{1,0:T(8,128)(2,1)S(1)}, u32[]{:S(2)}, u32[]{:S(2)}) collective-permute-start(bf16[192,384]{1,0:T(8,128)(2,1)S(1)} %get-tuple-element.172.refs_0_), channel_id=1, source_target_pairs={{0,8},{1,9},{2,10},{3,11},{4,12},{5,13},{6,14},{7,15},{8,0},{9,1},... | collective-permute-start | bytes 442376 | tf_op jit(solution)/shard_map/ppermute | solution.py:590
  132.3 3.2 %collective-permute-done.42.refs_1_ = bf16[192,384]{1,0:T(8,128)(2,1)S(1)} collective-permute-done((bf16[192,384]{1,0:T(8,128)(2,1)S(1)}, bf16[192,384]{1,0:T(8,128)(2,1)S(1)}, u32[]{:S(2)}, u32[]{:S(2)}) %collective-permute-start.42) | collective-permute-done | bytes 147488 | tf_op jit(solution)/shard_map/ppermute | solution.py:590
  138.2 3.1 %collective-permute-start.43 = (bf16[192,384]{1,0:T(8,128)(2,1)S(1)}, bf16[192,384]{1,0:T(8,128)(2,1)S(1)}, u32[]{:S(2)}, u32[]{:S(2)}) collective-permute-start(bf16[192,384]{1,0:T(8,128)(2,1)S(1)} %get-tuple-element.172.refs_0_), channel_id=1, source_target_pairs={{0,16},{1,17},{2,18},{3,19},{4,20},{5,21},{6,22},{7,23},{8,24},{9,... | collective-permute-start | bytes 442376 | tf_op jit(solution)/shard_map/ppermute | solution.py:590
  142.6 8.0 %collective-permute-done.43.refs_0_ = bf16[192,384]{1,0:T(8,128)(2,1)S(1)} collective-permute-done((bf16[192,384]{1,0:T(8,128)(2,1)S(1)}, bf16[192,384]{1,0:T(8,128)(2,1)S(1)}, u32[]{:S(2)}, u32[]{:S(2)}) %collective-permute-start.43) | collective-permute-done | bytes 147488 | tf_op jit(solution)/shard_map/ppermute | solution.py:590
  154.4 6.4 %collective-permute-done.49.refs_6_ = bf16[384,384]{1,0:T(8,128)(2,1)S(1)} collective-permute-done((bf16[384,384]{1,0:T(8,128)(2,1)S(1)}, bf16[384,384]{1,0:T(8,128)(2,1)S(1)}, u32[]{:S(2)}, u32[]{:S(2)}) %collective-permute-start.49) | collective-permute-done | bytes 294944 | tf_op jit(solution)/shard_map/ppermute | solution.py:590
  164.2 3.3 %collective-permute-done.50.refs_7_ = bf16[384,384]{1,0:T(8,128)(2,1)S(1)} collective-permute-done((bf16[384,384]{1,0:T(8,128)(2,1)S(1)}, bf16[384,384]{1,0:T(8,128)(2,1)S(1)}, u32[]{:S(2)}, u32[]{:S(2)}) %collective-permute-start.50) | collective-permute-done | bytes 294944 | tf_op jit(solution)/shard_map/ppermute | solution.py:590
  167.5 3.4 %final.1 = (f32[768,384]{1,0:T(8,128)}, f32[768,384]{1,0:T(8,128)}, f32[768,384]{1,0:T(8,128)}, f32[384,768]{1,0:T(8,128)}, f32[768]{0:T(1024)}, /*index=5*/f32[6,32]{1,0:T(8,128)}, f32[768]{0:T(1024)}, f32[4,768]{1,0:T(4,128)}) custom-call(s32[3]{0:T(128)S(1)} %pad_add_fusion.ids, bf16[416,384]{1,0:T(8,128)(2,1)S(1)} %join.6.refs_0_, ...), custom_call_target="tpu_custom_call" | custom-call | bytes 14040000 | tf_op jit(solution)/shard_map/final/pallas_call | solution.py:53
  (127 shorter events, 67.9 us)
Async XLA Ops:
  2.5 10.5 %collective-permute-start = (bf16[80,384]{1,0:T(8,128)(2,1)S(1)}, bf16[80,384]{1,0:T(8,128)(2,1)S(1)}, u32[]{:S(2)}, u32[]{:S(2)}) collective-permute-start(bf16[80,384]{1,0:T(8,128)(2,1)S(1)} %get-tuple-element.102), channel_id=1, source_target_pairs={{0,8},{1,9},{2,10},{3,11},{4,12},{5,13},{6,14},{7,15},{8,0},{9,1},... | collective-permute-start | bytes 184328 | tf_op jit(solution)/shard_map/ppermute | solution.py:590
  14.8 12.4 %collective-permute-start.7 = (bf16[576,384]{1,0:T(8,128)(2,1)S(1)}, bf16[576,384]{1,0:T(8,128)(2,1)S(1)}, u32[]{:S(2)}, u32[]{:S(2)}) collective-permute-start(bf16[576,384]{1,0:T(8,128)(2,1)S(1)} %join.4.refs_8_.refs_0_), channel_id=1, source_target_pairs={{0,2},{1,5},{2,0},{3,7},{4,6},{5,1},{6,4},{7,3},{8,10},{9,13},{10,... | collective-permute-start | bytes 1327112 | tf_op jit(solution)/shard_map/ppermute | solution.py:590
  16.4 11.1 %collective-permute-start.8 = (bf16[576,384]{1,0:T(8,128)(2,1)S(1)}, bf16[576,384]{1,0:T(8,128)(2,1)S(1)}, u32[]{:S(2)}, u32[]{:S(2)}) collective-permute-start(bf16[576,384]{1,0:T(8,128)(2,1)S(1)} %join.4.refs_8_.refs_0_), channel_id=1, source_target_pairs={{0,4},{1,3},{2,6},{3,1},{4,0},{5,7},{6,2},{7,5},{8,12},{9,11},{10,... | collective-permute-start | bytes 1327112 | tf_op jit(solution)/shard_map/ppermute | solution.py:590
  19.0 8.4 %collective-permute-start.4 = (bf16[80,384]{1,0:T(8,128)(2,1)S(1)}, bf16[80,384]{1,0:T(8,128)(2,1)S(1)}, u32[]{:S(2)}, u32[]{:S(2)}) collective-permute-start(bf16[80,384]{1,0:T(8,128)(2,1)S(1)} %get-tuple-element.108), channel_id=1, source_target_pairs={{0,8},{1,9},{2,10},{3,11},{4,12},{5,13},{6,14},{7,15},{8,0},{9,1},... | collective-permute-start | bytes 184328 | tf_op jit(solution)/shard_map/ppermute | solution.py:590
  19.1 8.3 %collective-permute-start.5 = (bf16[80,384]{1,0:T(8,128)(2,1)S(1)}, bf16[80,384]{1,0:T(8,128)(2,1)S(1)}, u32[]{:S(2)}, u32[]{:S(2)}) collective-permute-start(bf16[80,384]{1,0:T(8,128)(2,1)S(1)} %get-tuple-element.109), channel_id=1, source_target_pairs={{0,16},{1,17},{2,18},{3,19},{4,20},{5,21},{6,22},{7,23},{8,24},{9,... | collective-permute-start | bytes 184328 | tf_op jit(solution)/shard_map/ppermute | solution.py:590
  29.0 8.8 %collective-permute-start.9 = (bf16[320,384]{1,0:T(8,128)(2,1)S(1)}, bf16[320,384]{1,0:T(8,128)(2,1)S(1)}, u32[]{:S(2)}, u32[]{:S(2)}) collective-permute-start(bf16[320,384]{1,0:T(8,128)(2,1)S(1)} %join.5.refs_0_), channel_id=1, source_target_pairs={{0,2},{1,5},{2,0},{3,7},{4,6},{5,1},{6,4},{7,3},{8,10},{9,13},{10,... | collective-permute-start | bytes 737288 | tf_op jit(solution)/shard_map/ppermute | solution.py:590
  29.6 9.0 %collective-permute-start.10 = (bf16[320,384]{1,0:T(8,128)(2,1)S(1)}, bf16[320,384]{1,0:T(8,128)(2,1)S(1)}, u32[]{:S(2)}, u32[]{:S(2)}) collective-permute-start(bf16[320,384]{1,0:T(8,128)(2,1)S(1)} %join.5.refs_0_), channel_id=1, source_target_pairs={{0,4},{1,3},{2,6},{3,1},{4,0},{5,7},{6,2},{7,5},{8,12},{9,11},{10,... | collective-permute-start | bytes 737288 | tf_op jit(solution)/shard_map/ppermute | solution.py:590
  31.3 9.9 %collective-permute-start.19 = (bf16[576,384]{1,0:T(8,128)(2,1)S(1)}, bf16[576,384]{1,0:T(8,128)(2,1)S(1)}, u32[]{:S(2)}, u32[]{:S(2)}) collective-permute-start(bf16[576,384]{1,0:T(8,128)(2,1)S(1)} %collective-permute-done.7.refs_9_.refs_1_), channel_id=1, source_target_pairs={{0,4},{1,3},{2,6},{3,1},{4,0},{5,7},{6,2},{7,5},{8,12},{9,11},{10,... | collective-permute-start | bytes 1327112 | tf_op jit(solution)/shard_map/ppermute | solution.py:590
  39.1 12.5 %collective-permute-start.20 = (bf16[576,384]{1,0:T(8,128)(2,1)S(1)}, bf16[576,384]{1,0:T(8,128)(2,1)S(1)}, u32[]{:S(2)}, u32[]{:S(2)}) collective-permute-start(bf16[576,384]{1,0:T(8,128)(2,1)S(1)} %join.4.refs_8_.refs_0_), channel_id=1, source_target_pairs={{0,1},{1,0},{2,3},{3,2},{4,5},{5,4},{6,7},{7,6},{8,9},{9,8},{10,11... | collective-permute-start | bytes 1327112 | tf_op jit(solution)/shard_map/ppermute | solution.py:590
  41.3 10.3 %collective-permute-start.22 = (bf16[576,384]{1,0:T(8,128)(2,1)S(1)}, bf16[576,384]{1,0:T(8,128)(2,1)S(1)}, u32[]{:S(2)}, u32[]{:S(2)}) collective-permute-start(bf16[576,384]{1,0:T(8,128)(2,1)S(1)} %collective-permute-done.7.refs_9_.refs_1_), channel_id=1, source_target_pairs={{0,1},{1,0},{2,3},{3,2},{4,5},{5,4},{6,7},{7,6},{8,9},{9,8},{10,11... | collective-permute-start | bytes 1327112 | tf_op jit(solution)/shard_map/ppermute | solution.py:590
  58.2 8.9 %collective-permute-start.17 = (bf16[640,384]{1,0:T(8,128)(2,1)S(1)}, bf16[640,384]{1,0:T(8,128)(2,1)S(1)}, u32[]{:S(2)}, u32[]{:S(2)}) collective-permute-start(bf16[640,384]{1,0:T(8,128)(2,1)S(1)} %get-tuple-element.123), channel_id=1, source_target_pairs={{0,2},{1,5},{2,0},{3,7},{4,6},{5,1},{6,4},{7,3},{8,10},{9,13},{10,... | collective-permute-start | bytes 1474568 | tf_op jit(solution)/shard_map/ppermute | solution.py:590
  60.4 14.3 %collective-permute-start.25 = (bf16[640,384]{1,0:T(8,128)(2,1)S(1)}, bf16[640,384]{1,0:T(8,128)(2,1)S(1)}, u32[]{:S(2)}, u32[]{:S(2)}) collective-permute-start(bf16[640,384]{1,0:T(8,128)(2,1)S(1)} %get-tuple-element.132), channel_id=1, source_target_pairs={{0,2},{1,5},{2,0},{3,7},{4,6},{5,1},{6,4},{7,3},{8,10},{9,13},{10,... | collective-permute-start | bytes 1474568 | tf_op jit(solution)/shard_map/ppermute | solution.py:590
  67.7 12.6 %collective-permute-start.18 = (bf16[320,384]{1,0:T(8,128)(2,1)S(1)}, bf16[320,384]{1,0:T(8,128)(2,1)S(1)}, u32[]{:S(2)}, u32[]{:S(2)}) collective-permute-start(bf16[320,384]{1,0:T(8,128)(2,1)S(1)} %get-tuple-element.125), channel_id=1, source_target_pairs={{0,4},{1,3},{2,6},{3,1},{4,0},{5,7},{6,2},{7,5},{8,12},{9,11},{10,... | collective-permute-start | bytes 737288 | tf_op jit(solution)/shard_map/ppermute | solution.py:590
  82.4 7.8 %collective-permute-start.28 = (bf16[160,384]{1,0:T(8,128)(2,1)S(1)}, bf16[160,384]{1,0:T(8,128)(2,1)S(1)}, u32[]{:S(2)}, u32[]{:S(2)}) collective-permute-start(bf16[160,384]{1,0:T(8,128)(2,1)S(1)} %get-tuple-element.145), channel_id=1, source_target_pairs={{0,16},{1,17},{2,18},{3,19},{4,20},{5,21},{6,22},{7,23},{8,24},{9,... | collective-permute-start | bytes 368648 | tf_op jit(solution)/shard_map/ppermute | solution.py:590
  111.3 9.9 %collective-permute-start.39 = (bf16[224,384]{1,0:T(8,128)(2,1)S(1)}, bf16[224,384]{1,0:T(8,128)(2,1)S(1)}, u32[]{:S(2)}, u32[]{:S(2)}) collective-permute-start(bf16[224,384]{1,0:T(8,128)(2,1)S(1)} %get-tuple-element.169), channel_id=1, source_target_pairs={{0,8},{1,9},{2,10},{3,11},{4,12},{5,13},{6,14},{7,15},{8,0},{9,1},... | collective-permute-start | bytes 516104 | tf_op jit(solution)/shard_map/ppermute | solution.py:590
  112.7 15.6 %collective-permute-start.40 = (bf16[224,384]{1,0:T(8,128)(2,1)S(1)}, bf16[224,384]{1,0:T(8,128)(2,1)S(1)}, u32[]{:S(2)}, u32[]{:S(2)}) collective-permute-start(bf16[224,384]{1,0:T(8,128)(2,1)S(1)} %get-tuple-element.170), channel_id=1, source_target_pairs={{0,16},{1,17},{2,18},{3,19},{4,20},{5,21},{6,22},{7,23},{8,24},{9,... | collective-permute-start | bytes 516104 | tf_op jit(solution)/shard_map/ppermute | solution.py:590
  113.8 14.4 %collective-permute-start.41 = (bf16[224,384]{1,0:T(8,128)(2,1)S(1)}, bf16[224,384]{1,0:T(8,128)(2,1)S(1)}, u32[]{:S(2)}, u32[]{:S(2)}) collective-permute-start(bf16[224,384]{1,0:T(8,128)(2,1)S(1)} %get-tuple-element.171), channel_id=1, source_target_pairs={{0,24},{1,25},{2,26},{3,27},{4,28},{5,29},{6,30},{7,31},{8,16},{9,... | collective-permute-start | bytes 516104 | tf_op jit(solution)/shard_map/ppermute | solution.py:590
  136.1 14.4 %collective-permute-start.45 = (bf16[416,384]{1,0:T(8,128)(2,1)S(1)}, bf16[416,384]{1,0:T(8,128)(2,1)S(1)}, u32[]{:S(2)}, u32[]{:S(2)}) collective-permute-start(bf16[416,384]{1,0:T(8,128)(2,1)S(1)} %join.6.refs_0_), channel_id=1, source_target_pairs={{0,2},{1,5},{2,0},{3,7},{4,6},{5,1},{6,4},{7,3},{8,10},{9,13},{10,... | collective-permute-start | bytes 958472 | tf_op jit(solution)/shard_map/ppermute | solution.py:590
  137.2 13.4 %collective-permute-start.46 = (bf16[416,384]{1,0:T(8,128)(2,1)S(1)}, bf16[416,384]{1,0:T(8,128)(2,1)S(1)}, u32[]{:S(2)}, u32[]{:S(2)}) collective-permute-start(bf16[416,384]{1,0:T(8,128)(2,1)S(1)} %join.6.refs_0_), channel_id=1, source_target_pairs={{0,4},{1,3},{2,6},{3,1},{4,0},{5,7},{6,2},{7,5},{8,12},{9,11},{10,... | collective-permute-start | bytes 958472 | tf_op jit(solution)/shard_map/ppermute | solution.py:590
  138.2 12.4 %collective-permute-start.43 = (bf16[192,384]{1,0:T(8,128)(2,1)S(1)}, bf16[192,384]{1,0:T(8,128)(2,1)S(1)}, u32[]{:S(2)}, u32[]{:S(2)}) collective-permute-start(bf16[192,384]{1,0:T(8,128)(2,1)S(1)} %get-tuple-element.172.refs_0_), channel_id=1, source_target_pairs={{0,16},{1,17},{2,18},{3,19},{4,20},{5,21},{6,22},{7,23},{8,24},{9,... | collective-permute-start | bytes 442376 | tf_op jit(solution)/shard_map/ppermute | solution.py:590
  141.3 9.3 %collective-permute-start.44 = (bf16[192,384]{1,0:T(8,128)(2,1)S(1)}, bf16[192,384]{1,0:T(8,128)(2,1)S(1)}, u32[]{:S(2)}, u32[]{:S(2)}) collective-permute-start(bf16[192,384]{1,0:T(8,128)(2,1)S(1)} %get-tuple-element.172.refs_0_), channel_id=1, source_target_pairs={{0,24},{1,25},{2,26},{3,27},{4,28},{5,29},{6,30},{7,31},{8,16},{9,... | collective-permute-start | bytes 442376 | tf_op jit(solution)/shard_map/ppermute | solution.py:590
  151.1 9.6 %collective-permute-start.49 = (bf16[384,384]{1,0:T(8,128)(2,1)S(1)}, bf16[384,384]{1,0:T(8,128)(2,1)S(1)}, u32[]{:S(2)}, u32[]{:S(2)}) collective-permute-start(bf16[384,384]{1,0:T(8,128)(2,1)S(1)} %join.7.refs_4_), channel_id=1, source_target_pairs={{0,4},{1,3},{2,6},{3,1},{4,0},{5,7},{6,2},{7,5},{8,12},{9,11},{10,... | collective-permute-start | bytes 884744 | tf_op jit(solution)/shard_map/ppermute | solution.py:590
  152.1 12.0 %collective-permute-start.47 = (bf16[416,384]{1,0:T(8,128)(2,1)S(1)}, bf16[416,384]{1,0:T(8,128)(2,1)S(1)}, u32[]{:S(2)}, u32[]{:S(2)}) collective-permute-start(bf16[416,384]{1,0:T(8,128)(2,1)S(1)} %collective-permute-done.45.refs_1_), channel_id=1, source_target_pairs={{0,4},{1,3},{2,6},{3,1},{4,0},{5,7},{6,2},{7,5},{8,12},{9,11},{10,... | collective-permute-start | bytes 958472 | tf_op jit(solution)/shard_map/ppermute | solution.py:590
  153.2 8.7 %collective-permute-start.48 = (bf16[384,384]{1,0:T(8,128)(2,1)S(1)}, bf16[384,384]{1,0:T(8,128)(2,1)S(1)}, u32[]{:S(2)}, u32[]{:S(2)}) collective-permute-start(bf16[384,384]{1,0:T(8,128)(2,1)S(1)} %join.7.refs_4_), channel_id=1, source_target_pairs={{0,2},{1,5},{2,0},{3,7},{4,6},{5,1},{6,4},{7,3},{8,10},{9,13},{10,... | collective-permute-start | bytes 884744 | tf_op jit(solution)/shard_map/ppermute | solution.py:590
  (40 other events, 347.8 us)

commit v3 on v2

--- a/solution.py
+++ b/solution.py
@@ -224,15 +224,17 @@
         start += ref.shape[0]
 
 
+def in_order(own, other, even):
+    return jnp.concatenate([jnp.where(even, own, other), jnp.where(even, other, own)], axis=1)
+
+
 def expert_body(rows, ids, *refs):
     own, other = refs[:4], refs[4:8]
     w_in, w_out, act, slope, part_mine, part_other = refs[8:]
     t = ids[2]
-    in_mine, in_other = row_halves(w_in[0], t)
-    out_mine, out_other = halves(w_out[0], t)
     for p in range(4):
         span = pl.ds(p * rows, rows)
-        pre = nn(own[p][...], in_mine) + nn(other[p][...], in_other)
+        pre = nn(in_order(own[p][...], other[p][...], t == 0), w_in[0])
         square = pre * pre
         bent = jnp.tanh(gelu_scale * (pre + 0.044715 * pre * square))
         half = 0.5 * (1.0 + bent)
@@ -241,49 +243,39 @@
         slope[span, :] = half + 0.5 * pre * (1.0 - bent * bent) * (
             gelu_scale * (1.0 + 3 * 0.044715 * square)
         )
-        part_mine[span, :] = nn(value, out_mine).astype(bf16)
-        part_other[span, :] = nn(value, out_other).astype(bf16)
+        mine, rest = halves(nn(value, w_out[0]).astype(bf16), t)
+        part_mine[span, :] = mine
+        part_other[span, :] = rest
 
 
 def expert_back_body(rows, experts, ids, *refs):
     own, other, cot_own, cot_other = refs[:4], refs[4:8], refs[8:12], refs[12:16]
-    w_in, w_out, router, slope, grad_pre, grad_mine, grad_other, back_mine, back_other = refs[16:]
+    w_in, w_out, router, slope, grad_pre, grads, back_mine, back_other = refs[16:]
     e, t = ids[0], ids[2]
-    in_mine, in_other = row_halves(w_in[0], t)
-    out_mine, out_other = halves(w_out[0], t)
-    router_mine, router_other = halves(router[...], t)
     for p in range(4):
         span = pl.ds(p * rows, rows)
-        logits = nt(own[p][...], router_mine) + nt(other[p][...], router_other)
+        cot_rows = pl.ds(0, rows)
+        logits = nt(in_order(own[p][...], other[p][...], t == 0), router[...])
         raised = jnp.exp(logits - jnp.max(logits, axis=-1, keepdims=True))
         chosen = jnp.where(iota(raised.shape, 1) == e, raised, 0.0)
         gate = jnp.sum(chosen, axis=-1, keepdims=True) / jnp.sum(raised, axis=-1, keepdims=True)
-        first = (gate * cot_own[p][pl.ds(0, rows), :].astype(f32)).astype(bf16)
-        second = (gate * cot_other[p][pl.ds(0, rows), :].astype(f32)).astype(bf16)
-        grad_mine[span, :] = first
-        grad_other[span, :] = second
-        grad_act = nt(first, out_mine) + nt(second, out_other)
-        value = (grad_act * slope[span, :]).astype(bf16)
+        cot = in_order(cot_own[p][cot_rows, :], cot_other[p][cot_rows, :], t == 0)
+        grad = (gate * cot.astype(f32)).astype(bf16)
+        grads[span, :] = grad
+        value = (nt(grad, w_out[0]) * slope[span, :]).astype(bf16)
         grad_pre[span, :] = value
-        back_mine[span, :] = nt(value, in_mine).astype(bf16)
-        back_other[span, :] = nt(value, in_other).astype(bf16)
+        mine, rest = halves(nt(value, w_in[0]).astype(bf16), t)
+        back_mine[span, :] = mine
+        back_other[span, :] = rest
 
 
 def expert_grads_body(rows, ids, *refs):
     own, other = refs[:4], refs[4:8]
-    act, grad_pre, grad_mine, grad_other, out_in, out_out = refs[8:]
+    act, grad_pre, grads, out_in, out_out = refs[8:]
     even = ids[2] == 0
-    low = jnp.where(even, grad_mine[...], grad_other[...])
-    high = jnp.where(even, grad_other[...], grad_mine[...])
-    width = low.shape[1]
-    left = act[...]
-    out_out[0, :, :width] = tn(left, low)
-    out_out[0, :, width:] = tn(left, high)
-    first = jnp.concatenate([jnp.where(even, own[p][...], other[p][...]) for p in range(4)], axis=0)
-    second = jnp.concatenate([jnp.where(even, other[p][...], own[p][...]) for p in range(4)], axis=0)
-    right = grad_pre[...]
-    out_in[0, :width, :] = tn(first, right)
-    out_in[0, width:, :] = tn(second, right)
+    out_out[0] = tn(act[...], grads[...])
+    sent = jnp.concatenate([in_order(own[p][...], other[p][...], even) for p in range(4)], axis=0)
+    out_in[0] = tn(sent, grad_pre[...])
 
 
 def pair_sum_body(ids, mine, received, keep, send):
@@ -507,29 +499,29 @@
 def final_body(groups, experts, rows, ids, *refs):
     pieces, hot, outs = refs[:8], refs[8], refs[9:13]
     gain_attn, bias, gain_ffn, router = refs[13:17]
-    stack, square, small = refs[17:]
+    square, small = refs[17:]
     e, q, t = ids[0], ids[1], ids[2]
-    depth = stack.shape[2]
-    per = groups // 2
+    depth = square.shape[0] // groups
+    per = groups - 1
 
     def place_of(chip):
         away = q ^ chip
         return jnp.where((t == 1) & ((away == 1) | (away == 2)), 3 - away, away)
 
     for p in range(4):
-        for s in range(groups):
-            piece = pieces[s // per * 4 + p]
-            stack[p, s] = piece[pl.ds(s % per * depth, depth), :].astype(f32)
         small[p] = decode(pieces[p], per * depth, rows)
     for m in range(4):
+        out = outs[m] if m < 3 else square
         place = place_of(m)
-        for k in range(groups):
-            block = stack[place, k ^ e]
-            span = pl.ds(k * depth, depth)
-            if m < 3:
-                outs[m][span, :] = block
-            else:
-                square[span, :] = block
+        for p in range(4):
+
+            @pl.when(place == p)
+            def _(p=p, out=out):
+                for s in range(groups):
+                    start = pl.multiple_of((s ^ e) * depth, 8)
+                    piece = pieces[s // per * 4 + p]
+                    out[pl.ds(start, depth), :] = piece[pl.ds(s % per * depth, depth), :].astype(f32)
+
     outs[3][...] = square[...].T
     total = widen(small[place_of(0)] + small[place_of(1)] + small[place_of(2)] + small[place_of(3)])
     gain_attn[...] = total[0]
@@ -715,11 +707,11 @@
         plane_sum_body, "plane_sum", ids, [one_wide, one], keep, send(go, to_first)
     )
     part_last = send(go, to_second)
-    grad_pre, grad_mine, grad_other, back_mine, back_other = call(
+    grad_pre, expert_cot, back_mine, back_other = call(
         functools.partial(expert_back_body, slot_count, experts),
         "expert_back",
         ids,
-        [((all_rows, units), bf16), rows_half, rows_half, rows_half, rows_half],
+        [((all_rows, units), bf16), ((all_rows, width), bf16), rows_half, rows_half],
         *row_own,
         *row_other,
         *cot_own,
@@ -744,8 +736,7 @@
         *row_other,
         act,
         grad_pre,
-        grad_mine,
-        grad_other,
+        expert_cot,
         limit=40,
     )
     part_last, back_last, grad_in, grad_out = lax.optimization_barrier(
@@ -826,7 +817,7 @@
         small_ffn,
         bias,
     )
-    right_all[1], small = lax.optimization_barrier((right_all[1], small))
+    *right_all, small = lax.optimization_barrier((*right_all, small))
     right_pair = [send(right_all[p], to_pair) for p in (0, 2, 1, 3)]
     depth = width // groups
     blocks = call(
@@ -850,14 +841,14 @@
         scratch=[pltpu.VMEM((groups, 2 * small_rows, local), f32)],
     )
     spread = exchange([reduced] * groups)
-    near, rest = spread[: groups // 2], spread[groups // 2 :]
+    near, rest = spread[:-1], spread[-1:]
     matrix = join(near + [code])
     first, second = send(matrix, to_first), send(matrix, to_second)
     *rest, first, second = lax.optimization_barrier((*rest, first, second))
     far = send(first, to_second)
-    matrix_two = join(list(rest))
+    matrix_two = rest[0]
     first_two, second_two = send(matrix_two, to_first), send(matrix_two, to_second)
-    far_two = send(second_two, to_first)
+    far_two = send(matrix_two, to_far)
     grads = call(
         functools.partial(final_body, groups, experts, small_rows),
         "final",
@@ -875,7 +866,6 @@
         far_two,
         hot,
         scratch=[
-            pltpu.VMEM((4, groups, depth, local), f32),
             pltpu.VMEM((width, local), f32),
             pltpu.VMEM((4, 2 * small_rows, local), f32),
         ],

time: 171 us -> 169 us (0.988)
  Pallas kernels: 39.7 us -> 37.9 us
    pallas_call x22 -> x21, Pallas kernels: 39.7 us -> 37.9 us  [call(): pl.pallas_call(body, out_shape=shapes, in_specs=[pl.BlockSpec(memory_spac...]
  transfers between devices with their start and end apart: 51 -> 51, of which waited for: 26 -> 32; matrix products, arithmetic and copies ran while one was open for 0% -> 0% of each run, Pallas kernels for 14% -> 14%
where the time goes in v3:
time: 169 us
  waiting for transfers between devices  78.7 us (47%)
  starting transfers between devices  51.2 us (30%)
  Pallas kernels  37.9 us (22%)
    ppermute x51, waiting for transfers between devices, send(): return lax.ppermute(array, ('dp', 'tensor'), pairs)  78.7 us
    ppermute x51, starting transfers between devices, send(): return lax.ppermute(array, ('dp', 'tensor'), pairs)  51.2 us
    pallas_call x21, Pallas kernels, call(): pl.pallas_call(body, out_shape=shapes, in_specs=[pl.BlockSpec(memory_spac...  37.9 us
  transfers between devices with their start and end apart: 51, of which 32 were waited for; matrix products, arithmetic and copies ran while one was open for 0% of the time, Pallas kernels for 14%

profile of v3, /device:TPU:0, one launch (start us, length us, event | category | flops | bytes accessed | tf_op | source)
XLA Modules:
  0.0 168.9 jit_solution(5668580479765661693)
XLA Ops:
  2.5 3.1 %collective-permute-start = (bf16[80,384]{1,0:T(8,128)(2,1)S(1)}, bf16[80,384]{1,0:T(8,128)(2,1)S(1)}, u32[]{:S(2)}, u32[]{:S(2)}) collective-permute-start(bf16[80,384]{1,0:T(8,128)(2,1)S(1)} %get-tuple-element.103), channel_id=1, source_target_pairs={{0,8},{1,9},{2,10},{3,11},{4,12},{5,13},{6,14},{7,15},{8,0},{9,1},... | collective-permute-start | bytes 184328 | tf_op jit(solution)/shard_map/ppermute | solution.py:582
  5.6 2.6 %collective-permute-start.1 = (bf16[80,384]{1,0:T(8,128)(2,1)S(1)}, bf16[80,384]{1,0:T(8,128)(2,1)S(1)}, u32[]{:S(2)}, u32[]{:S(2)}) collective-permute-start(bf16[80,384]{1,0:T(8,128)(2,1)S(1)} %get-tuple-element.104), channel_id=1, source_target_pairs={{0,16},{1,17},{2,18},{3,19},{4,20},{5,21},{6,22},{7,23},{8,24},{9,... | collective-permute-start | bytes 184328 | tf_op jit(solution)/shard_map/ppermute | solution.py:582
  8.2 4.8 %front.1 = (bf16[256,384]{1,0:T(8,128)(2,1)S(1)}, f32[128,768]{1,0:T(8,128)S(1)}, bf16[128,384]{1,0:T(8,128)(2,1)S(1)}, bf16[128,384]{1,0:T(8,128)(2,1)S(1)}, bf...) custom-call(s32[3]{0:T(128)S(1)} %pad_add_fusion.ids, bf16[128,768]{1,0:T(8,128)(2,1)} %tokens.3, f32[768]{0:T(1024)} %gain.5, ...), custom_call_target="tpu_custom_call" | custom-call | bytes 18000000 | tf_op jit(solution)/shard_map/front/pallas_call | solution.py:53
  19.1 3.3 %collective-permute-start.5 = (bf16[80,384]{1,0:T(8,128)(2,1)S(1)}, bf16[80,384]{1,0:T(8,128)(2,1)S(1)}, u32[]{:S(2)}, u32[]{:S(2)}) collective-permute-start(bf16[80,384]{1,0:T(8,128)(2,1)S(1)} %get-tuple-element.110), channel_id=1, source_target_pairs={{0,16},{1,17},{2,18},{3,19},{4,20},{5,21},{6,22},{7,23},{8,24},{9,... | collective-permute-start | bytes 184328 | tf_op jit(solution)/shard_map/ppermute | solution.py:582
  23.5 3.7 %collective-permute-done.7.refs_9_.refs_1_ = bf16[576,384]{1,0:T(8,128)(2,1)S(1)} collective-permute-done((bf16[576,384]{1,0:T(8,128)(2,1)S(1)}, bf16[576,384]{1,0:T(8,128)(2,1)S(1)}, u32[]{:S(2)}, u32[]{:S(2)}) %collective-permute-start.7) | collective-permute-done | bytes 442400 | tf_op jit(solution)/shard_map/ppermute | solution.py:582
  31.6 6.2 %collective-permute-done.9.refs_1_ = bf16[320,384]{1,0:T(8,128)(2,1)S(1)} collective-permute-done((bf16[320,384]{1,0:T(8,128)(2,1)S(1)}, bf16[320,384]{1,0:T(8,128)(2,1)S(1)}, u32[]{:S(2)}, u32[]{:S(2)}) %collective-permute-start.9) | collective-permute-done | bytes 245792 | tf_op jit(solution)/shard_map/ppermute | solution.py:582
  46.9 3.4 %expert.1 = (bf16[1280,384]{1,0:T(8,128)(2,1)S(1)}, f32[1280,384]{1,0:T(8,128)S(1)}, bf16[1280,384]{1,0:T(8,128)(2,1)S(1)}, bf16[1280,384]{1,0:T(8,128)(2,1)S(1)}) custom-call(s32[3]{0:T(128)S(1)} %pad_add_fusion.ids, bf16[320,384]{1,0:T(8,128)(2,1)S(1)} %join.4.refs_0_, bf16[320,384]{1,0:T(8,128)(2,1)S(1)} %collective-permute-done.9.refs_1_, ...), custom_call_target="tpu_custom_call" | custom-call | bytes 15840000 | tf_op jit(solution)/shard_map/expert/pallas_call | solution.py:53
  50.8 5.6 %expert_back.1 = (bf16[1280,384]{1,0:T(8,128)(2,1)S(1)}, bf16[1280,768]{1,0:T(8,128)(2,1)S(1)}, bf16[1280,384]{1,0:T(8,128)(2,1)S(1)}, bf16[1280,384]{1,0:T(8,128)(2,1)S(1)}) custom-call(s32[3]{0:T(128)S(1)} %pad_add_fusion.ids, bf16[320,384]{1,0:T(8,128)(2,1)S(1)} %join.4.refs_0_, bf16[320,384]{1,0:T(8,128)(2,1)S(1)} %collective-permute-done.9.refs_1_, ...), custom_call_target="tpu_custom_call" | custom-call | bytes 19440000 | tf_op jit(solution)/shard_map/expert_back/pallas_call | solution.py:53
  61.0 5.3 %collective-permute-done.17.received = bf16[640,384]{1,0:T(8,128)(2,1)S(1)} collective-permute-done((bf16[640,384]{1,0:T(8,128)(2,1)S(1)}, bf16[640,384]{1,0:T(8,128)(2,1)S(1)}, u32[]{:S(2)}, u32[]{:S(2)}) %collective-permute-start.17) | collective-permute-done | bytes 491552 | tf_op jit(solution)/shard_map/ppermute | solution.py:582
  68.0 5.9 %collective-permute-done.25.received = bf16[640,384]{1,0:T(8,128)(2,1)S(1)} collective-permute-done((bf16[640,384]{1,0:T(8,128)(2,1)S(1)}, bf16[640,384]{1,0:T(8,128)(2,1)S(1)}, u32[]{:S(2)}, u32[]{:S(2)}) %collective-permute-start.25) | collective-permute-done | bytes 491552 | tf_op jit(solution)/shard_map/ppermute | solution.py:582
  75.5 3.8 %expert_grads.1 = (f32[1,768,384]{2,1,0:T(8,128)}, f32[1,384,768]{2,1,0:T(8,128)}) custom-call(s32[3]{0:T(128)S(1)} %pad_add_fusion.ids, bf16[320,384]{1,0:T(8,128)(2,1)S(1)} %join.4.refs_0_, bf16[320,384]{1,0:T(8,128)(2,1)S(1)} %collective-permute-done.9.refs_1_, bf16[320,384]{1,0:T(8,128)(2,1)S(1)} %collective-permute-done.10.refs_2_, ...), custom_call_target="tpu_custom_call" | custom-call | bytes 14400000 | tf_op jit(solution)/shard_map/expert_grads/pallas_call | solution.py:53
  81.5 2.8 %collective-permute-start.28 = (bf16[160,384]{1,0:T(8,128)(2,1)S(1)}, bf16[160,384]{1,0:T(8,128)(2,1)S(1)}, u32[]{:S(2)}, u32[]{:S(2)}) collective-permute-start(bf16[160,384]{1,0:T(8,128)(2,1)S(1)} %get-tuple-element.145), channel_id=1, source_target_pairs={{0,16},{1,17},{2,18},{3,19},{4,20},{5,21},{6,22},{7,23},{8,24},{9,... | collective-permute-start | bytes 368648 | tf_op jit(solution)/shard_map/ppermute | solution.py:582
  96.2 2.4 %attend_back.1 = (bf16[128,384]{1,0:T(8,128)(2,1)S(1)}, bf16[128,384]{1,0:T(8,128)(2,1)S(1)}, bf16[128,384]{1,0:T(8,128)(2,1)S(1)}, bf16[128,384]{1,0:T(8,128)(2...) custom-call(s32[3]{0:T(128)S(1)} %pad_add_fusion.ids, bf16[128,768]{1,0:T(8,128)(2,1)S(1)} %get-tuple-element.151.att, ...), custom_call_target="tpu_custom_call" | custom-call | bytes 9000000 | tf_op jit(solution)/shard_map/attend_back/pallas_call | solution.py:53
  105.0 2.2 %collective-permute-done.34.refs_11_ = bf16[128,384]{1,0:T(8,128)(2,1)S(1)} collective-permute-done((bf16[128,384]{1,0:T(8,128)(2,1)S(1)}, bf16[128,384]{1,0:T(8,128)(2,1)S(1)}, u32[]{:S(2)}, u32[]{:S(2)}) %collective-permute-start.34) | collective-permute-done | bytes 98336 | tf_op jit(solution)/shard_map/ppermute | solution.py:582
  114.9 5.4 %collective-permute-done.39.refs_1_ = bf16[224,384]{1,0:T(8,128)(2,1)S(1)} collective-permute-done((bf16[224,384]{1,0:T(8,128)(2,1)S(1)}, bf16[224,384]{1,0:T(8,128)(2,1)S(1)}, u32[]{:S(2)}, u32[]{:S(2)}) %collective-permute-start.39) | collective-permute-done | bytes 172064 | tf_op jit(solution)/shard_map/ppermute | solution.py:582
  120.3 7.1 %collective-permute-done.40.refs_2_ = bf16[224,384]{1,0:T(8,128)(2,1)S(1)} collective-permute-done((bf16[224,384]{1,0:T(8,128)(2,1)S(1)}, bf16[224,384]{1,0:T(8,128)(2,1)S(1)}, u32[]{:S(2)}, u32[]{:S(2)}) %collective-permute-start.40) | collective-permute-done | bytes 172064 | tf_op jit(solution)/shard_map/ppermute | solution.py:582
  128.1 3.4 %collective-permute-start.42 = (bf16[192,384]{1,0:T(8,128)(2,1)S(1)}, bf16[192,384]{1,0:T(8,128)(2,1)S(1)}, u32[]{:S(2)}, u32[]{:S(2)}) collective-permute-start(bf16[192,384]{1,0:T(8,128)(2,1)S(1)} %get-tuple-element.175.refs_0_), channel_id=1, source_target_pairs={{0,8},{1,9},{2,10},{3,11},{4,12},{5,13},{6,14},{7,15},{8,0},{9,1},... | collective-permute-start | bytes 442376 | tf_op jit(solution)/shard_map/ppermute | solution.py:582
  132.5 4.0 %collective-permute-done.42.refs_1_ = bf16[192,384]{1,0:T(8,128)(2,1)S(1)} collective-permute-done((bf16[192,384]{1,0:T(8,128)(2,1)S(1)}, bf16[192,384]{1,0:T(8,128)(2,1)S(1)}, u32[]{:S(2)}, u32[]{:S(2)}) %collective-permute-start.42) | collective-permute-done | bytes 147488 | tf_op jit(solution)/shard_map/ppermute | solution.py:582
  136.5 3.8 %collective-permute-done.43.refs_2_ = bf16[192,384]{1,0:T(8,128)(2,1)S(1)} collective-permute-done((bf16[192,384]{1,0:T(8,128)(2,1)S(1)}, bf16[192,384]{1,0:T(8,128)(2,1)S(1)}, u32[]{:S(2)}, u32[]{:S(2)}) %collective-permute-start.43) | collective-permute-done | bytes 147488 | tf_op jit(solution)/shard_map/ppermute | solution.py:582
  143.3 2.4 %collective-permute-start.44 = (bf16[192,384]{1,0:T(8,128)(2,1)S(1)}, bf16[192,384]{1,0:T(8,128)(2,1)S(1)}, u32[]{:S(2)}, u32[]{:S(2)}) collective-permute-start(bf16[192,384]{1,0:T(8,128)(2,1)S(1)} %get-tuple-element.175.refs_0_), channel_id=1, source_target_pairs={{0,24},{1,25},{2,26},{3,27},{4,28},{5,29},{6,30},{7,31},{8,16},{9,... | collective-permute-start | bytes 442376 | tf_op jit(solution)/shard_map/ppermute | solution.py:582
  145.7 4.5 %collective-permute-done.44.refs_4_ = bf16[192,384]{1,0:T(8,128)(2,1)S(1)} collective-permute-done((bf16[192,384]{1,0:T(8,128)(2,1)S(1)}, bf16[192,384]{1,0:T(8,128)(2,1)S(1)}, u32[]{:S(2)}, u32[]{:S(2)}) %collective-permute-start.44) | collective-permute-done | bytes 147488 | tf_op jit(solution)/shard_map/ppermute | solution.py:582
  156.8 3.2 %collective-permute-done.48.refs_5_ = bf16[192,384]{1,0:T(8,128)(2,1)S(1)} collective-permute-done((bf16[192,384]{1,0:T(8,128)(2,1)S(1)}, bf16[192,384]{1,0:T(8,128)(2,1)S(1)}, u32[]{:S(2)}, u32[]{:S(2)}) %collective-permute-start.48) | collective-permute-done | bytes 147488 | tf_op jit(solution)/shard_map/ppermute | solution.py:582
  160.0 5.7 %collective-permute-done.49.refs_6_ = bf16[192,384]{1,0:T(8,128)(2,1)S(1)} collective-permute-done((bf16[192,384]{1,0:T(8,128)(2,1)S(1)}, bf16[192,384]{1,0:T(8,128)(2,1)S(1)}, u32[]{:S(2)}, u32[]{:S(2)}) %collective-permute-start.49) | collective-permute-done | bytes 147488 | tf_op jit(solution)/shard_map/ppermute | solution.py:582
  165.7 3.2 %final.1 = (f32[768,384]{1,0:T(8,128)}, f32[768,384]{1,0:T(8,128)}, f32[768,384]{1,0:T(8,128)}, f32[384,768]{1,0:T(8,128)}, f32[768]{0:T(1024)}, /*index=5*/f32[6,32]{1,0:T(8,128)}, f32[768]{0:T(1024)}, f32[4,768]{1,0:T(4,128)}) custom-call(s32[3]{0:T(128)S(1)} %pad_add_fusion.ids, bf16[608,384]{1,0:T(8,128)(2,1)S(1)} %join.5.refs_0_, ...), custom_call_target="tpu_custom_call" | custom-call | bytes 14040000 | tf_op jit(solution)/shard_map/final/pallas_call | solution.py:53
  (126 shorter events, 70.1 us)
Async XLA Ops:
  2.5 10.5 %collective-permute-start = (bf16[80,384]{1,0:T(8,128)(2,1)S(1)}, bf16[80,384]{1,0:T(8,128)(2,1)S(1)}, u32[]{:S(2)}, u32[]{:S(2)}) collective-permute-start(bf16[80,384]{1,0:T(8,128)(2,1)S(1)} %get-tuple-element.103), channel_id=1, source_target_pairs={{0,8},{1,9},{2,10},{3,11},{4,12},{5,13},{6,14},{7,15},{8,0},{9,1},... | collective-permute-start | bytes 184328 | tf_op jit(solution)/shard_map/ppermute | solution.py:582
  14.8 12.4 %collective-permute-start.7 = (bf16[576,384]{1,0:T(8,128)(2,1)S(1)}, bf16[576,384]{1,0:T(8,128)(2,1)S(1)}, u32[]{:S(2)}, u32[]{:S(2)}) collective-permute-start(bf16[576,384]{1,0:T(8,128)(2,1)S(1)} %join.3.refs_8_.refs_0_), channel_id=1, source_target_pairs={{0,2},{1,5},{2,0},{3,7},{4,6},{5,1},{6,4},{7,3},{8,10},{9,13},{10,... | collective-permute-start | bytes 1327112 | tf_op jit(solution)/shard_map/ppermute | solution.py:582
  16.4 11.1 %collective-permute-start.8 = (bf16[576,384]{1,0:T(8,128)(2,1)S(1)}, bf16[576,384]{1,0:T(8,128)(2,1)S(1)}, u32[]{:S(2)}, u32[]{:S(2)}) collective-permute-start(bf16[576,384]{1,0:T(8,128)(2,1)S(1)} %join.3.refs_8_.refs_0_), channel_id=1, source_target_pairs={{0,4},{1,3},{2,6},{3,1},{4,0},{5,7},{6,2},{7,5},{8,12},{9,11},{10,... | collective-permute-start | bytes 1327112 | tf_op jit(solution)/shard_map/ppermute | solution.py:582
  19.0 8.4 %collective-permute-start.4 = (bf16[80,384]{1,0:T(8,128)(2,1)S(1)}, bf16[80,384]{1,0:T(8,128)(2,1)S(1)}, u32[]{:S(2)}, u32[]{:S(2)}) collective-permute-start(bf16[80,384]{1,0:T(8,128)(2,1)S(1)} %get-tuple-element.109), channel_id=1, source_target_pairs={{0,8},{1,9},{2,10},{3,11},{4,12},{5,13},{6,14},{7,15},{8,0},{9,1},... | collective-permute-start | bytes 184328 | tf_op jit(solution)/shard_map/ppermute | solution.py:582
  19.1 8.3 %collective-permute-start.5 = (bf16[80,384]{1,0:T(8,128)(2,1)S(1)}, bf16[80,384]{1,0:T(8,128)(2,1)S(1)}, u32[]{:S(2)}, u32[]{:S(2)}) collective-permute-start(bf16[80,384]{1,0:T(8,128)(2,1)S(1)} %get-tuple-element.110), channel_id=1, source_target_pairs={{0,16},{1,17},{2,18},{3,19},{4,20},{5,21},{6,22},{7,23},{8,24},{9,... | collective-permute-start | bytes 184328 | tf_op jit(solution)/shard_map/ppermute | solution.py:582
  29.0 8.8 %collective-permute-start.9 = (bf16[320,384]{1,0:T(8,128)(2,1)S(1)}, bf16[320,384]{1,0:T(8,128)(2,1)S(1)}, u32[]{:S(2)}, u32[]{:S(2)}) collective-permute-start(bf16[320,384]{1,0:T(8,128)(2,1)S(1)} %join.4.refs_0_), channel_id=1, source_target_pairs={{0,2},{1,5},{2,0},{3,7},{4,6},{5,1},{6,4},{7,3},{8,10},{9,13},{10,... | collective-permute-start | bytes 737288 | tf_op jit(solution)/shard_map/ppermute | solution.py:582
  29.6 9.0 %collective-permute-start.10 = (bf16[320,384]{1,0:T(8,128)(2,1)S(1)}, bf16[320,384]{1,0:T(8,128)(2,1)S(1)}, u32[]{:S(2)}, u32[]{:S(2)}) collective-permute-start(bf16[320,384]{1,0:T(8,128)(2,1)S(1)} %join.4.refs_0_), channel_id=1, source_target_pairs={{0,4},{1,3},{2,6},{3,1},{4,0},{5,7},{6,2},{7,5},{8,12},{9,11},{10,... | collective-permute-start | bytes 737288 | tf_op jit(solution)/shard_map/ppermute | solution.py:582
  31.3 9.9 %collective-permute-start.19 = (bf16[576,384]{1,0:T(8,128)(2,1)S(1)}, bf16[576,384]{1,0:T(8,128)(2,1)S(1)}, u32[]{:S(2)}, u32[]{:S(2)}) collective-permute-start(bf16[576,384]{1,0:T(8,128)(2,1)S(1)} %collective-permute-done.7.refs_9_.refs_1_), channel_id=1, source_target_pairs={{0,4},{1,3},{2,6},{3,1},{4,0},{5,7},{6,2},{7,5},{8,12},{9,11},{10,... | collective-permute-start | bytes 1327112 | tf_op jit(solution)/shard_map/ppermute | solution.py:582
  39.1 11.6 %collective-permute-start.20 = (bf16[576,384]{1,0:T(8,128)(2,1)S(1)}, bf16[576,384]{1,0:T(8,128)(2,1)S(1)}, u32[]{:S(2)}, u32[]{:S(2)}) collective-permute-start(bf16[576,384]{1,0:T(8,128)(2,1)S(1)} %join.3.refs_8_.refs_0_), channel_id=1, source_target_pairs={{0,1},{1,0},{2,3},{3,2},{4,5},{5,4},{6,7},{7,6},{8,9},{9,8},{10,11... | collective-permute-start | bytes 1327112 | tf_op jit(solution)/shard_map/ppermute | solution.py:582
  41.3 9.5 %collective-permute-start.22 = (bf16[576,384]{1,0:T(8,128)(2,1)S(1)}, bf16[576,384]{1,0:T(8,128)(2,1)S(1)}, u32[]{:S(2)}, u32[]{:S(2)}) collective-permute-start(bf16[576,384]{1,0:T(8,128)(2,1)S(1)} %collective-permute-done.7.refs_9_.refs_1_), channel_id=1, source_target_pairs={{0,1},{1,0},{2,3},{3,2},{4,5},{5,4},{6,7},{7,6},{8,9},{9,8},{10,11... | collective-permute-start | bytes 1327112 | tf_op jit(solution)/shard_map/ppermute | solution.py:582
  57.3 8.9 %collective-permute-start.17 = (bf16[640,384]{1,0:T(8,128)(2,1)S(1)}, bf16[640,384]{1,0:T(8,128)(2,1)S(1)}, u32[]{:S(2)}, u32[]{:S(2)}) collective-permute-start(bf16[640,384]{1,0:T(8,128)(2,1)S(1)} %get-tuple-element.124), channel_id=1, source_target_pairs={{0,2},{1,5},{2,0},{3,7},{4,6},{5,1},{6,4},{7,3},{8,10},{9,13},{10,... | collective-permute-start | bytes 1474568 | tf_op jit(solution)/shard_map/ppermute | solution.py:582
  59.8 14.1 %collective-permute-start.25 = (bf16[640,384]{1,0:T(8,128)(2,1)S(1)}, bf16[640,384]{1,0:T(8,128)(2,1)S(1)}, u32[]{:S(2)}, u32[]{:S(2)}) collective-permute-start(bf16[640,384]{1,0:T(8,128)(2,1)S(1)} %get-tuple-element.133), channel_id=1, source_target_pairs={{0,2},{1,5},{2,0},{3,7},{4,6},{5,1},{6,4},{7,3},{8,10},{9,13},{10,... | collective-permute-start | bytes 1474568 | tf_op jit(solution)/shard_map/ppermute | solution.py:582
  66.9 12.4 %collective-permute-start.18 = (bf16[320,384]{1,0:T(8,128)(2,1)S(1)}, bf16[320,384]{1,0:T(8,128)(2,1)S(1)}, u32[]{:S(2)}, u32[]{:S(2)}) collective-permute-start(bf16[320,384]{1,0:T(8,128)(2,1)S(1)} %get-tuple-element.126), channel_id=1, source_target_pairs={{0,4},{1,3},{2,6},{3,1},{4,0},{5,7},{6,2},{7,5},{8,12},{9,11},{10,... | collective-permute-start | bytes 737288 | tf_op jit(solution)/shard_map/ppermute | solution.py:582
  81.5 7.9 %collective-permute-start.28 = (bf16[160,384]{1,0:T(8,128)(2,1)S(1)}, bf16[160,384]{1,0:T(8,128)(2,1)S(1)}, u32[]{:S(2)}, u32[]{:S(2)}) collective-permute-start(bf16[160,384]{1,0:T(8,128)(2,1)S(1)} %get-tuple-element.145), channel_id=1, source_target_pairs={{0,16},{1,17},{2,18},{3,19},{4,20},{5,21},{6,22},{7,23},{8,24},{9,... | collective-permute-start | bytes 368648 | tf_op jit(solution)/shard_map/ppermute | solution.py:582
  110.5 9.8 %collective-permute-start.39 = (bf16[224,384]{1,0:T(8,128)(2,1)S(1)}, bf16[224,384]{1,0:T(8,128)(2,1)S(1)}, u32[]{:S(2)}, u32[]{:S(2)}) collective-permute-start(bf16[224,384]{1,0:T(8,128)(2,1)S(1)} %get-tuple-element.172), channel_id=1, source_target_pairs={{0,8},{1,9},{2,10},{3,11},{4,12},{5,13},{6,14},{7,15},{8,0},{9,1},... | collective-permute-start | bytes 516104 | tf_op jit(solution)/shard_map/ppermute | solution.py:582
  111.9 15.5 %collective-permute-start.40 = (bf16[224,384]{1,0:T(8,128)(2,1)S(1)}, bf16[224,384]{1,0:T(8,128)(2,1)S(1)}, u32[]{:S(2)}, u32[]{:S(2)}) collective-permute-start(bf16[224,384]{1,0:T(8,128)(2,1)S(1)} %get-tuple-element.173), channel_id=1, source_target_pairs={{0,16},{1,17},{2,18},{3,19},{4,20},{5,21},{6,22},{7,23},{8,24},{9,... | collective-permute-start | bytes 516104 | tf_op jit(solution)/shard_map/ppermute | solution.py:582
  112.9 14.5 %collective-permute-start.41 = (bf16[224,384]{1,0:T(8,128)(2,1)S(1)}, bf16[224,384]{1,0:T(8,128)(2,1)S(1)}, u32[]{:S(2)}, u32[]{:S(2)}) collective-permute-start(bf16[224,384]{1,0:T(8,128)(2,1)S(1)} %get-tuple-element.174), channel_id=1, source_target_pairs={{0,24},{1,25},{2,26},{3,27},{4,28},{5,29},{6,30},{7,31},{8,16},{9,... | collective-permute-start | bytes 516104 | tf_op jit(solution)/shard_map/ppermute | solution.py:582
  128.1 8.4 %collective-permute-start.42 = (bf16[192,384]{1,0:T(8,128)(2,1)S(1)}, bf16[192,384]{1,0:T(8,128)(2,1)S(1)}, u32[]{:S(2)}, u32[]{:S(2)}) collective-permute-start(bf16[192,384]{1,0:T(8,128)(2,1)S(1)} %get-tuple-element.175.refs_0_), channel_id=1, source_target_pairs={{0,8},{1,9},{2,10},{3,11},{4,12},{5,13},{6,14},{7,15},{8,0},{9,1},... | collective-permute-start | bytes 442376 | tf_op jit(solution)/shard_map/ppermute | solution.py:582
  131.5 8.8 %collective-permute-start.43 = (bf16[192,384]{1,0:T(8,128)(2,1)S(1)}, bf16[192,384]{1,0:T(8,128)(2,1)S(1)}, u32[]{:S(2)}, u32[]{:S(2)}) collective-permute-start(bf16[192,384]{1,0:T(8,128)(2,1)S(1)} %get-tuple-element.175.refs_0_), channel_id=1, source_target_pairs={{0,16},{1,17},{2,18},{3,19},{4,20},{5,21},{6,22},{7,23},{8,24},{9,... | collective-permute-start | bytes 442376 | tf_op jit(solution)/shard_map/ppermute | solution.py:582
  140.9 10.6 %collective-permute-start.45 = (bf16[608,384]{1,0:T(8,128)(2,1)S(1)}, bf16[608,384]{1,0:T(8,128)(2,1)S(1)}, u32[]{:S(2)}, u32[]{:S(2)}) collective-permute-start(bf16[608,384]{1,0:T(8,128)(2,1)S(1)} %join.5.refs_0_), channel_id=1, source_target_pairs={{0,2},{1,5},{2,0},{3,7},{4,6},{5,1},{6,4},{7,3},{8,10},{9,13},{10,... | collective-permute-start | bytes 1400840 | tf_op jit(solution)/shard_map/ppermute | solution.py:582
  142.3 10.1 %collective-permute-start.46 = (bf16[608,384]{1,0:T(8,128)(2,1)S(1)}, bf16[608,384]{1,0:T(8,128)(2,1)S(1)}, u32[]{:S(2)}, u32[]{:S(2)}) collective-permute-start(bf16[608,384]{1,0:T(8,128)(2,1)S(1)} %join.5.refs_0_), channel_id=1, source_target_pairs={{0,4},{1,3},{2,6},{3,1},{4,0},{5,7},{6,2},{7,5},{8,12},{9,11},{10,... | collective-permute-start | bytes 1400840 | tf_op jit(solution)/shard_map/ppermute | solution.py:582
  152.4 13.3 %collective-permute-start.47 = (bf16[608,384]{1,0:T(8,128)(2,1)S(1)}, bf16[608,384]{1,0:T(8,128)(2,1)S(1)}, u32[]{:S(2)}, u32[]{:S(2)}) collective-permute-start(bf16[608,384]{1,0:T(8,128)(2,1)S(1)} %collective-permute-done.45.refs_1_), channel_id=1, source_target_pairs={{0,4},{1,3},{2,6},{3,1},{4,0},{5,7},{6,2},{7,5},{8,12},{9,11},{10,... | collective-permute-start | bytes 1400840 | tf_op jit(solution)/shard_map/ppermute | solution.py:582
  153.8 11.9 %collective-permute-start.49 = (bf16[192,384]{1,0:T(8,128)(2,1)S(1)}, bf16[192,384]{1,0:T(8,128)(2,1)S(1)}, u32[]{:S(2)}, u32[]{:S(2)}) collective-permute-start(bf16[192,384]{1,0:T(8,128)(2,1)S(1)} %collective-permute-done.44.refs_4_), channel_id=1, source_target_pairs={{0,4},{1,3},{2,6},{3,1},{4,0},{5,7},{6,2},{7,5},{8,12},{9,11},{10,... | collective-permute-start | bytes 442376 | tf_op jit(solution)/shard_map/ppermute | solution.py:582
  155.0 10.8 %collective-permute-start.50 = (bf16[192,384]{1,0:T(8,128)(2,1)S(1)}, bf16[192,384]{1,0:T(8,128)(2,1)S(1)}, u32[]{:S(2)}, u32[]{:S(2)}) collective-permute-start(bf16[192,384]{1,0:T(8,128)(2,1)S(1)} %collective-permute-done.44.refs_4_), channel_id=1, source_target_pairs={{0,6},{1,7},{2,4},{3,5},{4,2},{5,3},{6,0},{7,1},{8,14},{9,15},{10,... | collective-permute-start | bytes 442376 | tf_op jit(solution)/shard_map/ppermute | solution.py:582
  (40 other events, 328.7 us)

commit v4 on v3

--- a/solution.py
+++ b/solution.py
@@ -112,7 +112,8 @@
     return copies
 
 
-def route_body(experts, stride, ids, routes_far, cot_far, slots, *refs):
+def route_body(order, stride, ids, routes_far, cot_far, slots, *refs):
+    experts = len(order)
     chunks, (routes, cot, sems) = refs[:experts], refs[experts:]
     copies = fetch((routes_far, cot_far), (routes, cot), sems)
     copies[0].wait()
@@ -132,7 +133,7 @@
     copies[1].wait()
     mine, _ = halves(cot[...], t)
     for s in range(experts):
-        place = iota((stride, length), 0) + s * stride
+        place = iota((stride, length), 0) + order[s] * stride
         pick = ((place == slot0) | (place == slot1)).astype(bf16)
         chunks[s][...] = nn(pick, mine).astype(bf16)
 
@@ -168,28 +169,27 @@
     allowed = (seq_cols == seq_cols.T) & (iota((rows, rows), 0) >= iota((rows, rows), 1))
     table = nn(rel[...], hot[...], lax.Precision.HIGHEST)
     lane = iota((rows, LANES), 1)
-    for pair in range(queries.shape[1] // LANES):
-        span = slice(pair * LANES, (pair + 1) * LANES)
-        q, k, v = queries[:, span], keys[:, span], values[:, span]
-        mixed = []
-        for side in range(2):
-            head = pair * 2 + side
-            mine = (lane < HEAD_DIM) if side == 0 else (lane >= HEAD_DIM)
-            raw = nt(jnp.where(mine, q, jnp.zeros_like(q)), k)
-            bias = pltpu.roll(
-                jnp.broadcast_to(table[head : head + 1, :], (rows, rows)),
-                0,
-                1,
-                stride=1,
-                stride_axis=0,
-            )
-            scores = jnp.where(allowed, raw * HEAD_DIM ** (-0.5) + bias, -1e30)
-            top = jnp.max(scores, axis=-1, keepdims=True)
-            raised = jnp.exp(scores - top)
-            weight = raised / jnp.sum(raised, axis=-1, keepdims=True)
-            probs[head] = weight
-            mixed.append(nn(weight.astype(bf16), v))
-        mixed_out[:, span] = jnp.where(lane < HEAD_DIM, mixed[0], mixed[1]).astype(bf16)
+    pairs = [slice(i, i + LANES) for i in range(0, queries.shape[1], LANES)]
+    heads = [(span, lane < HEAD_DIM if side == 0 else lane >= HEAD_DIM) for span in pairs for side in (0, 1)]
+    raw = [
+        nt(jnp.where(mine, queries[:, span], jnp.zeros((), bf16)), keys[:, span])
+        for span, mine in heads
+    ]
+    biases = [
+        pltpu.roll(
+            jnp.broadcast_to(table[i : i + 1, :], (rows, rows)), 0, 1, stride=1, stride_axis=0
+        )
+        for i in range(len(heads))
+    ]
+    scores = [jnp.where(allowed, r * HEAD_DIM ** (-0.5) + b, -1e30) for r, b in zip(raw, biases)]
+    tops = [jnp.max(x, axis=-1, keepdims=True) for x in scores]
+    raised = [jnp.exp(x - top) for x, top in zip(scores, tops)]
+    weights = [x / jnp.sum(x, axis=-1, keepdims=True) for x in raised]
+    mixed = [nn(x.astype(bf16), values[:, span]) for x, (span, _) in zip(weights, heads)]
+    for i, x in enumerate(weights):
+        probs[i] = x
+    for i, span in enumerate(pairs):
+        mixed_out[:, span] = jnp.where(lane < HEAD_DIM, mixed[2 * i], mixed[2 * i + 1]).astype(bf16)
     copies[8].wait()
     part[...] = nn(mixed_out[...], wo[...])
 
@@ -200,7 +200,7 @@
     return raised / jnp.sum(raised, axis=-1, keepdims=True)
 
 
-def middle_body(experts, stride, ids, own, other, tokens, gain, router, slots, residual, normed, probs, *chunks):
+def middle_body(order, stride, ids, own, other, tokens, gain, router, slots, residual, normed, probs, *chunks):
     t = ids[2]
     wide = tokens[...].astype(f32) + (own[...] + other[...])
     residual[...] = wide
@@ -209,8 +209,8 @@
     normed[...] = value
     mine, _ = halves(value, t)
     length = slots.shape[1]
-    for s in range(experts):
-        place = iota((stride, length), 0) + s * stride
+    for s in range(len(order)):
+        place = iota((stride, length), 0) + order[s] * stride
         pick = ((place == slots[0:1, :]) | (place == slots[1:2, :])).astype(bf16)
         chunks[s][...] = nn(pick, mine).astype(bf16)
     probs[...] = router_of(value, router[...])
@@ -252,15 +252,19 @@
     own, other, cot_own, cot_other = refs[:4], refs[4:8], refs[8:12], refs[12:16]
     w_in, w_out, router, slope, grad_pre, grads, back_mine, back_other = refs[16:]
     e, t = ids[0], ids[2]
+    gates = []
+    for p in range(4):
+        logits = nt(in_order(own[p][...], other[p][...], t == 0), router[...])
+        raised = jnp.exp(logits - jnp.max(logits, axis=-1, keepdims=True))
+        chosen = jnp.where(iota(raised.shape, 1) == e, raised, 0.0)
+        gates.append(
+            jnp.sum(chosen, axis=-1, keepdims=True) / jnp.sum(raised, axis=-1, keepdims=True)
+        )
     for p in range(4):
         span = pl.ds(p * rows, rows)
         cot_rows = pl.ds(0, rows)
-        logits = nt(in_order(own[p][...], other[p][...], t == 0), router[...])
-        raised = jnp.exp(logits - jnp.max(logits, axis=-1, keepdims=True))
-        chosen = jnp.where(iota(raised.shape, 1) == e, raised, 0.0)
-        gate = jnp.sum(chosen, axis=-1, keepdims=True) / jnp.sum(raised, axis=-1, keepdims=True)
         cot = in_order(cot_own[p][cot_rows, :], cot_other[p][cot_rows, :], t == 0)
-        grad = (gate * cot.astype(f32)).astype(bf16)
+        grad = (gates[p] * cot.astype(f32)).astype(bf16)
         grads[span, :] = grad
         value = (nt(grad, w_out[0]) * slope[span, :]).astype(bf16)
         grad_pre[span, :] = value
@@ -307,7 +311,8 @@
         chunks[s][pl.ds(stride, stride), :] = second[s * stride : (s + 1) * stride]
 
 
-def combine_body(experts, stride, ids, *refs):
+def combine_body(order, stride, ids, *refs):
+    experts = len(order)
     chunks = refs[:experts]
     slots, routes, probs, cot, residual, packed = refs[experts:]
     t = ids[2]
@@ -327,7 +332,7 @@
         )
         chosen = None
         for s in range(experts):
-            place = (iota((length, stride), 1) + s * stride).astype(f32)
+            place = (iota((length, stride), 1) + order[s] * stride).astype(f32)
             pick = (place == slot[:, :1]).astype(bf16)
             value = nn(pick, chunks[s][pl.ds(0, stride), :])
             grad = nn(pick, chunks[s][pl.ds(stride, stride), :])
@@ -384,28 +389,31 @@
     rows = grad.shape[0]
     lane = iota((rows, LANES), 1)
     scale = HEAD_DIM ** (-0.5)
-    for pair in range(q_in.shape[1] // LANES):
-        span = slice(pair * LANES, (pair + 1) * LANES)
-        grad_mixed = nt(grad, wo[span, :]).astype(bf16)
-        q, k, v = q_in[:, span], k_in[:, span], v_in[:, span]
-        mixed = mixed_in[pl.ds(rows, rows), span].astype(f32)
-        dq, dk, dv = [], [], []
-        for side in range(2):
-            head = pair * 2 + side
-            mine = (lane < HEAD_DIM) if side == 0 else (lane >= HEAD_DIM)
-            part = jnp.where(mine, grad_mixed, jnp.zeros_like(grad_mixed))
-            weight = probs[head]
-            dv.append(tn(weight.astype(bf16), grad_mixed))
-            delta = jnp.sum(part.astype(f32) * mixed, axis=-1, keepdims=True)
-            scores = weight * (nt(part, v) - delta)
-            bias[0:1, head * rows : (head + 1) * rows] = sums_by_distance(scores)
-            scores = scores.astype(bf16)
-            dq.append(nn(scores, k))
-            dk.append(tn(scores, q))
-        first = lane < HEAD_DIM
-        stack[0, :, span] = (jnp.where(first, dq[0], dq[1]) * scale).astype(bf16)
-        stack[1, :, span] = (jnp.where(first, dk[0], dk[1]) * scale).astype(bf16)
-        stack[2, :, span] = jnp.where(first, dv[0], dv[1]).astype(bf16)
+    pairs = [slice(i, i + LANES) for i in range(0, q_in.shape[1], LANES)]
+    heads = [(i, lane < HEAD_DIM if side == 0 else lane >= HEAD_DIM) for i in range(len(pairs)) for side in (0, 1)]
+    grad_mixed = [nt(grad, wo[span, :]).astype(bf16) for span in pairs]
+    queries, keys, values = ([ref[:, span] for span in pairs] for ref in (q_in, k_in, v_in))
+    mixed = [mixed_in[pl.ds(rows, rows), span].astype(f32) for span in pairs]
+    weights = [probs[i] for i in range(len(heads))]
+    parts = [jnp.where(mine, grad_mixed[i], jnp.zeros((), bf16)) for i, mine in heads]
+    inner = [nt(part, values[i]) for part, (i, _) in zip(parts, heads)]
+    deltas = [
+        jnp.sum(part.astype(f32) * mixed[i], axis=-1, keepdims=True)
+        for part, (i, _) in zip(parts, heads)
+    ]
+    scores = [w * (x - delta) for w, x, delta in zip(weights, inner, deltas)]
+    half = [x.astype(bf16) for x in scores]
+    dv = [tn(w.astype(bf16), grad_mixed[i]) for w, (i, _) in zip(weights, heads)]
+    dq = [nn(x, keys[i]) for x, (i, _) in zip(half, heads)]
+    dk = [tn(x, queries[i]) for x, (i, _) in zip(half, heads)]
+    sums = [sums_by_distance(x) for x in scores]
+    first = lane < HEAD_DIM
+    for i, span in enumerate(pairs):
+        stack[0, :, span] = (jnp.where(first, dq[2 * i], dq[2 * i + 1]) * scale).astype(bf16)
+        stack[1, :, span] = (jnp.where(first, dk[2 * i], dk[2 * i + 1]) * scale).astype(bf16)
+        stack[2, :, span] = jnp.where(first, dv[2 * i], dv[2 * i + 1]).astype(bf16)
+    for i, row in enumerate(sums):
+        bias[0:1, i * rows : (i + 1) * rows] = row
     stack[3] = halves(grad, t)[0]
     r0[...] = stack[q_id]
     r1[...] = stack[q_id ^ (1 + t)]
@@ -448,7 +456,7 @@
     return jnp.concatenate([tall[:rows], tall[rows:]], axis=1)
 
 
-def partial_body(groups, ids, *refs):
+def partial_body(order, ids, *refs):
     early_own, early_other = refs[:4], refs[4:8]
     right, right_pair, small = refs[8:12], refs[12:16], refs[16]
     blocks, total = refs[17:-1], refs[-1]
@@ -469,16 +477,18 @@
     rights = jnp.concatenate(rights, axis=0)
     total[:width, :] = tn(jnp.concatenate(low, axis=0), rights)
     total[width:, :] = tn(jnp.concatenate(high, axis=0), rights)
+    groups = len(order)
     depth = total.shape[0] // groups
     lead, rest = encode(small[...])
     for s in range(groups):
-        start = pl.multiple_of((e ^ s) * depth, 8)
+        start = pl.multiple_of((e ^ order[s]) * depth, 8)
         blocks[s][pl.ds(0, depth), :] = total[pl.ds(start, depth), :].astype(bf16)
         blocks[s][pl.ds(depth, lead.shape[0]), :] = lead
         blocks[s][pl.ds(depth + lead.shape[0], lead.shape[0]), :] = rest
 
 
-def reduce_body(groups, rows, ids, *refs):
+def reduce_body(order, rows, ids, *refs):
+    groups = len(order)
     arrived, outs = refs[:groups], refs[groups:]
     depth = outs[0].shape[0]
     total = arrived[0][pl.ds(0, depth), :].astype(f32)
@@ -487,7 +497,7 @@
     outs[0][...] = total.astype(bf16)
     code, stack = outs[1:]
     for s in range(groups):
-        stack[s] = decode(arrived[s], depth, rows)
+        stack[order[s]] = decode(arrived[s], depth, rows)
     small = stack[ids[0]]
     for k in range(1, groups):
         small = small + stack[ids[0] ^ k]
@@ -496,7 +506,8 @@
     code[pl.ds(2 * rows, 2 * rows), :] = (small - lead.astype(f32)).astype(bf16)
 
 
-def final_body(groups, experts, rows, ids, *refs):
+def final_body(order, experts, rows, ids, *refs):
+    groups = len(order)
     pieces, hot, outs = refs[:8], refs[8], refs[9:13]
     gain_attn, bias, gain_ffn, router = refs[13:17]
     square, small = refs[17:]
@@ -518,7 +529,7 @@
             @pl.when(place == p)
             def _(p=p, out=out):
                 for s in range(groups):
-                    start = pl.multiple_of((s ^ e) * depth, 8)
+                    start = pl.multiple_of((order[s] ^ e) * depth, 8)
                     piece = pieces[s // per * 4 + p]
                     out[pl.ds(start, depth), :] = piece[pl.ds(s % per * depth, depth), :].astype(f32)
 
@@ -596,8 +607,13 @@
     def to_group(step):
         return lambda e, q, t: (e ^ step, q, t)
 
-    def exchange(chunks):
-        return [chunks[0]] + [send(chunks[s], to_group(s)) for s in range(1, len(chunks))]
+    order = (0, *range(groups // 2, groups), *range(1, groups // 2))
+    last_order = (0, *range(groups // 2, groups - 1), *range(1, groups // 2), groups - 1)
+
+    def exchange(chunks, order=order):
+        return [chunks[0]] + [
+            send(chunk, to_group(step)) for chunk, step in zip(chunks[1:], order[1:])
+        ]
 
     def join(arrays):
         rows = sum(a.shape[0] for a in arrays)
@@ -623,7 +639,7 @@
     chunk = ((stride, half), bf16)
     local_out = ((length, local), bf16)
     slots, *cot_chunks = call(
-        functools.partial(route_body, experts, stride),
+        functools.partial(route_body, order, stride),
         "route",
         ids,
         [((TOP, length), jnp.int32)] + [chunk] * experts,
@@ -668,7 +684,7 @@
     cot_near = spread_first(join(cot_arrived + [early]))
     att_other = send(att_part, to_pair)
     residual, normed_two, router_probs, *row_chunks = call(
-        functools.partial(middle_body, experts, stride),
+        functools.partial(middle_body, order, stride),
         "middle",
         ids,
         [((length, width), f32), ((length, width), bf16), ((length, experts), f32)]
@@ -754,7 +770,7 @@
     )
     returned = exchange(chunks)
     packed = call(
-        functools.partial(combine_body, experts, stride),
+        functools.partial(combine_body, order, stride),
         "combine",
         ids,
         [((length, width + LANES), f32)],
@@ -821,7 +837,7 @@
     right_pair = [send(right_all[p], to_pair) for p in (0, 2, 1, 3)]
     depth = width // groups
     blocks = call(
-        functools.partial(partial_body, groups),
+        functools.partial(partial_body, order),
         "partial",
         ids,
         [((depth + 4 * small_rows, local), bf16)] * groups,
@@ -833,14 +849,14 @@
         scratch=[pltpu.VMEM((width, local), f32)],
     )
     reduced, code = call(
-        functools.partial(reduce_body, groups, small_rows),
+        functools.partial(reduce_body, order, small_rows),
         "reduce",
         ids,
         [((depth, local), bf16), ((4 * small_rows, local), bf16)],
         *exchange(blocks),
         scratch=[pltpu.VMEM((groups, 2 * small_rows, local), f32)],
     )
-    spread = exchange([reduced] * groups)
+    spread = exchange([reduced] * groups, last_order)
     near, rest = spread[:-1], spread[-1:]
     matrix = join(near + [code])
     first, second = send(matrix, to_first), send(matrix, to_second)
@@ -850,7 +866,7 @@
     first_two, second_two = send(matrix_two, to_first), send(matrix_two, to_second)
     far_two = send(matrix_two, to_far)
     grads = call(
-        functools.partial(final_body, groups, experts, small_rows),
+        functools.partial(final_body, last_order, experts, small_rows),
         "final",
         ids,
         [((width, local), f32)] * 3

time: 169 us -> 166 us (0.982)
  Pallas kernels: 37.9 us -> 34.5 us
  waiting for transfers between devices: 78.7 us -> 80.6 us
    pallas_call x21, Pallas kernels: 37.9 us -> 34.5 us  [call(): pl.pallas_call(body, out_shape=shapes, in_specs=[pl.BlockSpec(memory_spac...]
    ppermute x51, waiting for transfers between devices: 78.7 us -> 80.6 us  [send(): return lax.ppermute(array, ('dp', 'tensor'), pairs)]
  transfers between devices with their start and end apart: 51 -> 51, of which waited for: 32 -> 31; matrix products, arithmetic and copies ran while one was open for 0% -> 0% of each run, Pallas kernels for 14% -> 13%
where the time goes in v4:
time: 166 us
  waiting for transfers between devices  80.6 us (49%)
  starting transfers between devices  49.7 us (30%)
  Pallas kernels  34.5 us (21%)
    ppermute x51, waiting for transfers between devices, send(): return lax.ppermute(array, ('dp', 'tensor'), pairs)  80.6 us
    ppermute x51, starting transfers between devices, send(): return lax.ppermute(array, ('dp', 'tensor'), pairs)  49.7 us
    pallas_call x21, Pallas kernels, call(): pl.pallas_call(body, out_shape=shapes, in_specs=[pl.BlockSpec(memory_spac...  34.5 us
  transfers between devices with their start and end apart: 51, of which 31 were waited for; matrix products, arithmetic and copies ran while one was open for 0% of the time, Pallas kernels for 13%

profile of v4, /device:TPU:0, one launch (start us, length us, event | category | flops | bytes accessed | tf_op | source)
XLA Modules:
  0.0 165.8 jit_solution(708858263443043882)
XLA Ops:
  2.5 4.1 %collective-permute-start = (bf16[80,384]{1,0:T(8,128)(2,1)S(1)}, bf16[80,384]{1,0:T(8,128)(2,1)S(1)}, u32[]{:S(2)}, u32[]{:S(2)}) collective-permute-start(bf16[80,384]{1,0:T(8,128)(2,1)S(1)} %get-tuple-element.103), channel_id=1, source_target_pairs={{0,16},{1,17},{2,18},{3,19},{4,20},{5,21},{6,22},{7,23},{8,24},{9,... | collective-permute-start | bytes 184328 | tf_op jit(solution)/shard_map/ppermute | solution.py:593
  8.2 3.7 %front.1 = (bf16[256,384]{1,0:T(8,128)(2,1)S(1)}, f32[128,768]{1,0:T(8,128)S(1)}, bf16[128,384]{1,0:T(8,128)(2,1)S(1)}, bf16[128,384]{1,0:T(8,128)(2,1)S(1)}, bf...) custom-call(s32[3]{0:T(128)S(1)} %pad_add_fusion.ids, bf16[128,768]{1,0:T(8,128)(2,1)} %tokens.3, f32[768]{0:T(1024)} %gain.5, ...), custom_call_target="tpu_custom_call" | custom-call | bytes 18000000 | tf_op jit(solution)/shard_map/front/pallas_call | solution.py:53
  17.7 2.4 %collective-permute-start.4 = (bf16[80,384]{1,0:T(8,128)(2,1)S(1)}, bf16[80,384]{1,0:T(8,128)(2,1)S(1)}, u32[]{:S(2)}, u32[]{:S(2)}) collective-permute-start(bf16[80,384]{1,0:T(8,128)(2,1)S(1)} %get-tuple-element.109), channel_id=1, source_target_pairs={{0,16},{1,17},{2,18},{3,19},{4,20},{5,21},{6,22},{7,23},{8,24},{9,... | collective-permute-start | bytes 184328 | tf_op jit(solution)/shard_map/ppermute | solution.py:593
  21.2 4.6 %collective-permute-done.7.refs_9_.refs_1_ = bf16[576,384]{1,0:T(8,128)(2,1)S(1)} collective-permute-done((bf16[576,384]{1,0:T(8,128)(2,1)S(1)}, bf16[576,384]{1,0:T(8,128)(2,1)S(1)}, u32[]{:S(2)}, u32[]{:S(2)}) %collective-permute-start.7) | collective-permute-done | bytes 442400 | tf_op jit(solution)/shard_map/ppermute | solution.py:593
  30.2 5.3 %collective-permute-done.9.refs_1_ = bf16[320,384]{1,0:T(8,128)(2,1)S(1)} collective-permute-done((bf16[320,384]{1,0:T(8,128)(2,1)S(1)}, bf16[320,384]{1,0:T(8,128)(2,1)S(1)}, u32[]{:S(2)}, u32[]{:S(2)}) %collective-permute-start.9) | collective-permute-done | bytes 245792 | tf_op jit(solution)/shard_map/ppermute | solution.py:593
  45.3 3.4 %expert.1 = (bf16[1280,384]{1,0:T(8,128)(2,1)S(1)}, f32[1280,384]{1,0:T(8,128)S(1)}, bf16[1280,384]{1,0:T(8,128)(2,1)S(1)}, bf16[1280,384]{1,0:T(8,128)(2,1)S(1)}) custom-call(s32[3]{0:T(128)S(1)} %pad_add_fusion.ids, bf16[320,384]{1,0:T(8,128)(2,1)S(1)} %join.4.refs_0_, bf16[320,384]{1,0:T(8,128)(2,1)S(1)} %collective-permute-done.9.refs_1_, ...), custom_call_target="tpu_custom_call" | custom-call | bytes 15840000 | tf_op jit(solution)/shard_map/expert/pallas_call | solution.py:53
  49.2 3.8 %expert_back.1 = (bf16[1280,384]{1,0:T(8,128)(2,1)S(1)}, bf16[1280,768]{1,0:T(8,128)(2,1)S(1)}, bf16[1280,384]{1,0:T(8,128)(2,1)S(1)}, bf16[1280,384]{1,0:T(8,128)(2,1)S(1)}) custom-call(s32[3]{0:T(128)S(1)} %pad_add_fusion.ids, bf16[320,384]{1,0:T(8,128)(2,1)S(1)} %join.4.refs_0_, bf16[320,384]{1,0:T(8,128)(2,1)S(1)} %collective-permute-done.9.refs_1_, ...), custom_call_target="tpu_custom_call" | custom-call | bytes 19440000 | tf_op jit(solution)/shard_map/expert_back/pallas_call | solution.py:53
  57.8 5.1 %collective-permute-done.17.received = bf16[640,384]{1,0:T(8,128)(2,1)S(1)} collective-permute-done((bf16[640,384]{1,0:T(8,128)(2,1)S(1)}, bf16[640,384]{1,0:T(8,128)(2,1)S(1)}, u32[]{:S(2)}, u32[]{:S(2)}) %collective-permute-start.17) | collective-permute-done | bytes 491552 | tf_op jit(solution)/shard_map/ppermute | solution.py:593
  64.7 5.9 %collective-permute-done.25.received = bf16[640,384]{1,0:T(8,128)(2,1)S(1)} collective-permute-done((bf16[640,384]{1,0:T(8,128)(2,1)S(1)}, bf16[640,384]{1,0:T(8,128)(2,1)S(1)}, u32[]{:S(2)}, u32[]{:S(2)}) %collective-permute-start.25) | collective-permute-done | bytes 491552 | tf_op jit(solution)/shard_map/ppermute | solution.py:593
  72.4 3.8 %expert_grads.1 = (f32[1,768,384]{2,1,0:T(8,128)}, f32[1,384,768]{2,1,0:T(8,128)}) custom-call(s32[3]{0:T(128)S(1)} %pad_add_fusion.ids, bf16[320,384]{1,0:T(8,128)(2,1)S(1)} %join.4.refs_0_, bf16[320,384]{1,0:T(8,128)(2,1)S(1)} %collective-permute-done.9.refs_1_, bf16[320,384]{1,0:T(8,128)(2,1)S(1)} %collective-permute-done.10.refs_2_, ...), custom_call_target="tpu_custom_call" | custom-call | bytes 14400000 | tf_op jit(solution)/shard_map/expert_grads/pallas_call | solution.py:53
  78.1 2.3 %collective-permute-start.27 = (bf16[160,384]{1,0:T(8,128)(2,1)S(1)}, bf16[160,384]{1,0:T(8,128)(2,1)S(1)}, u32[]{:S(2)}, u32[]{:S(2)}) collective-permute-start(bf16[160,384]{1,0:T(8,128)(2,1)S(1)} %get-tuple-element.144), channel_id=1, source_target_pairs={{0,16},{1,17},{2,18},{3,19},{4,20},{5,21},{6,22},{7,23},{8,24},{9,... | collective-permute-start | bytes 368648 | tf_op jit(solution)/shard_map/ppermute | solution.py:593
  81.6 4.3 %collective-permute-done.27.refs_1_ = bf16[160,384]{1,0:T(8,128)(2,1)S(1)} collective-permute-done((bf16[160,384]{1,0:T(8,128)(2,1)S(1)}, bf16[160,384]{1,0:T(8,128)(2,1)S(1)}, u32[]{:S(2)}, u32[]{:S(2)}) %collective-permute-start.27) | collective-permute-done | bytes 122912 | tf_op jit(solution)/shard_map/ppermute | solution.py:593
  93.5 1.9 %attend_back.1 = (bf16[128,384]{1,0:T(8,128)(2,1)S(1)}, bf16[128,384]{1,0:T(8,128)(2,1)S(1)}, bf16[128,384]{1,0:T(8,128)(2,1)S(1)}, bf16[128,384]{1,0:T(8,128)(2...) custom-call(s32[3]{0:T(128)S(1)} %pad_add_fusion.ids, bf16[128,768]{1,0:T(8,128)(2,1)S(1)} %get-tuple-element.151.att, ...), custom_call_target="tpu_custom_call" | custom-call | bytes 9000000 | tf_op jit(solution)/shard_map/attend_back/pallas_call | solution.py:53
  101.6 2.1 %collective-permute-done.34.refs_11_ = bf16[128,384]{1,0:T(8,128)(2,1)S(1)} collective-permute-done((bf16[128,384]{1,0:T(8,128)(2,1)S(1)}, bf16[128,384]{1,0:T(8,128)(2,1)S(1)}, u32[]{:S(2)}, u32[]{:S(2)}) %collective-permute-start.34) | collective-permute-done | bytes 98336 | tf_op jit(solution)/shard_map/ppermute | solution.py:593
  107.0 2.1 %collective-permute-start.39 = (bf16[224,384]{1,0:T(8,128)(2,1)S(1)}, bf16[224,384]{1,0:T(8,128)(2,1)S(1)}, u32[]{:S(2)}, u32[]{:S(2)}) collective-permute-start(bf16[224,384]{1,0:T(8,128)(2,1)S(1)} %get-tuple-element.172), channel_id=1, source_target_pairs={{0,16},{1,17},{2,18},{3,19},{4,20},{5,21},{6,22},{7,23},{8,24},{9,... | collective-permute-start | bytes 516104 | tf_op jit(solution)/shard_map/ppermute | solution.py:593
  110.5 11.6 %collective-permute-done.39.refs_1_ = bf16[224,384]{1,0:T(8,128)(2,1)S(1)} collective-permute-done((bf16[224,384]{1,0:T(8,128)(2,1)S(1)}, bf16[224,384]{1,0:T(8,128)(2,1)S(1)}, u32[]{:S(2)}, u32[]{:S(2)}) %collective-permute-start.39) | collective-permute-done | bytes 172064 | tf_op jit(solution)/shard_map/ppermute | solution.py:593
  124.0 4.2 %collective-permute-start.42 = (bf16[192,384]{1,0:T(8,128)(2,1)S(1)}, bf16[192,384]{1,0:T(8,128)(2,1)S(1)}, u32[]{:S(2)}, u32[]{:S(2)}) collective-permute-start(bf16[192,384]{1,0:T(8,128)(2,1)S(1)} %get-tuple-element.175.refs_0_), channel_id=1, source_target_pairs={{0,16},{1,17},{2,18},{3,19},{4,20},{5,21},{6,22},{7,23},{8,24},{9,... | collective-permute-start | bytes 442376 | tf_op jit(solution)/shard_map/ppermute | solution.py:593
  128.2 7.1 %collective-permute-done.42.refs_1_ = bf16[192,384]{1,0:T(8,128)(2,1)S(1)} collective-permute-done((bf16[192,384]{1,0:T(8,128)(2,1)S(1)}, bf16[192,384]{1,0:T(8,128)(2,1)S(1)}, u32[]{:S(2)}, u32[]{:S(2)}) %collective-permute-start.42) | collective-permute-done | bytes 147488 | tf_op jit(solution)/shard_map/ppermute | solution.py:593
  136.3 1.9 %collective-permute-start.45 = (bf16[608,384]{1,0:T(8,128)(2,1)S(1)}, bf16[608,384]{1,0:T(8,128)(2,1)S(1)}, u32[]{:S(2)}, u32[]{:S(2)}) collective-permute-start(bf16[608,384]{1,0:T(8,128)(2,1)S(1)} %join.5.refs_0_), channel_id=1, source_target_pairs={{0,2},{1,5},{2,0},{3,7},{4,6},{5,1},{6,4},{7,3},{8,10},{9,13},{10,... | collective-permute-start | bytes 1400840 | tf_op jit(solution)/shard_map/ppermute | solution.py:593
  139.6 5.7 %collective-permute-done.44.refs_4_ = bf16[192,384]{1,0:T(8,128)(2,1)S(1)} collective-permute-done((bf16[192,384]{1,0:T(8,128)(2,1)S(1)}, bf16[192,384]{1,0:T(8,128)(2,1)S(1)}, u32[]{:S(2)}, u32[]{:S(2)}) %collective-permute-start.44) | collective-permute-done | bytes 147488 | tf_op jit(solution)/shard_map/ppermute | solution.py:593
  145.3 3.3 %collective-permute-done.45.refs_1_ = bf16[608,384]{1,0:T(8,128)(2,1)S(1)} collective-permute-done((bf16[608,384]{1,0:T(8,128)(2,1)S(1)}, bf16[608,384]{1,0:T(8,128)(2,1)S(1)}, u32[]{:S(2)}, u32[]{:S(2)}) %collective-permute-start.45) | collective-permute-done | bytes 466976 | tf_op jit(solution)/shard_map/ppermute | solution.py:593
  153.0 3.3 %collective-permute-done.48.refs_5_ = bf16[192,384]{1,0:T(8,128)(2,1)S(1)} collective-permute-done((bf16[192,384]{1,0:T(8,128)(2,1)S(1)}, bf16[192,384]{1,0:T(8,128)(2,1)S(1)}, u32[]{:S(2)}, u32[]{:S(2)}) %collective-permute-start.48) | collective-permute-done | bytes 147488 | tf_op jit(solution)/shard_map/ppermute | solution.py:593
  156.3 6.4 %collective-permute-done.49.refs_6_ = bf16[192,384]{1,0:T(8,128)(2,1)S(1)} collective-permute-done((bf16[192,384]{1,0:T(8,128)(2,1)S(1)}, bf16[192,384]{1,0:T(8,128)(2,1)S(1)}, u32[]{:S(2)}, u32[]{:S(2)}) %collective-permute-start.49) | collective-permute-done | bytes 147488 | tf_op jit(solution)/shard_map/ppermute | solution.py:593
  162.7 3.2 %final.1 = (f32[768,384]{1,0:T(8,128)}, f32[768,384]{1,0:T(8,128)}, f32[768,384]{1,0:T(8,128)}, f32[384,768]{1,0:T(8,128)}, f32[768]{0:T(1024)}, /*index=5*/f32[6,32]{1,0:T(8,128)}, f32[768]{0:T(1024)}, f32[4,768]{1,0:T(4,128)}) custom-call(s32[3]{0:T(128)S(1)} %pad_add_fusion.ids, bf16[608,384]{1,0:T(8,128)(2,1)S(1)} %join.5.refs_0_, ...), custom_call_target="tpu_custom_call" | custom-call | bytes 14040000 | tf_op jit(solution)/shard_map/final/pallas_call | solution.py:53
  (126 shorter events, 63.5 us)
Async XLA Ops:
  2.5 9.4 %collective-permute-start = (bf16[80,384]{1,0:T(8,128)(2,1)S(1)}, bf16[80,384]{1,0:T(8,128)(2,1)S(1)}, u32[]{:S(2)}, u32[]{:S(2)}) collective-permute-start(bf16[80,384]{1,0:T(8,128)(2,1)S(1)} %get-tuple-element.103), channel_id=1, source_target_pairs={{0,16},{1,17},{2,18},{3,19},{4,20},{5,21},{6,22},{7,23},{8,24},{9,... | collective-permute-start | bytes 184328 | tf_op jit(solution)/shard_map/ppermute | solution.py:593
  13.4 12.4 %collective-permute-start.7 = (bf16[576,384]{1,0:T(8,128)(2,1)S(1)}, bf16[576,384]{1,0:T(8,128)(2,1)S(1)}, u32[]{:S(2)}, u32[]{:S(2)}) collective-permute-start(bf16[576,384]{1,0:T(8,128)(2,1)S(1)} %join.3.refs_8_.refs_0_), channel_id=1, source_target_pairs={{0,2},{1,5},{2,0},{3,7},{4,6},{5,1},{6,4},{7,3},{8,10},{9,13},{10,... | collective-permute-start | bytes 1327112 | tf_op jit(solution)/shard_map/ppermute | solution.py:593
  15.0 11.1 %collective-permute-start.8 = (bf16[576,384]{1,0:T(8,128)(2,1)S(1)}, bf16[576,384]{1,0:T(8,128)(2,1)S(1)}, u32[]{:S(2)}, u32[]{:S(2)}) collective-permute-start(bf16[576,384]{1,0:T(8,128)(2,1)S(1)} %join.3.refs_8_.refs_0_), channel_id=1, source_target_pairs={{0,4},{1,3},{2,6},{3,1},{4,0},{5,7},{6,2},{7,5},{8,12},{9,11},{10,... | collective-permute-start | bytes 1327112 | tf_op jit(solution)/shard_map/ppermute | solution.py:593
  17.7 8.4 %collective-permute-start.4 = (bf16[80,384]{1,0:T(8,128)(2,1)S(1)}, bf16[80,384]{1,0:T(8,128)(2,1)S(1)}, u32[]{:S(2)}, u32[]{:S(2)}) collective-permute-start(bf16[80,384]{1,0:T(8,128)(2,1)S(1)} %get-tuple-element.109), channel_id=1, source_target_pairs={{0,16},{1,17},{2,18},{3,19},{4,20},{5,21},{6,22},{7,23},{8,24},{9,... | collective-permute-start | bytes 184328 | tf_op jit(solution)/shard_map/ppermute | solution.py:593
  26.8 8.7 %collective-permute-start.9 = (bf16[320,384]{1,0:T(8,128)(2,1)S(1)}, bf16[320,384]{1,0:T(8,128)(2,1)S(1)}, u32[]{:S(2)}, u32[]{:S(2)}) collective-permute-start(bf16[320,384]{1,0:T(8,128)(2,1)S(1)} %join.4.refs_0_), channel_id=1, source_target_pairs={{0,2},{1,5},{2,0},{3,7},{4,6},{5,1},{6,4},{7,3},{8,10},{9,13},{10,... | collective-permute-start | bytes 737288 | tf_op jit(solution)/shard_map/ppermute | solution.py:593
  28.2 9.1 %collective-permute-start.10 = (bf16[320,384]{1,0:T(8,128)(2,1)S(1)}, bf16[320,384]{1,0:T(8,128)(2,1)S(1)}, u32[]{:S(2)}, u32[]{:S(2)}) collective-permute-start(bf16[320,384]{1,0:T(8,128)(2,1)S(1)} %join.4.refs_0_), channel_id=1, source_target_pairs={{0,4},{1,3},{2,6},{3,1},{4,0},{5,7},{6,2},{7,5},{8,12},{9,11},{10,... | collective-permute-start | bytes 737288 | tf_op jit(solution)/shard_map/ppermute | solution.py:593
  30.0 9.6 %collective-permute-start.19 = (bf16[576,384]{1,0:T(8,128)(2,1)S(1)}, bf16[576,384]{1,0:T(8,128)(2,1)S(1)}, u32[]{:S(2)}, u32[]{:S(2)}) collective-permute-start(bf16[576,384]{1,0:T(8,128)(2,1)S(1)} %collective-permute-done.7.refs_9_.refs_1_), channel_id=1, source_target_pairs={{0,4},{1,3},{2,6},{3,1},{4,0},{5,7},{6,2},{7,5},{8,12},{9,11},{10,... | collective-permute-start | bytes 1327112 | tf_op jit(solution)/shard_map/ppermute | solution.py:593
  30.2 7.5 %collective-permute-start.12 = (bf16[320,384]{1,0:T(8,128)(2,1)S(1)}, bf16[320,384]{1,0:T(8,128)(2,1)S(1)}, u32[]{:S(2)}, u32[]{:S(2)}) collective-permute-start(bf16[320,384]{1,0:T(8,128)(2,1)S(1)} %join.4.refs_0_), channel_id=1, source_target_pairs={{0,1},{1,0},{2,3},{3,2},{4,5},{5,4},{6,7},{7,6},{8,9},{9,8},{10,11... | collective-permute-start | bytes 737288 | tf_op jit(solution)/shard_map/ppermute | solution.py:593
  37.8 11.4 %collective-permute-start.20 = (bf16[576,384]{1,0:T(8,128)(2,1)S(1)}, bf16[576,384]{1,0:T(8,128)(2,1)S(1)}, u32[]{:S(2)}, u32[]{:S(2)}) collective-permute-start(bf16[576,384]{1,0:T(8,128)(2,1)S(1)} %join.3.refs_8_.refs_0_), channel_id=1, source_target_pairs={{0,1},{1,0},{2,3},{3,2},{4,5},{5,4},{6,7},{7,6},{8,9},{9,8},{10,11... | collective-permute-start | bytes 1327112 | tf_op jit(solution)/shard_map/ppermute | solution.py:593
  39.6 9.6 %collective-permute-start.22 = (bf16[576,384]{1,0:T(8,128)(2,1)S(1)}, bf16[576,384]{1,0:T(8,128)(2,1)S(1)}, u32[]{:S(2)}, u32[]{:S(2)}) collective-permute-start(bf16[576,384]{1,0:T(8,128)(2,1)S(1)} %collective-permute-done.7.refs_9_.refs_1_), channel_id=1, source_target_pairs={{0,1},{1,0},{2,3},{3,2},{4,5},{5,4},{6,7},{7,6},{8,9},{9,8},{10,11... | collective-permute-start | bytes 1327112 | tf_op jit(solution)/shard_map/ppermute | solution.py:593
  54.0 8.9 %collective-permute-start.17 = (bf16[640,384]{1,0:T(8,128)(2,1)S(1)}, bf16[640,384]{1,0:T(8,128)(2,1)S(1)}, u32[]{:S(2)}, u32[]{:S(2)}) collective-permute-start(bf16[640,384]{1,0:T(8,128)(2,1)S(1)} %get-tuple-element.124), channel_id=1, source_target_pairs={{0,2},{1,5},{2,0},{3,7},{4,6},{5,1},{6,4},{7,3},{8,10},{9,13},{10,... | collective-permute-start | bytes 1474568 | tf_op jit(solution)/shard_map/ppermute | solution.py:593
  56.4 14.1 %collective-permute-start.25 = (bf16[640,384]{1,0:T(8,128)(2,1)S(1)}, bf16[640,384]{1,0:T(8,128)(2,1)S(1)}, u32[]{:S(2)}, u32[]{:S(2)}) collective-permute-start(bf16[640,384]{1,0:T(8,128)(2,1)S(1)} %get-tuple-element.133), channel_id=1, source_target_pairs={{0,2},{1,5},{2,0},{3,7},{4,6},{5,1},{6,4},{7,3},{8,10},{9,13},{10,... | collective-permute-start | bytes 1474568 | tf_op jit(solution)/shard_map/ppermute | solution.py:593
  63.5 12.7 %collective-permute-start.18 = (bf16[320,384]{1,0:T(8,128)(2,1)S(1)}, bf16[320,384]{1,0:T(8,128)(2,1)S(1)}, u32[]{:S(2)}, u32[]{:S(2)}) collective-permute-start(bf16[320,384]{1,0:T(8,128)(2,1)S(1)} %get-tuple-element.126), channel_id=1, source_target_pairs={{0,4},{1,3},{2,6},{3,1},{4,0},{5,7},{6,2},{7,5},{8,12},{9,11},{10,... | collective-permute-start | bytes 737288 | tf_op jit(solution)/shard_map/ppermute | solution.py:593
  78.1 7.8 %collective-permute-start.27 = (bf16[160,384]{1,0:T(8,128)(2,1)S(1)}, bf16[160,384]{1,0:T(8,128)(2,1)S(1)}, u32[]{:S(2)}, u32[]{:S(2)}) collective-permute-start(bf16[160,384]{1,0:T(8,128)(2,1)S(1)} %get-tuple-element.144), channel_id=1, source_target_pairs={{0,16},{1,17},{2,18},{3,19},{4,20},{5,21},{6,22},{7,23},{8,24},{9,... | collective-permute-start | bytes 368648 | tf_op jit(solution)/shard_map/ppermute | solution.py:593
  107.0 15.2 %collective-permute-start.39 = (bf16[224,384]{1,0:T(8,128)(2,1)S(1)}, bf16[224,384]{1,0:T(8,128)(2,1)S(1)}, u32[]{:S(2)}, u32[]{:S(2)}) collective-permute-start(bf16[224,384]{1,0:T(8,128)(2,1)S(1)} %get-tuple-element.172), channel_id=1, source_target_pairs={{0,16},{1,17},{2,18},{3,19},{4,20},{5,21},{6,22},{7,23},{8,24},{9,... | collective-permute-start | bytes 516104 | tf_op jit(solution)/shard_map/ppermute | solution.py:593
  109.1 13.1 %collective-permute-start.40 = (bf16[224,384]{1,0:T(8,128)(2,1)S(1)}, bf16[224,384]{1,0:T(8,128)(2,1)S(1)}, u32[]{:S(2)}, u32[]{:S(2)}) collective-permute-start(bf16[224,384]{1,0:T(8,128)(2,1)S(1)} %get-tuple-element.173), channel_id=1, source_target_pairs={{0,24},{1,25},{2,26},{3,27},{4,28},{5,29},{6,30},{7,31},{8,16},{9,... | collective-permute-start | bytes 516104 | tf_op jit(solution)/shard_map/ppermute | solution.py:593
  110.1 13.3 %collective-permute-start.41 = (bf16[224,384]{1,0:T(8,128)(2,1)S(1)}, bf16[224,384]{1,0:T(8,128)(2,1)S(1)}, u32[]{:S(2)}, u32[]{:S(2)}) collective-permute-start(bf16[224,384]{1,0:T(8,128)(2,1)S(1)} %get-tuple-element.174), channel_id=1, source_target_pairs={{0,8},{1,9},{2,10},{3,11},{4,12},{5,13},{6,14},{7,15},{8,0},{9,1},... | collective-permute-start | bytes 516104 | tf_op jit(solution)/shard_map/ppermute | solution.py:593
  124.0 11.3 %collective-permute-start.42 = (bf16[192,384]{1,0:T(8,128)(2,1)S(1)}, bf16[192,384]{1,0:T(8,128)(2,1)S(1)}, u32[]{:S(2)}, u32[]{:S(2)}) collective-permute-start(bf16[192,384]{1,0:T(8,128)(2,1)S(1)} %get-tuple-element.175.refs_0_), channel_id=1, source_target_pairs={{0,16},{1,17},{2,18},{3,19},{4,20},{5,21},{6,22},{7,23},{8,24},{9,... | collective-permute-start | bytes 442376 | tf_op jit(solution)/shard_map/ppermute | solution.py:593
  128.2 7.4 %collective-permute-start.43 = (bf16[192,384]{1,0:T(8,128)(2,1)S(1)}, bf16[192,384]{1,0:T(8,128)(2,1)S(1)}, u32[]{:S(2)}, u32[]{:S(2)}) collective-permute-start(bf16[192,384]{1,0:T(8,128)(2,1)S(1)} %get-tuple-element.175.refs_0_), channel_id=1, source_target_pairs={{0,8},{1,9},{2,10},{3,11},{4,12},{5,13},{6,14},{7,15},{8,0},{9,1},... | collective-permute-start | bytes 442376 | tf_op jit(solution)/shard_map/ppermute | solution.py:593
  136.3 12.4 %collective-permute-start.45 = (bf16[608,384]{1,0:T(8,128)(2,1)S(1)}, bf16[608,384]{1,0:T(8,128)(2,1)S(1)}, u32[]{:S(2)}, u32[]{:S(2)}) collective-permute-start(bf16[608,384]{1,0:T(8,128)(2,1)S(1)} %join.5.refs_0_), channel_id=1, source_target_pairs={{0,2},{1,5},{2,0},{3,7},{4,6},{5,1},{6,4},{7,3},{8,10},{9,13},{10,... | collective-permute-start | bytes 1400840 | tf_op jit(solution)/shard_map/ppermute | solution.py:593
  138.2 10.5 %collective-permute-start.46 = (bf16[608,384]{1,0:T(8,128)(2,1)S(1)}, bf16[608,384]{1,0:T(8,128)(2,1)S(1)}, u32[]{:S(2)}, u32[]{:S(2)}) collective-permute-start(bf16[608,384]{1,0:T(8,128)(2,1)S(1)} %join.5.refs_0_), channel_id=1, source_target_pairs={{0,4},{1,3},{2,6},{3,1},{4,0},{5,7},{6,2},{7,5},{8,12},{9,11},{10,... | collective-permute-start | bytes 1400840 | tf_op jit(solution)/shard_map/ppermute | solution.py:593
  148.7 14.0 %collective-permute-start.47 = (bf16[608,384]{1,0:T(8,128)(2,1)S(1)}, bf16[608,384]{1,0:T(8,128)(2,1)S(1)}, u32[]{:S(2)}, u32[]{:S(2)}) collective-permute-start(bf16[608,384]{1,0:T(8,128)(2,1)S(1)} %collective-permute-done.45.refs_1_), channel_id=1, source_target_pairs={{0,4},{1,3},{2,6},{3,1},{4,0},{5,7},{6,2},{7,5},{8,12},{9,11},{10,... | collective-permute-start | bytes 1400840 | tf_op jit(solution)/shard_map/ppermute | solution.py:593
  151.2 11.4 %collective-permute-start.49 = (bf16[192,384]{1,0:T(8,128)(2,1)S(1)}, bf16[192,384]{1,0:T(8,128)(2,1)S(1)}, u32[]{:S(2)}, u32[]{:S(2)}) collective-permute-start(bf16[192,384]{1,0:T(8,128)(2,1)S(1)} %collective-permute-done.44.refs_4_), channel_id=1, source_target_pairs={{0,4},{1,3},{2,6},{3,1},{4,0},{5,7},{6,2},{7,5},{8,12},{9,11},{10,... | collective-permute-start | bytes 442376 | tf_op jit(solution)/shard_map/ppermute | solution.py:593
  151.6 11.0 %collective-permute-start.50 = (bf16[192,384]{1,0:T(8,128)(2,1)S(1)}, bf16[192,384]{1,0:T(8,128)(2,1)S(1)}, u32[]{:S(2)}, u32[]{:S(2)}) collective-permute-start(bf16[192,384]{1,0:T(8,128)(2,1)S(1)} %collective-permute-done.44.refs_4_), channel_id=1, source_target_pairs={{0,6},{1,7},{2,4},{3,5},{4,2},{5,3},{6,0},{7,1},{8,14},{9,15},{10,... | collective-permute-start | bytes 442376 | tf_op jit(solution)/shard_map/ppermute | solution.py:593
  (40 other events, 319.8 us)

commit v5 on v4

--- a/solution.py
+++ b/solution.py
@@ -502,25 +502,25 @@
     for k in range(1, groups):
         small = small + stack[ids[0] ^ k]
     lead = small.astype(bf16)
-    code[pl.ds(0, 2 * rows), :] = lead
-    code[pl.ds(2 * rows, 2 * rows), :] = (small - lead.astype(f32)).astype(bf16)
+    code[pl.ds(0, depth), :] = outs[0][...]
+    code[pl.ds(depth, 2 * rows), :] = lead
+    code[pl.ds(depth + 2 * rows, 2 * rows), :] = (small - lead.astype(f32)).astype(bf16)
 
 
 def final_body(order, experts, rows, ids, *refs):
     groups = len(order)
-    pieces, hot, outs = refs[:8], refs[8], refs[9:13]
-    gain_attn, bias, gain_ffn, router = refs[13:17]
-    square, small = refs[17:]
+    pieces, hot, outs = refs[:12], refs[12], refs[13:17]
+    gain_attn, bias, gain_ffn, router = refs[17:21]
+    square, small = refs[21:]
     e, q, t = ids[0], ids[1], ids[2]
     depth = square.shape[0] // groups
-    per = groups - 1
 
     def place_of(chip):
         away = q ^ chip
         return jnp.where((t == 1) & ((away == 1) | (away == 2)), 3 - away, away)
 
     for p in range(4):
-        small[p] = decode(pieces[p], per * depth, rows)
+        small[p] = decode(pieces[p], depth, rows)
     for m in range(4):
         out = outs[m] if m < 3 else square
         place = place_of(m)
@@ -530,8 +530,9 @@
             def _(p=p, out=out):
                 for s in range(groups):
                     start = pl.multiple_of((order[s] ^ e) * depth, 8)
-                    piece = pieces[s // per * 4 + p]
-                    out[pl.ds(start, depth), :] = piece[pl.ds(s % per * depth, depth), :].astype(f32)
+                    step, at = (0, 0) if s == 0 else (2, 0) if s == groups - 1 else (1, s - 1)
+                    piece = pieces[step * 4 + p]
+                    out[pl.ds(start, depth), :] = piece[pl.ds(at * depth, depth), :].astype(f32)
 
     outs[3][...] = square[...].T
     total = widen(small[place_of(0)] + small[place_of(1)] + small[place_of(2)] + small[place_of(3)])
@@ -852,19 +853,22 @@
         functools.partial(reduce_body, order, small_rows),
         "reduce",
         ids,
-        [((depth, local), bf16), ((4 * small_rows, local), bf16)],
+        [((depth, local), bf16), ((depth + 4 * small_rows, local), bf16)],
         *exchange(blocks),
         scratch=[pltpu.VMEM((groups, 2 * small_rows, local), f32)],
     )
     spread = exchange([reduced] * groups, last_order)
-    near, rest = spread[:-1], spread[-1:]
-    matrix = join(near + [code])
-    first, second = send(matrix, to_first), send(matrix, to_second)
-    *rest, first, second = lax.optimization_barrier((*rest, first, second))
-    far = send(first, to_second)
-    matrix_two = rest[0]
-    first_two, second_two = send(matrix_two, to_first), send(matrix_two, to_second)
-    far_two = send(matrix_two, to_far)
+    def near(matrix):
+        return [matrix, send(matrix, to_first), send(matrix, to_second)]
+
+    start = near(code)
+    joint = lax.optimization_barrier((*spread[1:-1], *start[1:]))
+    start[1:] = joint[-2:]
+    start.append(send(start[1], to_second))
+    inner = near(join(joint[:-2]))
+    last, *inner[1:], start[3] = lax.optimization_barrier((spread[-1], *inner[1:], start[3]))
+    inner.append(send(inner[1], to_second))
+    final_pieces = start + inner + near(last) + [send(last, to_far)]
     grads = call(
         functools.partial(final_body, last_order, experts, small_rows),
         "final",
@@ -872,14 +876,7 @@
         [((width, local), f32)] * 3
         + [((local, width), f32), ((width,), f32), ((heads, bucket_count), f32)]
         + [((width,), f32), ((experts, width), f32)],
-        matrix,
-        first,
-        second,
-        far,
-        matrix_two,
-        first_two,
-        second_two,
-        far_two,
+        *final_pieces,
         hot,
         scratch=[
             pltpu.VMEM((width, local), f32),

time: 166 us -> 164 us (0.988)
  waiting for transfers between devices: 80.6 us -> 75.6 us
  starting transfers between devices: 49.7 us -> 52.8 us
    ppermute x51 -> x54, waiting for transfers between devices: 80.6 us -> 75.6 us  [send(): return lax.ppermute(array, ('dp', 'tensor'), pairs)]
    ppermute x51 -> x54, starting transfers between devices: 49.7 us -> 52.8 us  [send(): return lax.ppermute(array, ('dp', 'tensor'), pairs)]
  transfers between devices with their start and end apart: 51 -> 54, of which waited for: 31 -> 30; matrix products, arithmetic and copies ran while one was open for 0% -> 0% of each run, Pallas kernels for 13% -> 13%
where the time goes in v5:
time: 164 us
  waiting for transfers between devices  75.6 us (46%)
  starting transfers between devices  52.8 us (32%)
  Pallas kernels  34.5 us (21%)
    ppermute x54, waiting for transfers between devices, send(): return lax.ppermute(array, ('dp', 'tensor'), pairs)  75.6 us
    ppermute x54, starting transfers between devices, send(): return lax.ppermute(array, ('dp', 'tensor'), pairs)  52.8 us
    pallas_call x21, Pallas kernels, call(): pl.pallas_call(body, out_shape=shapes, in_specs=[pl.BlockSpec(memory_spac...  34.5 us
  transfers between devices with their start and end apart: 54, of which 30 were waited for; matrix products, arithmetic and copies ran while one was open for 0% of the time, Pallas kernels for 13%

profile of v5, /device:TPU:0, one launch (start us, length us, event | category | flops | bytes accessed | tf_op | source)
XLA Modules:
  0.0 164.0 jit_solution(5165589206319086572)
XLA Ops:
  2.5 4.1 %collective-permute-start = (bf16[80,384]{1,0:T(8,128)(2,1)S(1)}, bf16[80,384]{1,0:T(8,128)(2,1)S(1)}, u32[]{:S(2)}, u32[]{:S(2)}) collective-permute-start(bf16[80,384]{1,0:T(8,128)(2,1)S(1)} %get-tuple-element.108), channel_id=1, source_target_pairs={{0,16},{1,17},{2,18},{3,19},{4,20},{5,21},{6,22},{7,23},{8,24},{9,... | collective-permute-start | bytes 184328 | tf_op jit(solution)/shard_map/ppermute | solution.py:594
  8.2 3.7 %front.1 = (bf16[256,384]{1,0:T(8,128)(2,1)S(1)}, f32[128,768]{1,0:T(8,128)S(1)}, bf16[128,384]{1,0:T(8,128)(2,1)S(1)}, bf16[128,384]{1,0:T(8,128)(2,1)S(1)}, bf...) custom-call(s32[3]{0:T(128)S(1)} %pad_add_fusion.ids, bf16[128,768]{1,0:T(8,128)(2,1)} %tokens.3, f32[768]{0:T(1024)} %gain.5, ...), custom_call_target="tpu_custom_call" | custom-call | bytes 18000000 | tf_op jit(solution)/shard_map/front/pallas_call | solution.py:53
  17.7 2.4 %collective-permute-start.4 = (bf16[80,384]{1,0:T(8,128)(2,1)S(1)}, bf16[80,384]{1,0:T(8,128)(2,1)S(1)}, u32[]{:S(2)}, u32[]{:S(2)}) collective-permute-start(bf16[80,384]{1,0:T(8,128)(2,1)S(1)} %get-tuple-element.114), channel_id=1, source_target_pairs={{0,16},{1,17},{2,18},{3,19},{4,20},{5,21},{6,22},{7,23},{8,24},{9,... | collective-permute-start | bytes 184328 | tf_op jit(solution)/shard_map/ppermute | solution.py:594
  21.2 4.6 %collective-permute-done.7.refs_9_.refs_1_ = bf16[576,384]{1,0:T(8,128)(2,1)S(1)} collective-permute-done((bf16[576,384]{1,0:T(8,128)(2,1)S(1)}, bf16[576,384]{1,0:T(8,128)(2,1)S(1)}, u32[]{:S(2)}, u32[]{:S(2)}) %collective-permute-start.7) | collective-permute-done | bytes 442400 | tf_op jit(solution)/shard_map/ppermute | solution.py:594
  30.2 5.3 %collective-permute-done.9.refs_1_ = bf16[320,384]{1,0:T(8,128)(2,1)S(1)} collective-permute-done((bf16[320,384]{1,0:T(8,128)(2,1)S(1)}, bf16[320,384]{1,0:T(8,128)(2,1)S(1)}, u32[]{:S(2)}, u32[]{:S(2)}) %collective-permute-start.9) | collective-permute-done | bytes 245792 | tf_op jit(solution)/shard_map/ppermute | solution.py:594
  43.4 1.9 %collective-permute-done.15.refs_7_ = bf16[320,384]{1,0:T(8,128)(2,1)S(1)} collective-permute-done((bf16[320,384]{1,0:T(8,128)(2,1)S(1)}, bf16[320,384]{1,0:T(8,128)(2,1)S(1)}, u32[]{:S(2)}, u32[]{:S(2)}) %collective-permute-start.15) | collective-permute-done | bytes 245792 | tf_op jit(solution)/shard_map/ppermute | solution.py:594
  45.3 3.4 %expert.1 = (bf16[1280,384]{1,0:T(8,128)(2,1)S(1)}, f32[1280,384]{1,0:T(8,128)S(1)}, bf16[1280,384]{1,0:T(8,128)(2,1)S(1)}, bf16[1280,384]{1,0:T(8,128)(2,1)S(1)}) custom-call(s32[3]{0:T(128)S(1)} %pad_add_fusion.ids, bf16[320,384]{1,0:T(8,128)(2,1)S(1)} %join.4.refs_0_, bf16[320,384]{1,0:T(8,128)(2,1)S(1)} %collective-permute-done.9.refs_1_, ...), custom_call_target="tpu_custom_call" | custom-call | bytes 15840000 | tf_op jit(solution)/shard_map/expert/pallas_call | solution.py:53
  49.2 3.8 %expert_back.1 = (bf16[1280,384]{1,0:T(8,128)(2,1)S(1)}, bf16[1280,768]{1,0:T(8,128)(2,1)S(1)}, bf16[1280,384]{1,0:T(8,128)(2,1)S(1)}, bf16[1280,384]{1,0:T(8,128)(2,1)S(1)}) custom-call(s32[3]{0:T(128)S(1)} %pad_add_fusion.ids, bf16[320,384]{1,0:T(8,128)(2,1)S(1)} %join.4.refs_0_, bf16[320,384]{1,0:T(8,128)(2,1)S(1)} %collective-permute-done.9.refs_1_, ...), custom_call_target="tpu_custom_call" | custom-call | bytes 19440000 | tf_op jit(solution)/shard_map/expert_back/pallas_call | solution.py:53
  57.8 5.1 %collective-permute-done.17.received = bf16[640,384]{1,0:T(8,128)(2,1)S(1)} collective-permute-done((bf16[640,384]{1,0:T(8,128)(2,1)S(1)}, bf16[640,384]{1,0:T(8,128)(2,1)S(1)}, u32[]{:S(2)}, u32[]{:S(2)}) %collective-permute-start.17) | collective-permute-done | bytes 491552 | tf_op jit(solution)/shard_map/ppermute | solution.py:594
  64.7 5.9 %collective-permute-done.25.received = bf16[640,384]{1,0:T(8,128)(2,1)S(1)} collective-permute-done((bf16[640,384]{1,0:T(8,128)(2,1)S(1)}, bf16[640,384]{1,0:T(8,128)(2,1)S(1)}, u32[]{:S(2)}, u32[]{:S(2)}) %collective-permute-start.25) | collective-permute-done | bytes 491552 | tf_op jit(solution)/shard_map/ppermute | solution.py:594
  72.4 3.8 %expert_grads.1 = (f32[1,768,384]{2,1,0:T(8,128)}, f32[1,384,768]{2,1,0:T(8,128)}) custom-call(s32[3]{0:T(128)S(1)} %pad_add_fusion.ids, bf16[320,384]{1,0:T(8,128)(2,1)S(1)} %join.4.refs_0_, bf16[320,384]{1,0:T(8,128)(2,1)S(1)} %collective-permute-done.9.refs_1_, bf16[320,384]{1,0:T(8,128)(2,1)S(1)} %collective-permute-done.10.refs_2_, ...), custom_call_target="tpu_custom_call" | custom-call | bytes 14400000 | tf_op jit(solution)/shard_map/expert_grads/pallas_call | solution.py:53
  78.1 2.3 %collective-permute-start.27 = (bf16[160,384]{1,0:T(8,128)(2,1)S(1)}, bf16[160,384]{1,0:T(8,128)(2,1)S(1)}, u32[]{:S(2)}, u32[]{:S(2)}) collective-permute-start(bf16[160,384]{1,0:T(8,128)(2,1)S(1)} %get-tuple-element.149), channel_id=1, source_target_pairs={{0,16},{1,17},{2,18},{3,19},{4,20},{5,21},{6,22},{7,23},{8,24},{9,... | collective-permute-start | bytes 368648 | tf_op jit(solution)/shard_map/ppermute | solution.py:594
  81.6 4.3 %collective-permute-done.27.refs_1_ = bf16[160,384]{1,0:T(8,128)(2,1)S(1)} collective-permute-done((bf16[160,384]{1,0:T(8,128)(2,1)S(1)}, bf16[160,384]{1,0:T(8,128)(2,1)S(1)}, u32[]{:S(2)}, u32[]{:S(2)}) %collective-permute-start.27) | collective-permute-done | bytes 122912 | tf_op jit(solution)/shard_map/ppermute | solution.py:594
  91.6 1.8 %norm_back.1 = (bf16[128,768]{1,0:T(8,128)(2,1)}, f32[128,768]{1,0:T(8,128)S(1)}, bf16[128,768]{1,0:T(8,128)(2,1)S(1)}, f32[5,768]{1,0:T(8,128)S(1)}) custom-call(s32[3]{0:T(128)S(1)} %pad_add_fusion.ids, f32[128,896]{1,0:T(8,128)S(1)} %combine.1.own, f32[128,896]{1,0:T(8,128)S(1)} %collective-permute-done.30.other, ...), custom_call_target="tpu_custom_call" | custom-call | bytes 2880000 | tf_op jit(solution)/shard_map/norm_back/pallas_call | solution.py:53
  93.5 1.9 %attend_back.1 = (bf16[128,384]{1,0:T(8,128)(2,1)S(1)}, bf16[128,384]{1,0:T(8,128)(2,1)S(1)}, bf16[128,384]{1,0:T(8,128)(2,1)S(1)}, bf16[128,384]{1,0:T(8,128)(2...) custom-call(s32[3]{0:T(128)S(1)} %pad_add_fusion.ids, bf16[128,768]{1,0:T(8,128)(2,1)S(1)} %get-tuple-element.156.att, ...), custom_call_target="tpu_custom_call" | custom-call | bytes 9000000 | tf_op jit(solution)/shard_map/attend_back/pallas_call | solution.py:53
  101.6 2.1 %collective-permute-done.34.refs_11_ = bf16[128,384]{1,0:T(8,128)(2,1)S(1)} collective-permute-done((bf16[128,384]{1,0:T(8,128)(2,1)S(1)}, bf16[128,384]{1,0:T(8,128)(2,1)S(1)}, u32[]{:S(2)}, u32[]{:S(2)}) %collective-permute-start.34) | collective-permute-done | bytes 98336 | tf_op jit(solution)/shard_map/ppermute | solution.py:594
  107.0 2.1 %collective-permute-start.39 = (bf16[224,384]{1,0:T(8,128)(2,1)S(1)}, bf16[224,384]{1,0:T(8,128)(2,1)S(1)}, u32[]{:S(2)}, u32[]{:S(2)}) collective-permute-start(bf16[224,384]{1,0:T(8,128)(2,1)S(1)} %get-tuple-element.177), channel_id=1, source_target_pairs={{0,16},{1,17},{2,18},{3,19},{4,20},{5,21},{6,22},{7,23},{8,24},{9,... | collective-permute-start | bytes 516104 | tf_op jit(solution)/shard_map/ppermute | solution.py:594
  110.5 11.6 %collective-permute-done.39.refs_1_ = bf16[224,384]{1,0:T(8,128)(2,1)S(1)} collective-permute-done((bf16[224,384]{1,0:T(8,128)(2,1)S(1)}, bf16[224,384]{1,0:T(8,128)(2,1)S(1)}, u32[]{:S(2)}, u32[]{:S(2)}) %collective-permute-start.39) | collective-permute-done | bytes 172064 | tf_op jit(solution)/shard_map/ppermute | solution.py:594
  126.6 4.0 %collective-permute-start.42 = (bf16[192,384]{1,0:T(8,128)(2,1)S(1)}, bf16[192,384]{1,0:T(8,128)(2,1)S(1)}, u32[]{:S(2)}, u32[]{:S(2)}) collective-permute-start(bf16[192,384]{1,0:T(8,128)(2,1)S(1)} %get-tuple-element.181), channel_id=1, source_target_pairs={{0,16},{1,17},{2,18},{3,19},{4,20},{5,21},{6,22},{7,23},{8,24},{9,... | collective-permute-start | bytes 442376 | tf_op jit(solution)/shard_map/ppermute | solution.py:594
  130.6 6.5 %collective-permute-done.42.refs_0_ = bf16[192,384]{1,0:T(8,128)(2,1)S(1)} collective-permute-done((bf16[192,384]{1,0:T(8,128)(2,1)S(1)}, bf16[192,384]{1,0:T(8,128)(2,1)S(1)}, u32[]{:S(2)}, u32[]{:S(2)}) %collective-permute-start.42) | collective-permute-done | bytes 147488 | tf_op jit(solution)/shard_map/ppermute | solution.py:594
  141.8 6.2 %collective-permute-done.46.refs_8_ = bf16[192,384]{1,0:T(8,128)(2,1)S(1)} collective-permute-done((bf16[192,384]{1,0:T(8,128)(2,1)S(1)}, bf16[192,384]{1,0:T(8,128)(2,1)S(1)}, u32[]{:S(2)}, u32[]{:S(2)}) %collective-permute-start.46) | collective-permute-done | bytes 147488 | tf_op jit(solution)/shard_map/ppermute | solution.py:594
  152.5 3.3 %collective-permute-done.51.refs_9_ = bf16[192,384]{1,0:T(8,128)(2,1)S(1)} collective-permute-done((bf16[192,384]{1,0:T(8,128)(2,1)S(1)}, bf16[192,384]{1,0:T(8,128)(2,1)S(1)}, u32[]{:S(2)}, u32[]{:S(2)}) %collective-permute-start.51) | collective-permute-done | bytes 147488 | tf_op jit(solution)/shard_map/ppermute | solution.py:594
  155.8 5.0 %collective-permute-done.52.refs_10_ = bf16[192,384]{1,0:T(8,128)(2,1)S(1)} collective-permute-done((bf16[192,384]{1,0:T(8,128)(2,1)S(1)}, bf16[192,384]{1,0:T(8,128)(2,1)S(1)}, u32[]{:S(2)}, u32[]{:S(2)}) %collective-permute-start.52) | collective-permute-done | bytes 147488 | tf_op jit(solution)/shard_map/ppermute | solution.py:594
  160.8 3.2 %final.1 = (f32[768,384]{1,0:T(8,128)}, f32[768,384]{1,0:T(8,128)}, f32[768,384]{1,0:T(8,128)}, f32[384,768]{1,0:T(8,128)}, f32[768]{0:T(1024)}, /*index=5*/f32[6,32]{1,0:T(8,128)}, f32[768]{0:T(1024)}, f32[4,768]{1,0:T(4,128)}) custom-call(s32[3]{0:T(128)S(1)} %pad_add_fusion.ids, bf16[224,384]{1,0:T(8,128)(2,1)S(1)} %get-tuple-element.180.refs_0_, ...), custom_call_target="tpu_custom_call" | custom-call | bytes 14040000 | tf_op jit(solution)/shard_map/final/pallas_call | solution.py:53
  (132 shorter events, 64.9 us)
Async XLA Ops:
  2.5 9.4 %collective-permute-start = (bf16[80,384]{1,0:T(8,128)(2,1)S(1)}, bf16[80,384]{1,0:T(8,128)(2,1)S(1)}, u32[]{:S(2)}, u32[]{:S(2)}) collective-permute-start(bf16[80,384]{1,0:T(8,128)(2,1)S(1)} %get-tuple-element.108), channel_id=1, source_target_pairs={{0,16},{1,17},{2,18},{3,19},{4,20},{5,21},{6,22},{7,23},{8,24},{9,... | collective-permute-start | bytes 184328 | tf_op jit(solution)/shard_map/ppermute | solution.py:594
  13.4 12.4 %collective-permute-start.7 = (bf16[576,384]{1,0:T(8,128)(2,1)S(1)}, bf16[576,384]{1,0:T(8,128)(2,1)S(1)}, u32[]{:S(2)}, u32[]{:S(2)}) collective-permute-start(bf16[576,384]{1,0:T(8,128)(2,1)S(1)} %join.3.refs_8_.refs_0_), channel_id=1, source_target_pairs={{0,2},{1,5},{2,0},{3,7},{4,6},{5,1},{6,4},{7,3},{8,10},{9,13},{10,... | collective-permute-start | bytes 1327112 | tf_op jit(solution)/shard_map/ppermute | solution.py:594
  15.0 11.1 %collective-permute-start.8 = (bf16[576,384]{1,0:T(8,128)(2,1)S(1)}, bf16[576,384]{1,0:T(8,128)(2,1)S(1)}, u32[]{:S(2)}, u32[]{:S(2)}) collective-permute-start(bf16[576,384]{1,0:T(8,128)(2,1)S(1)} %join.3.refs_8_.refs_0_), channel_id=1, source_target_pairs={{0,4},{1,3},{2,6},{3,1},{4,0},{5,7},{6,2},{7,5},{8,12},{9,11},{10,... | collective-permute-start | bytes 1327112 | tf_op jit(solution)/shard_map/ppermute | solution.py:594
  17.7 8.4 %collective-permute-start.4 = (bf16[80,384]{1,0:T(8,128)(2,1)S(1)}, bf16[80,384]{1,0:T(8,128)(2,1)S(1)}, u32[]{:S(2)}, u32[]{:S(2)}) collective-permute-start(bf16[80,384]{1,0:T(8,128)(2,1)S(1)} %get-tuple-element.114), channel_id=1, source_target_pairs={{0,16},{1,17},{2,18},{3,19},{4,20},{5,21},{6,22},{7,23},{8,24},{9,... | collective-permute-start | bytes 184328 | tf_op jit(solution)/shard_map/ppermute | solution.py:594
  26.8 8.7 %collective-permute-start.9 = (bf16[320,384]{1,0:T(8,128)(2,1)S(1)}, bf16[320,384]{1,0:T(8,128)(2,1)S(1)}, u32[]{:S(2)}, u32[]{:S(2)}) collective-permute-start(bf16[320,384]{1,0:T(8,128)(2,1)S(1)} %join.4.refs_0_), channel_id=1, source_target_pairs={{0,2},{1,5},{2,0},{3,7},{4,6},{5,1},{6,4},{7,3},{8,10},{9,13},{10,... | collective-permute-start | bytes 737288 | tf_op jit(solution)/shard_map/ppermute | solution.py:594
  28.2 9.1 %collective-permute-start.10 = (bf16[320,384]{1,0:T(8,128)(2,1)S(1)}, bf16[320,384]{1,0:T(8,128)(2,1)S(1)}, u32[]{:S(2)}, u32[]{:S(2)}) collective-permute-start(bf16[320,384]{1,0:T(8,128)(2,1)S(1)} %join.4.refs_0_), channel_id=1, source_target_pairs={{0,4},{1,3},{2,6},{3,1},{4,0},{5,7},{6,2},{7,5},{8,12},{9,11},{10,... | collective-permute-start | bytes 737288 | tf_op jit(solution)/shard_map/ppermute | solution.py:594
  30.0 9.6 %collective-permute-start.19 = (bf16[576,384]{1,0:T(8,128)(2,1)S(1)}, bf16[576,384]{1,0:T(8,128)(2,1)S(1)}, u32[]{:S(2)}, u32[]{:S(2)}) collective-permute-start(bf16[576,384]{1,0:T(8,128)(2,1)S(1)} %collective-permute-done.7.refs_9_.refs_1_), channel_id=1, source_target_pairs={{0,4},{1,3},{2,6},{3,1},{4,0},{5,7},{6,2},{7,5},{8,12},{9,11},{10,... | collective-permute-start | bytes 1327112 | tf_op jit(solution)/shard_map/ppermute | solution.py:594
  37.8 11.4 %collective-permute-start.20 = (bf16[576,384]{1,0:T(8,128)(2,1)S(1)}, bf16[576,384]{1,0:T(8,128)(2,1)S(1)}, u32[]{:S(2)}, u32[]{:S(2)}) collective-permute-start(bf16[576,384]{1,0:T(8,128)(2,1)S(1)} %join.3.refs_8_.refs_0_), channel_id=1, source_target_pairs={{0,1},{1,0},{2,3},{3,2},{4,5},{5,4},{6,7},{7,6},{8,9},{9,8},{10,11... | collective-permute-start | bytes 1327112 | tf_op jit(solution)/shard_map/ppermute | solution.py:594
  39.6 9.6 %collective-permute-start.22 = (bf16[576,384]{1,0:T(8,128)(2,1)S(1)}, bf16[576,384]{1,0:T(8,128)(2,1)S(1)}, u32[]{:S(2)}, u32[]{:S(2)}) collective-permute-start(bf16[576,384]{1,0:T(8,128)(2,1)S(1)} %collective-permute-done.7.refs_9_.refs_1_), channel_id=1, source_target_pairs={{0,1},{1,0},{2,3},{3,2},{4,5},{5,4},{6,7},{7,6},{8,9},{9,8},{10,11... | collective-permute-start | bytes 1327112 | tf_op jit(solution)/shard_map/ppermute | solution.py:594
  54.0 8.9 %collective-permute-start.17 = (bf16[640,384]{1,0:T(8,128)(2,1)S(1)}, bf16[640,384]{1,0:T(8,128)(2,1)S(1)}, u32[]{:S(2)}, u32[]{:S(2)}) collective-permute-start(bf16[640,384]{1,0:T(8,128)(2,1)S(1)} %get-tuple-element.129), channel_id=1, source_target_pairs={{0,2},{1,5},{2,0},{3,7},{4,6},{5,1},{6,4},{7,3},{8,10},{9,13},{10,... | collective-permute-start | bytes 1474568 | tf_op jit(solution)/shard_map/ppermute | solution.py:594
  56.4 14.1 %collective-permute-start.25 = (bf16[640,384]{1,0:T(8,128)(2,1)S(1)}, bf16[640,384]{1,0:T(8,128)(2,1)S(1)}, u32[]{:S(2)}, u32[]{:S(2)}) collective-permute-start(bf16[640,384]{1,0:T(8,128)(2,1)S(1)} %get-tuple-element.138), channel_id=1, source_target_pairs={{0,2},{1,5},{2,0},{3,7},{4,6},{5,1},{6,4},{7,3},{8,10},{9,13},{10,... | collective-permute-start | bytes 1474568 | tf_op jit(solution)/shard_map/ppermute | solution.py:594
  63.5 12.7 %collective-permute-start.18 = (bf16[320,384]{1,0:T(8,128)(2,1)S(1)}, bf16[320,384]{1,0:T(8,128)(2,1)S(1)}, u32[]{:S(2)}, u32[]{:S(2)}) collective-permute-start(bf16[320,384]{1,0:T(8,128)(2,1)S(1)} %get-tuple-element.131), channel_id=1, source_target_pairs={{0,4},{1,3},{2,6},{3,1},{4,0},{5,7},{6,2},{7,5},{8,12},{9,11},{10,... | collective-permute-start | bytes 737288 | tf_op jit(solution)/shard_map/ppermute | solution.py:594
  107.0 15.2 %collective-permute-start.39 = (bf16[224,384]{1,0:T(8,128)(2,1)S(1)}, bf16[224,384]{1,0:T(8,128)(2,1)S(1)}, u32[]{:S(2)}, u32[]{:S(2)}) collective-permute-start(bf16[224,384]{1,0:T(8,128)(2,1)S(1)} %get-tuple-element.177), channel_id=1, source_target_pairs={{0,16},{1,17},{2,18},{3,19},{4,20},{5,21},{6,22},{7,23},{8,24},{9,... | collective-permute-start | bytes 516104 | tf_op jit(solution)/shard_map/ppermute | solution.py:594
  109.1 13.1 %collective-permute-start.40 = (bf16[224,384]{1,0:T(8,128)(2,1)S(1)}, bf16[224,384]{1,0:T(8,128)(2,1)S(1)}, u32[]{:S(2)}, u32[]{:S(2)}) collective-permute-start(bf16[224,384]{1,0:T(8,128)(2,1)S(1)} %get-tuple-element.178), channel_id=1, source_target_pairs={{0,24},{1,25},{2,26},{3,27},{4,28},{5,29},{6,30},{7,31},{8,16},{9,... | collective-permute-start | bytes 516104 | tf_op jit(solution)/shard_map/ppermute | solution.py:594
  110.1 13.3 %collective-permute-start.41 = (bf16[224,384]{1,0:T(8,128)(2,1)S(1)}, bf16[224,384]{1,0:T(8,128)(2,1)S(1)}, u32[]{:S(2)}, u32[]{:S(2)}) collective-permute-start(bf16[224,384]{1,0:T(8,128)(2,1)S(1)} %get-tuple-element.179), channel_id=1, source_target_pairs={{0,8},{1,9},{2,10},{3,11},{4,12},{5,13},{6,14},{7,15},{8,0},{9,1},... | collective-permute-start | bytes 516104 | tf_op jit(solution)/shard_map/ppermute | solution.py:594
  124.1 13.2 %collective-permute-start.44 = (bf16[224,384]{1,0:T(8,128)(2,1)S(1)}, bf16[224,384]{1,0:T(8,128)(2,1)S(1)}, u32[]{:S(2)}, u32[]{:S(2)}) collective-permute-start(bf16[224,384]{1,0:T(8,128)(2,1)S(1)} %get-tuple-element.180.refs_0_), channel_id=1, source_target_pairs={{0,2},{1,5},{2,0},{3,7},{4,6},{5,1},{6,4},{7,3},{8,10},{9,13},{10,... | collective-permute-start | bytes 516104 | tf_op jit(solution)/shard_map/ppermute | solution.py:594
  125.6 11.7 %collective-permute-start.45 = (bf16[224,384]{1,0:T(8,128)(2,1)S(1)}, bf16[224,384]{1,0:T(8,128)(2,1)S(1)}, u32[]{:S(2)}, u32[]{:S(2)}) collective-permute-start(bf16[224,384]{1,0:T(8,128)(2,1)S(1)} %get-tuple-element.180.refs_0_), channel_id=1, source_target_pairs={{0,4},{1,3},{2,6},{3,1},{4,0},{5,7},{6,2},{7,5},{8,12},{9,11},{10,... | collective-permute-start | bytes 516104 | tf_op jit(solution)/shard_map/ppermute | solution.py:594
  126.6 10.5 %collective-permute-start.42 = (bf16[192,384]{1,0:T(8,128)(2,1)S(1)}, bf16[192,384]{1,0:T(8,128)(2,1)S(1)}, u32[]{:S(2)}, u32[]{:S(2)}) collective-permute-start(bf16[192,384]{1,0:T(8,128)(2,1)S(1)} %get-tuple-element.181), channel_id=1, source_target_pairs={{0,16},{1,17},{2,18},{3,19},{4,20},{5,21},{6,22},{7,23},{8,24},{9,... | collective-permute-start | bytes 442376 | tf_op jit(solution)/shard_map/ppermute | solution.py:594
  137.8 10.1 %collective-permute-start.47 = (bf16[384,384]{1,0:T(8,128)(2,1)S(1)}, bf16[384,384]{1,0:T(8,128)(2,1)S(1)}, u32[]{:S(2)}, u32[]{:S(2)}) collective-permute-start(bf16[384,384]{1,0:T(8,128)(2,1)S(1)} %join.5.refs_4_), channel_id=1, source_target_pairs={{0,2},{1,5},{2,0},{3,7},{4,6},{5,1},{6,4},{7,3},{8,10},{9,13},{10,... | collective-permute-start | bytes 884744 | tf_op jit(solution)/shard_map/ppermute | solution.py:594
  138.9 9.1 %collective-permute-start.48 = (bf16[384,384]{1,0:T(8,128)(2,1)S(1)}, bf16[384,384]{1,0:T(8,128)(2,1)S(1)}, u32[]{:S(2)}, u32[]{:S(2)}) collective-permute-start(bf16[384,384]{1,0:T(8,128)(2,1)S(1)} %join.5.refs_4_), channel_id=1, source_target_pairs={{0,4},{1,3},{2,6},{3,1},{4,0},{5,7},{6,2},{7,5},{8,12},{9,11},{10,... | collective-permute-start | bytes 884744 | tf_op jit(solution)/shard_map/ppermute | solution.py:594
  139.8 8.1 %collective-permute-start.49 = (bf16[224,384]{1,0:T(8,128)(2,1)S(1)}, bf16[224,384]{1,0:T(8,128)(2,1)S(1)}, u32[]{:S(2)}, u32[]{:S(2)}) collective-permute-start(bf16[224,384]{1,0:T(8,128)(2,1)S(1)} %collective-permute-done.44.refs_1_), channel_id=1, source_target_pairs={{0,4},{1,3},{2,6},{3,1},{4,0},{5,7},{6,2},{7,5},{8,12},{9,11},{10,... | collective-permute-start | bytes 516104 | tf_op jit(solution)/shard_map/ppermute | solution.py:594
  148.0 12.8 %collective-permute-start.50 = (bf16[384,384]{1,0:T(8,128)(2,1)S(1)}, bf16[384,384]{1,0:T(8,128)(2,1)S(1)}, u32[]{:S(2)}, u32[]{:S(2)}) collective-permute-start(bf16[384,384]{1,0:T(8,128)(2,1)S(1)} %collective-permute-done.47.refs_5_), channel_id=1, source_target_pairs={{0,4},{1,3},{2,6},{3,1},{4,0},{5,7},{6,2},{7,5},{8,12},{9,11},{10,... | collective-permute-start | bytes 884744 | tf_op jit(solution)/shard_map/ppermute | solution.py:594
  150.8 10.0 %collective-permute-start.52 = (bf16[192,384]{1,0:T(8,128)(2,1)S(1)}, bf16[192,384]{1,0:T(8,128)(2,1)S(1)}, u32[]{:S(2)}, u32[]{:S(2)}) collective-permute-start(bf16[192,384]{1,0:T(8,128)(2,1)S(1)} %collective-permute-done.46.refs_8_), channel_id=1, source_target_pairs={{0,4},{1,3},{2,6},{3,1},{4,0},{5,7},{6,2},{7,5},{8,12},{9,11},{10,... | collective-permute-start | bytes 442376 | tf_op jit(solution)/shard_map/ppermute | solution.py:594
  151.1 9.7 %collective-permute-start.53 = (bf16[192,384]{1,0:T(8,128)(2,1)S(1)}, bf16[192,384]{1,0:T(8,128)(2,1)S(1)}, u32[]{:S(2)}, u32[]{:S(2)}) collective-permute-start(bf16[192,384]{1,0:T(8,128)(2,1)S(1)} %collective-permute-done.46.refs_8_), channel_id=1, source_target_pairs={{0,6},{1,7},{2,4},{3,5},{4,2},{5,3},{6,0},{7,1},{8,14},{9,15},{10,... | collective-permute-start | bytes 442376 | tf_op jit(solution)/shard_map/ppermute | solution.py:594
  (43 other events, 340.0 us)

commit v6 on v5

--- a/solution.py
+++ b/solution.py
@@ -866,7 +866,7 @@
     start[1:] = joint[-2:]
     start.append(send(start[1], to_second))
     inner = near(join(joint[:-2]))
-    last, *inner[1:], start[3] = lax.optimization_barrier((spread[-1], *inner[1:], start[3]))
+    last, start[3] = lax.optimization_barrier((spread[-1], start[3]))
     inner.append(send(inner[1], to_second))
     final_pieces = start + inner + near(last) + [send(last, to_far)]
     grads = call(

time: 164 us -> 163 us (level)
  waiting for transfers between devices: 75.6 us -> 73.2 us
    ppermute x54, waiting for transfers between devices: 75.6 us -> 73.2 us  [send(): return lax.ppermute(array, ('dp', 'tensor'), pairs)]
where the time goes in v6:
time: 163 us; the launch traced here: 162 us
  waiting for transfers between devices  73.2 us (45%)
  starting transfers between devices  53.6 us (33%)
  Pallas kernels  34.5 us (21%)
    ppermute x54, waiting for transfers between devices, send(): return lax.ppermute(array, ('dp', 'tensor'), pairs)  73.2 us
    ppermute x54, starting transfers between devices, send(): return lax.ppermute(array, ('dp', 'tensor'), pairs)  53.6 us
    pallas_call x21, Pallas kernels, call(): pl.pallas_call(body, out_shape=shapes, in_specs=[pl.BlockSpec(memory_spac...  34.5 us
  transfers between devices with their start and end apart: 54, of which 30 were waited for; matrix products, arithmetic and copies ran while one was open for 0% of the time, Pallas kernels for 13%

profile of v6, /device:TPU:0, one launch (start us, length us, event | category | flops | bytes accessed | tf_op | source)
XLA Modules:
  0.0 162.4 jit_solution(8138908935855372434)
XLA Ops:
  2.5 4.1 %collective-permute-start = (bf16[80,384]{1,0:T(8,128)(2,1)S(1)}, bf16[80,384]{1,0:T(8,128)(2,1)S(1)}, u32[]{:S(2)}, u32[]{:S(2)}) collective-permute-start(bf16[80,384]{1,0:T(8,128)(2,1)S(1)} %get-tuple-element.106), channel_id=1, source_target_pairs={{0,16},{1,17},{2,18},{3,19},{4,20},{5,21},{6,22},{7,23},{8,24},{9,... | collective-permute-start | bytes 184328 | tf_op jit(solution)/shard_map/ppermute | solution.py:594
  8.2 3.7 %front.1 = (bf16[256,384]{1,0:T(8,128)(2,1)S(1)}, f32[128,768]{1,0:T(8,128)S(1)}, bf16[128,384]{1,0:T(8,128)(2,1)S(1)}, bf16[128,384]{1,0:T(8,128)(2,1)S(1)}, bf...) custom-call(s32[3]{0:T(128)S(1)} %pad_add_fusion.ids, bf16[128,768]{1,0:T(8,128)(2,1)} %tokens.3, f32[768]{0:T(1024)} %gain.5, ...), custom_call_target="tpu_custom_call" | custom-call | bytes 18000000 | tf_op jit(solution)/shard_map/front/pallas_call | solution.py:53
  17.7 2.4 %collective-permute-start.4 = (bf16[80,384]{1,0:T(8,128)(2,1)S(1)}, bf16[80,384]{1,0:T(8,128)(2,1)S(1)}, u32[]{:S(2)}, u32[]{:S(2)}) collective-permute-start(bf16[80,384]{1,0:T(8,128)(2,1)S(1)} %get-tuple-element.112), channel_id=1, source_target_pairs={{0,16},{1,17},{2,18},{3,19},{4,20},{5,21},{6,22},{7,23},{8,24},{9,... | collective-permute-start | bytes 184328 | tf_op jit(solution)/shard_map/ppermute | solution.py:594
  21.2 4.6 %collective-permute-done.7.refs_9_.refs_1_ = bf16[576,384]{1,0:T(8,128)(2,1)S(1)} collective-permute-done((bf16[576,384]{1,0:T(8,128)(2,1)S(1)}, bf16[576,384]{1,0:T(8,128)(2,1)S(1)}, u32[]{:S(2)}, u32[]{:S(2)}) %collective-permute-start.7) | collective-permute-done | bytes 442400 | tf_op jit(solution)/shard_map/ppermute | solution.py:594
  30.2 5.3 %collective-permute-done.9.refs_1_ = bf16[320,384]{1,0:T(8,128)(2,1)S(1)} collective-permute-done((bf16[320,384]{1,0:T(8,128)(2,1)S(1)}, bf16[320,384]{1,0:T(8,128)(2,1)S(1)}, u32[]{:S(2)}, u32[]{:S(2)}) %collective-permute-start.9) | collective-permute-done | bytes 245792 | tf_op jit(solution)/shard_map/ppermute | solution.py:594
  43.4 1.9 %collective-permute-done.15.refs_7_ = bf16[320,384]{1,0:T(8,128)(2,1)S(1)} collective-permute-done((bf16[320,384]{1,0:T(8,128)(2,1)S(1)}, bf16[320,384]{1,0:T(8,128)(2,1)S(1)}, u32[]{:S(2)}, u32[]{:S(2)}) %collective-permute-start.15) | collective-permute-done | bytes 245792 | tf_op jit(solution)/shard_map/ppermute | solution.py:594
  45.3 3.4 %expert.1 = (bf16[1280,384]{1,0:T(8,128)(2,1)S(1)}, f32[1280,384]{1,0:T(8,128)S(1)}, bf16[1280,384]{1,0:T(8,128)(2,1)S(1)}, bf16[1280,384]{1,0:T(8,128)(2,1)S(1)}) custom-call(s32[3]{0:T(128)S(1)} %pad_add_fusion.ids, bf16[320,384]{1,0:T(8,128)(2,1)S(1)} %join.4.refs_0_, bf16[320,384]{1,0:T(8,128)(2,1)S(1)} %collective-permute-done.9.refs_1_, ...), custom_call_target="tpu_custom_call" | custom-call | bytes 15840000 | tf_op jit(solution)/shard_map/expert/pallas_call | solution.py:53
  49.2 3.8 %expert_back.1 = (bf16[1280,384]{1,0:T(8,128)(2,1)S(1)}, bf16[1280,768]{1,0:T(8,128)(2,1)S(1)}, bf16[1280,384]{1,0:T(8,128)(2,1)S(1)}, bf16[1280,384]{1,0:T(8,128)(2,1)S(1)}) custom-call(s32[3]{0:T(128)S(1)} %pad_add_fusion.ids, bf16[320,384]{1,0:T(8,128)(2,1)S(1)} %join.4.refs_0_, bf16[320,384]{1,0:T(8,128)(2,1)S(1)} %collective-permute-done.9.refs_1_, ...), custom_call_target="tpu_custom_call" | custom-call | bytes 19440000 | tf_op jit(solution)/shard_map/expert_back/pallas_call | solution.py:53
  57.8 5.1 %collective-permute-done.17.received = bf16[640,384]{1,0:T(8,128)(2,1)S(1)} collective-permute-done((bf16[640,384]{1,0:T(8,128)(2,1)S(1)}, bf16[640,384]{1,0:T(8,128)(2,1)S(1)}, u32[]{:S(2)}, u32[]{:S(2)}) %collective-permute-start.17) | collective-permute-done | bytes 491552 | tf_op jit(solution)/shard_map/ppermute | solution.py:594
  64.7 5.9 %collective-permute-done.25.received = bf16[640,384]{1,0:T(8,128)(2,1)S(1)} collective-permute-done((bf16[640,384]{1,0:T(8,128)(2,1)S(1)}, bf16[640,384]{1,0:T(8,128)(2,1)S(1)}, u32[]{:S(2)}, u32[]{:S(2)}) %collective-permute-start.25) | collective-permute-done | bytes 491552 | tf_op jit(solution)/shard_map/ppermute | solution.py:594
  72.4 3.8 %expert_grads.1 = (f32[1,768,384]{2,1,0:T(8,128)}, f32[1,384,768]{2,1,0:T(8,128)}) custom-call(s32[3]{0:T(128)S(1)} %pad_add_fusion.ids, bf16[320,384]{1,0:T(8,128)(2,1)S(1)} %join.4.refs_0_, bf16[320,384]{1,0:T(8,128)(2,1)S(1)} %collective-permute-done.9.refs_1_, bf16[320,384]{1,0:T(8,128)(2,1)S(1)} %collective-permute-done.10.refs_2_, ...), custom_call_target="tpu_custom_call" | custom-call | bytes 14400000 | tf_op jit(solution)/shard_map/expert_grads/pallas_call | solution.py:53
  78.1 2.3 %collective-permute-start.27 = (bf16[160,384]{1,0:T(8,128)(2,1)S(1)}, bf16[160,384]{1,0:T(8,128)(2,1)S(1)}, u32[]{:S(2)}, u32[]{:S(2)}) collective-permute-start(bf16[160,384]{1,0:T(8,128)(2,1)S(1)} %get-tuple-element.147), channel_id=1, source_target_pairs={{0,16},{1,17},{2,18},{3,19},{4,20},{5,21},{6,22},{7,23},{8,24},{9,... | collective-permute-start | bytes 368648 | tf_op jit(solution)/shard_map/ppermute | solution.py:594
  81.6 4.3 %collective-permute-done.27.refs_1_ = bf16[160,384]{1,0:T(8,128)(2,1)S(1)} collective-permute-done((bf16[160,384]{1,0:T(8,128)(2,1)S(1)}, bf16[160,384]{1,0:T(8,128)(2,1)S(1)}, u32[]{:S(2)}, u32[]{:S(2)}) %collective-permute-start.27) | collective-permute-done | bytes 122912 | tf_op jit(solution)/shard_map/ppermute | solution.py:594
  93.5 1.9 %attend_back.1 = (bf16[128,384]{1,0:T(8,128)(2,1)S(1)}, bf16[128,384]{1,0:T(8,128)(2,1)S(1)}, bf16[128,384]{1,0:T(8,128)(2,1)S(1)}, bf16[128,384]{1,0:T(8,128)(2...) custom-call(s32[3]{0:T(128)S(1)} %pad_add_fusion.ids, bf16[128,768]{1,0:T(8,128)(2,1)S(1)} %get-tuple-element.154.att, ...), custom_call_target="tpu_custom_call" | custom-call | bytes 9000000 | tf_op jit(solution)/shard_map/attend_back/pallas_call | solution.py:53
  101.6 2.1 %collective-permute-done.34.refs_11_ = bf16[128,384]{1,0:T(8,128)(2,1)S(1)} collective-permute-done((bf16[128,384]{1,0:T(8,128)(2,1)S(1)}, bf16[128,384]{1,0:T(8,128)(2,1)S(1)}, u32[]{:S(2)}, u32[]{:S(2)}) %collective-permute-start.34) | collective-permute-done | bytes 98336 | tf_op jit(solution)/shard_map/ppermute | solution.py:594
  107.0 2.1 %collective-permute-start.39 = (bf16[224,384]{1,0:T(8,128)(2,1)S(1)}, bf16[224,384]{1,0:T(8,128)(2,1)S(1)}, u32[]{:S(2)}, u32[]{:S(2)}) collective-permute-start(bf16[224,384]{1,0:T(8,128)(2,1)S(1)} %get-tuple-element.175), channel_id=1, source_target_pairs={{0,16},{1,17},{2,18},{3,19},{4,20},{5,21},{6,22},{7,23},{8,24},{9,... | collective-permute-start | bytes 516104 | tf_op jit(solution)/shard_map/ppermute | solution.py:594
  110.5 11.6 %collective-permute-done.39.refs_1_ = bf16[224,384]{1,0:T(8,128)(2,1)S(1)} collective-permute-done((bf16[224,384]{1,0:T(8,128)(2,1)S(1)}, bf16[224,384]{1,0:T(8,128)(2,1)S(1)}, u32[]{:S(2)}, u32[]{:S(2)}) %collective-permute-start.39) | collective-permute-done | bytes 172064 | tf_op jit(solution)/shard_map/ppermute | solution.py:594
  126.6 4.0 %collective-permute-start.42 = (bf16[192,384]{1,0:T(8,128)(2,1)S(1)}, bf16[192,384]{1,0:T(8,128)(2,1)S(1)}, u32[]{:S(2)}, u32[]{:S(2)}) collective-permute-start(bf16[192,384]{1,0:T(8,128)(2,1)S(1)} %get-tuple-element.179), channel_id=1, source_target_pairs={{0,16},{1,17},{2,18},{3,19},{4,20},{5,21},{6,22},{7,23},{8,24},{9,... | collective-permute-start | bytes 442376 | tf_op jit(solution)/shard_map/ppermute | solution.py:594
  130.6 6.5 %collective-permute-done.42.refs_0_ = bf16[192,384]{1,0:T(8,128)(2,1)S(1)} collective-permute-done((bf16[192,384]{1,0:T(8,128)(2,1)S(1)}, bf16[192,384]{1,0:T(8,128)(2,1)S(1)}, u32[]{:S(2)}, u32[]{:S(2)}) %collective-permute-start.42) | collective-permute-done | bytes 147488 | tf_op jit(solution)/shard_map/ppermute | solution.py:594
  141.8 6.0 %collective-permute-done.48.refs_5_ = bf16[384,384]{1,0:T(8,128)(2,1)S(1)} collective-permute-done((bf16[384,384]{1,0:T(8,128)(2,1)S(1)}, bf16[384,384]{1,0:T(8,128)(2,1)S(1)}, u32[]{:S(2)}, u32[]{:S(2)}) %collective-permute-start.48) | collective-permute-done | bytes 294944 | tf_op jit(solution)/shard_map/ppermute | solution.py:594
  150.9 2.2 %collective-permute-start.53 = (bf16[192,384]{1,0:T(8,128)(2,1)S(1)}, bf16[192,384]{1,0:T(8,128)(2,1)S(1)}, u32[]{:S(2)}, u32[]{:S(2)}) collective-permute-start(bf16[192,384]{1,0:T(8,128)(2,1)S(1)} %collective-permute-done.46.refs_8_), channel_id=1, source_target_pairs={{0,6},{1,7},{2,4},{3,5},{4,2},{5,3},{6,0},{7,1},{8,14},{9,15},{10,... | collective-permute-start | bytes 442376 | tf_op jit(solution)/shard_map/ppermute | solution.py:594
  153.1 3.3 %collective-permute-done.51.refs_9_ = bf16[192,384]{1,0:T(8,128)(2,1)S(1)} collective-permute-done((bf16[192,384]{1,0:T(8,128)(2,1)S(1)}, bf16[192,384]{1,0:T(8,128)(2,1)S(1)}, u32[]{:S(2)}, u32[]{:S(2)}) %collective-permute-start.51) | collective-permute-done | bytes 147488 | tf_op jit(solution)/shard_map/ppermute | solution.py:594
  156.4 2.9 %collective-permute-done.52.refs_10_ = bf16[192,384]{1,0:T(8,128)(2,1)S(1)} collective-permute-done((bf16[192,384]{1,0:T(8,128)(2,1)S(1)}, bf16[192,384]{1,0:T(8,128)(2,1)S(1)}, u32[]{:S(2)}, u32[]{:S(2)}) %collective-permute-start.52) | collective-permute-done | bytes 147488 | tf_op jit(solution)/shard_map/ppermute | solution.py:594
  159.3 3.2 %final.1 = (f32[768,384]{1,0:T(8,128)}, f32[768,384]{1,0:T(8,128)}, f32[768,384]{1,0:T(8,128)}, f32[384,768]{1,0:T(8,128)}, f32[768]{0:T(1024)}, /*index=5*/f32[6,32]{1,0:T(8,128)}, f32[768]{0:T(1024)}, f32[4,768]{1,0:T(4,128)}) custom-call(s32[3]{0:T(128)S(1)} %pad_add_fusion.ids, bf16[224,384]{1,0:T(8,128)(2,1)S(1)} %get-tuple-element.178.refs_0_, ...), custom_call_target="tpu_custom_call" | custom-call | bytes 14040000 | tf_op jit(solution)/shard_map/final/pallas_call | solution.py:53
  (132 shorter events, 65.3 us)
Async XLA Ops:
  2.5 9.4 %collective-permute-start = (bf16[80,384]{1,0:T(8,128)(2,1)S(1)}, bf16[80,384]{1,0:T(8,128)(2,1)S(1)}, u32[]{:S(2)}, u32[]{:S(2)}) collective-permute-start(bf16[80,384]{1,0:T(8,128)(2,1)S(1)} %get-tuple-element.106), channel_id=1, source_target_pairs={{0,16},{1,17},{2,18},{3,19},{4,20},{5,21},{6,22},{7,23},{8,24},{9,... | collective-permute-start | bytes 184328 | tf_op jit(solution)/shard_map/ppermute | solution.py:594
  13.4 12.4 %collective-permute-start.7 = (bf16[576,384]{1,0:T(8,128)(2,1)S(1)}, bf16[576,384]{1,0:T(8,128)(2,1)S(1)}, u32[]{:S(2)}, u32[]{:S(2)}) collective-permute-start(bf16[576,384]{1,0:T(8,128)(2,1)S(1)} %join.3.refs_8_.refs_0_), channel_id=1, source_target_pairs={{0,2},{1,5},{2,0},{3,7},{4,6},{5,1},{6,4},{7,3},{8,10},{9,13},{10,... | collective-permute-start | bytes 1327112 | tf_op jit(solution)/shard_map/ppermute | solution.py:594
  15.0 11.1 %collective-permute-start.8 = (bf16[576,384]{1,0:T(8,128)(2,1)S(1)}, bf16[576,384]{1,0:T(8,128)(2,1)S(1)}, u32[]{:S(2)}, u32[]{:S(2)}) collective-permute-start(bf16[576,384]{1,0:T(8,128)(2,1)S(1)} %join.3.refs_8_.refs_0_), channel_id=1, source_target_pairs={{0,4},{1,3},{2,6},{3,1},{4,0},{5,7},{6,2},{7,5},{8,12},{9,11},{10,... | collective-permute-start | bytes 1327112 | tf_op jit(solution)/shard_map/ppermute | solution.py:594
  17.7 8.4 %collective-permute-start.4 = (bf16[80,384]{1,0:T(8,128)(2,1)S(1)}, bf16[80,384]{1,0:T(8,128)(2,1)S(1)}, u32[]{:S(2)}, u32[]{:S(2)}) collective-permute-start(bf16[80,384]{1,0:T(8,128)(2,1)S(1)} %get-tuple-element.112), channel_id=1, source_target_pairs={{0,16},{1,17},{2,18},{3,19},{4,20},{5,21},{6,22},{7,23},{8,24},{9,... | collective-permute-start | bytes 184328 | tf_op jit(solution)/shard_map/ppermute | solution.py:594
  26.8 8.7 %collective-permute-start.9 = (bf16[320,384]{1,0:T(8,128)(2,1)S(1)}, bf16[320,384]{1,0:T(8,128)(2,1)S(1)}, u32[]{:S(2)}, u32[]{:S(2)}) collective-permute-start(bf16[320,384]{1,0:T(8,128)(2,1)S(1)} %join.4.refs_0_), channel_id=1, source_target_pairs={{0,2},{1,5},{2,0},{3,7},{4,6},{5,1},{6,4},{7,3},{8,10},{9,13},{10,... | collective-permute-start | bytes 737288 | tf_op jit(solution)/shard_map/ppermute | solution.py:594
  28.2 9.1 %collective-permute-start.10 = (bf16[320,384]{1,0:T(8,128)(2,1)S(1)}, bf16[320,384]{1,0:T(8,128)(2,1)S(1)}, u32[]{:S(2)}, u32[]{:S(2)}) collective-permute-start(bf16[320,384]{1,0:T(8,128)(2,1)S(1)} %join.4.refs_0_), channel_id=1, source_target_pairs={{0,4},{1,3},{2,6},{3,1},{4,0},{5,7},{6,2},{7,5},{8,12},{9,11},{10,... | collective-permute-start | bytes 737288 | tf_op jit(solution)/shard_map/ppermute | solution.py:594
  30.0 9.6 %collective-permute-start.19 = (bf16[576,384]{1,0:T(8,128)(2,1)S(1)}, bf16[576,384]{1,0:T(8,128)(2,1)S(1)}, u32[]{:S(2)}, u32[]{:S(2)}) collective-permute-start(bf16[576,384]{1,0:T(8,128)(2,1)S(1)} %collective-permute-done.7.refs_9_.refs_1_), channel_id=1, source_target_pairs={{0,4},{1,3},{2,6},{3,1},{4,0},{5,7},{6,2},{7,5},{8,12},{9,11},{10,... | collective-permute-start | bytes 1327112 | tf_op jit(solution)/shard_map/ppermute | solution.py:594
  37.8 11.4 %collective-permute-start.20 = (bf16[576,384]{1,0:T(8,128)(2,1)S(1)}, bf16[576,384]{1,0:T(8,128)(2,1)S(1)}, u32[]{:S(2)}, u32[]{:S(2)}) collective-permute-start(bf16[576,384]{1,0:T(8,128)(2,1)S(1)} %join.3.refs_8_.refs_0_), channel_id=1, source_target_pairs={{0,1},{1,0},{2,3},{3,2},{4,5},{5,4},{6,7},{7,6},{8,9},{9,8},{10,11... | collective-permute-start | bytes 1327112 | tf_op jit(solution)/shard_map/ppermute | solution.py:594
  39.6 9.6 %collective-permute-start.22 = (bf16[576,384]{1,0:T(8,128)(2,1)S(1)}, bf16[576,384]{1,0:T(8,128)(2,1)S(1)}, u32[]{:S(2)}, u32[]{:S(2)}) collective-permute-start(bf16[576,384]{1,0:T(8,128)(2,1)S(1)} %collective-permute-done.7.refs_9_.refs_1_), channel_id=1, source_target_pairs={{0,1},{1,0},{2,3},{3,2},{4,5},{5,4},{6,7},{7,6},{8,9},{9,8},{10,11... | collective-permute-start | bytes 1327112 | tf_op jit(solution)/shard_map/ppermute | solution.py:594
  54.0 8.9 %collective-permute-start.17 = (bf16[640,384]{1,0:T(8,128)(2,1)S(1)}, bf16[640,384]{1,0:T(8,128)(2,1)S(1)}, u32[]{:S(2)}, u32[]{:S(2)}) collective-permute-start(bf16[640,384]{1,0:T(8,128)(2,1)S(1)} %get-tuple-element.127), channel_id=1, source_target_pairs={{0,2},{1,5},{2,0},{3,7},{4,6},{5,1},{6,4},{7,3},{8,10},{9,13},{10,... | collective-permute-start | bytes 1474568 | tf_op jit(solution)/shard_map/ppermute | solution.py:594
  56.4 14.1 %collective-permute-start.25 = (bf16[640,384]{1,0:T(8,128)(2,1)S(1)}, bf16[640,384]{1,0:T(8,128)(2,1)S(1)}, u32[]{:S(2)}, u32[]{:S(2)}) collective-permute-start(bf16[640,384]{1,0:T(8,128)(2,1)S(1)} %get-tuple-element.136), channel_id=1, source_target_pairs={{0,2},{1,5},{2,0},{3,7},{4,6},{5,1},{6,4},{7,3},{8,10},{9,13},{10,... | collective-permute-start | bytes 1474568 | tf_op jit(solution)/shard_map/ppermute | solution.py:594
  63.5 12.7 %collective-permute-start.18 = (bf16[320,384]{1,0:T(8,128)(2,1)S(1)}, bf16[320,384]{1,0:T(8,128)(2,1)S(1)}, u32[]{:S(2)}, u32[]{:S(2)}) collective-permute-start(bf16[320,384]{1,0:T(8,128)(2,1)S(1)} %get-tuple-element.129), channel_id=1, source_target_pairs={{0,4},{1,3},{2,6},{3,1},{4,0},{5,7},{6,2},{7,5},{8,12},{9,11},{10,... | collective-permute-start | bytes 737288 | tf_op jit(solution)/shard_map/ppermute | solution.py:594
  107.0 15.2 %collective-permute-start.39 = (bf16[224,384]{1,0:T(8,128)(2,1)S(1)}, bf16[224,384]{1,0:T(8,128)(2,1)S(1)}, u32[]{:S(2)}, u32[]{:S(2)}) collective-permute-start(bf16[224,384]{1,0:T(8,128)(2,1)S(1)} %get-tuple-element.175), channel_id=1, source_target_pairs={{0,16},{1,17},{2,18},{3,19},{4,20},{5,21},{6,22},{7,23},{8,24},{9,... | collective-permute-start | bytes 516104 | tf_op jit(solution)/shard_map/ppermute | solution.py:594
  109.1 13.1 %collective-permute-start.40 = (bf16[224,384]{1,0:T(8,128)(2,1)S(1)}, bf16[224,384]{1,0:T(8,128)(2,1)S(1)}, u32[]{:S(2)}, u32[]{:S(2)}) collective-permute-start(bf16[224,384]{1,0:T(8,128)(2,1)S(1)} %get-tuple-element.176), channel_id=1, source_target_pairs={{0,24},{1,25},{2,26},{3,27},{4,28},{5,29},{6,30},{7,31},{8,16},{9,... | collective-permute-start | bytes 516104 | tf_op jit(solution)/shard_map/ppermute | solution.py:594
  110.1 13.3 %collective-permute-start.41 = (bf16[224,384]{1,0:T(8,128)(2,1)S(1)}, bf16[224,384]{1,0:T(8,128)(2,1)S(1)}, u32[]{:S(2)}, u32[]{:S(2)}) collective-permute-start(bf16[224,384]{1,0:T(8,128)(2,1)S(1)} %get-tuple-element.177), channel_id=1, source_target_pairs={{0,8},{1,9},{2,10},{3,11},{4,12},{5,13},{6,14},{7,15},{8,0},{9,1},... | collective-permute-start | bytes 516104 | tf_op jit(solution)/shard_map/ppermute | solution.py:594
  124.1 13.2 %collective-permute-start.44 = (bf16[224,384]{1,0:T(8,128)(2,1)S(1)}, bf16[224,384]{1,0:T(8,128)(2,1)S(1)}, u32[]{:S(2)}, u32[]{:S(2)}) collective-permute-start(bf16[224,384]{1,0:T(8,128)(2,1)S(1)} %get-tuple-element.178.refs_0_), channel_id=1, source_target_pairs={{0,2},{1,5},{2,0},{3,7},{4,6},{5,1},{6,4},{7,3},{8,10},{9,13},{10,... | collective-permute-start | bytes 516104 | tf_op jit(solution)/shard_map/ppermute | solution.py:594
  125.6 11.7 %collective-permute-start.45 = (bf16[224,384]{1,0:T(8,128)(2,1)S(1)}, bf16[224,384]{1,0:T(8,128)(2,1)S(1)}, u32[]{:S(2)}, u32[]{:S(2)}) collective-permute-start(bf16[224,384]{1,0:T(8,128)(2,1)S(1)} %get-tuple-element.178.refs_0_), channel_id=1, source_target_pairs={{0,4},{1,3},{2,6},{3,1},{4,0},{5,7},{6,2},{7,5},{8,12},{9,11},{10,... | collective-permute-start | bytes 516104 | tf_op jit(solution)/shard_map/ppermute | solution.py:594
  126.6 10.5 %collective-permute-start.42 = (bf16[192,384]{1,0:T(8,128)(2,1)S(1)}, bf16[192,384]{1,0:T(8,128)(2,1)S(1)}, u32[]{:S(2)}, u32[]{:S(2)}) collective-permute-start(bf16[192,384]{1,0:T(8,128)(2,1)S(1)} %get-tuple-element.179), channel_id=1, source_target_pairs={{0,16},{1,17},{2,18},{3,19},{4,20},{5,21},{6,22},{7,23},{8,24},{9,... | collective-permute-start | bytes 442376 | tf_op jit(solution)/shard_map/ppermute | solution.py:594
  137.8 9.9 %collective-permute-start.48 = (bf16[384,384]{1,0:T(8,128)(2,1)S(1)}, bf16[384,384]{1,0:T(8,128)(2,1)S(1)}, u32[]{:S(2)}, u32[]{:S(2)}) collective-permute-start(bf16[384,384]{1,0:T(8,128)(2,1)S(1)} %join.5.refs_4_), channel_id=1, source_target_pairs={{0,2},{1,5},{2,0},{3,7},{4,6},{5,1},{6,4},{7,3},{8,10},{9,13},{10,... | collective-permute-start | bytes 884744 | tf_op jit(solution)/shard_map/ppermute | solution.py:594
  138.9 10.7 %collective-permute-start.47 = (bf16[224,384]{1,0:T(8,128)(2,1)S(1)}, bf16[224,384]{1,0:T(8,128)(2,1)S(1)}, u32[]{:S(2)}, u32[]{:S(2)}) collective-permute-start(bf16[224,384]{1,0:T(8,128)(2,1)S(1)} %collective-permute-done.44.refs_1_), channel_id=1, source_target_pairs={{0,4},{1,3},{2,6},{3,1},{4,0},{5,7},{6,2},{7,5},{8,12},{9,11},{10,... | collective-permute-start | bytes 516104 | tf_op jit(solution)/shard_map/ppermute | solution.py:594
  139.8 9.7 %collective-permute-start.46 = (bf16[192,384]{1,0:T(8,128)(2,1)S(1)}, bf16[192,384]{1,0:T(8,128)(2,1)S(1)}, u32[]{:S(2)}, u32[]{:S(2)}) collective-permute-start(bf16[192,384]{1,0:T(8,128)(2,1)S(1)} %get-tuple-element.179), channel_id=1, source_target_pairs={{0,24},{1,25},{2,26},{3,27},{4,28},{5,29},{6,30},{7,31},{8,16},{9,... | collective-permute-start | bytes 442376 | tf_op jit(solution)/shard_map/ppermute | solution.py:594
  140.6 12.5 %collective-permute-start.49 = (bf16[384,384]{1,0:T(8,128)(2,1)S(1)}, bf16[384,384]{1,0:T(8,128)(2,1)S(1)}, u32[]{:S(2)}, u32[]{:S(2)}) collective-permute-start(bf16[384,384]{1,0:T(8,128)(2,1)S(1)} %join.5.refs_4_), channel_id=1, source_target_pairs={{0,4},{1,3},{2,6},{3,1},{4,0},{5,7},{6,2},{7,5},{8,12},{9,11},{10,... | collective-permute-start | bytes 884744 | tf_op jit(solution)/shard_map/ppermute | solution.py:594
  147.8 11.5 %collective-permute-start.50 = (bf16[384,384]{1,0:T(8,128)(2,1)S(1)}, bf16[384,384]{1,0:T(8,128)(2,1)S(1)}, u32[]{:S(2)}, u32[]{:S(2)}) collective-permute-start(bf16[384,384]{1,0:T(8,128)(2,1)S(1)} %collective-permute-done.48.refs_5_), channel_id=1, source_target_pairs={{0,4},{1,3},{2,6},{3,1},{4,0},{5,7},{6,2},{7,5},{8,12},{9,11},{10,... | collective-permute-start | bytes 884744 | tf_op jit(solution)/shard_map/ppermute | solution.py:594
  149.7 9.5 %collective-permute-start.52 = (bf16[192,384]{1,0:T(8,128)(2,1)S(1)}, bf16[192,384]{1,0:T(8,128)(2,1)S(1)}, u32[]{:S(2)}, u32[]{:S(2)}) collective-permute-start(bf16[192,384]{1,0:T(8,128)(2,1)S(1)} %collective-permute-done.46.refs_8_), channel_id=1, source_target_pairs={{0,4},{1,3},{2,6},{3,1},{4,0},{5,7},{6,2},{7,5},{8,12},{9,11},{10,... | collective-permute-start | bytes 442376 | tf_op jit(solution)/shard_map/ppermute | solution.py:594
  (43 other events, 339.8 us)

commit v7 on v6

--- a/solution.py
+++ b/solution.py
@@ -862,10 +862,9 @@
         return [matrix, send(matrix, to_first), send(matrix, to_second)]
 
     start = near(code)
-    joint = lax.optimization_barrier((*spread[1:-1], *start[1:]))
-    start[1:] = joint[-2:]
+    *joint, start[1] = lax.optimization_barrier((*spread[1:-1], start[1]))
     start.append(send(start[1], to_second))
-    inner = near(join(joint[:-2]))
+    inner = near(join(joint))
     last, start[3] = lax.optimization_barrier((spread[-1], start[3]))
     inner.append(send(inner[1], to_second))
     final_pieces = start + inner + near(last) + [send(last, to_far)]

time: 163 us -> 162 us (level)
  transfers between devices with their start and end apart: 54 -> 54, of which waited for: 30 -> 31; matrix products, arithmetic and copies ran while one was open for 0% -> 0% of each run, Pallas kernels for 13% -> 13%
where the time goes in v7:
time: 162 us
  waiting for transfers between devices  73.1 us (45%)
  starting transfers between devices  53 us (33%)
  Pallas kernels  34.5 us (21%)
    ppermute x54, waiting for transfers between devices, send(): return lax.ppermute(array, ('dp', 'tensor'), pairs)  73.1 us
    ppermute x54, starting transfers between devices, send(): return lax.ppermute(array, ('dp', 'tensor'), pairs)  53 us
    pallas_call x21, Pallas kernels, call(): pl.pallas_call(body, out_shape=shapes, in_specs=[pl.BlockSpec(memory_spac...  34.5 us
  transfers between devices with their start and end apart: 54, of which 31 were waited for; matrix products, arithmetic and copies ran while one was open for 0% of the time, Pallas kernels for 13%

profile of v7, /device:TPU:0, one launch (start us, length us, event | category | flops | bytes accessed | tf_op | source)
XLA Modules:
  0.0 161.7 jit_solution(18116646131625829643)
XLA Ops:
  2.5 4.1 %collective-permute-start = (bf16[80,384]{1,0:T(8,128)(2,1)S(1)}, bf16[80,384]{1,0:T(8,128)(2,1)S(1)}, u32[]{:S(2)}, u32[]{:S(2)}) collective-permute-start(bf16[80,384]{1,0:T(8,128)(2,1)S(1)} %get-tuple-element.105), channel_id=1, source_target_pairs={{0,16},{1,17},{2,18},{3,19},{4,20},{5,21},{6,22},{7,23},{8,24},{9,... | collective-permute-start | bytes 184328 | tf_op jit(solution)/shard_map/ppermute | solution.py:594
  8.2 3.7 %front.1 = (bf16[256,384]{1,0:T(8,128)(2,1)S(1)}, f32[128,768]{1,0:T(8,128)S(1)}, bf16[128,384]{1,0:T(8,128)(2,1)S(1)}, bf16[128,384]{1,0:T(8,128)(2,1)S(1)}, bf...) custom-call(s32[3]{0:T(128)S(1)} %pad_add_fusion.ids, bf16[128,768]{1,0:T(8,128)(2,1)} %tokens.3, f32[768]{0:T(1024)} %gain.5, ...), custom_call_target="tpu_custom_call" | custom-call | bytes 18000000 | tf_op jit(solution)/shard_map/front/pallas_call | solution.py:53
  17.7 2.4 %collective-permute-start.4 = (bf16[80,384]{1,0:T(8,128)(2,1)S(1)}, bf16[80,384]{1,0:T(8,128)(2,1)S(1)}, u32[]{:S(2)}, u32[]{:S(2)}) collective-permute-start(bf16[80,384]{1,0:T(8,128)(2,1)S(1)} %get-tuple-element.111), channel_id=1, source_target_pairs={{0,16},{1,17},{2,18},{3,19},{4,20},{5,21},{6,22},{7,23},{8,24},{9,... | collective-permute-start | bytes 184328 | tf_op jit(solution)/shard_map/ppermute | solution.py:594
  21.2 4.6 %collective-permute-done.7.refs_9_.refs_1_ = bf16[576,384]{1,0:T(8,128)(2,1)S(1)} collective-permute-done((bf16[576,384]{1,0:T(8,128)(2,1)S(1)}, bf16[576,384]{1,0:T(8,128)(2,1)S(1)}, u32[]{:S(2)}, u32[]{:S(2)}) %collective-permute-start.7) | collective-permute-done | bytes 442400 | tf_op jit(solution)/shard_map/ppermute | solution.py:594
  30.2 5.3 %collective-permute-done.9.refs_1_ = bf16[320,384]{1,0:T(8,128)(2,1)S(1)} collective-permute-done((bf16[320,384]{1,0:T(8,128)(2,1)S(1)}, bf16[320,384]{1,0:T(8,128)(2,1)S(1)}, u32[]{:S(2)}, u32[]{:S(2)}) %collective-permute-start.9) | collective-permute-done | bytes 245792 | tf_op jit(solution)/shard_map/ppermute | solution.py:594
  43.4 1.9 %collective-permute-done.15.refs_7_ = bf16[320,384]{1,0:T(8,128)(2,1)S(1)} collective-permute-done((bf16[320,384]{1,0:T(8,128)(2,1)S(1)}, bf16[320,384]{1,0:T(8,128)(2,1)S(1)}, u32[]{:S(2)}, u32[]{:S(2)}) %collective-permute-start.15) | collective-permute-done | bytes 245792 | tf_op jit(solution)/shard_map/ppermute | solution.py:594
  45.3 3.4 %expert.1 = (bf16[1280,384]{1,0:T(8,128)(2,1)S(1)}, f32[1280,384]{1,0:T(8,128)S(1)}, bf16[1280,384]{1,0:T(8,128)(2,1)S(1)}, bf16[1280,384]{1,0:T(8,128)(2,1)S(1)}) custom-call(s32[3]{0:T(128)S(1)} %pad_add_fusion.ids, bf16[320,384]{1,0:T(8,128)(2,1)S(1)} %join.4.refs_0_, bf16[320,384]{1,0:T(8,128)(2,1)S(1)} %collective-permute-done.9.refs_1_, ...), custom_call_target="tpu_custom_call" | custom-call | bytes 15840000 | tf_op jit(solution)/shard_map/expert/pallas_call | solution.py:53
  49.2 3.8 %expert_back.1 = (bf16[1280,384]{1,0:T(8,128)(2,1)S(1)}, bf16[1280,768]{1,0:T(8,128)(2,1)S(1)}, bf16[1280,384]{1,0:T(8,128)(2,1)S(1)}, bf16[1280,384]{1,0:T(8,128)(2,1)S(1)}) custom-call(s32[3]{0:T(128)S(1)} %pad_add_fusion.ids, bf16[320,384]{1,0:T(8,128)(2,1)S(1)} %join.4.refs_0_, bf16[320,384]{1,0:T(8,128)(2,1)S(1)} %collective-permute-done.9.refs_1_, ...), custom_call_target="tpu_custom_call" | custom-call | bytes 19440000 | tf_op jit(solution)/shard_map/expert_back/pallas_call | solution.py:53
  57.8 5.1 %collective-permute-done.17.received = bf16[640,384]{1,0:T(8,128)(2,1)S(1)} collective-permute-done((bf16[640,384]{1,0:T(8,128)(2,1)S(1)}, bf16[640,384]{1,0:T(8,128)(2,1)S(1)}, u32[]{:S(2)}, u32[]{:S(2)}) %collective-permute-start.17) | collective-permute-done | bytes 491552 | tf_op jit(solution)/shard_map/ppermute | solution.py:594
  64.7 5.9 %collective-permute-done.25.received = bf16[640,384]{1,0:T(8,128)(2,1)S(1)} collective-permute-done((bf16[640,384]{1,0:T(8,128)(2,1)S(1)}, bf16[640,384]{1,0:T(8,128)(2,1)S(1)}, u32[]{:S(2)}, u32[]{:S(2)}) %collective-permute-start.25) | collective-permute-done | bytes 491552 | tf_op jit(solution)/shard_map/ppermute | solution.py:594
  72.4 3.8 %expert_grads.1 = (f32[1,768,384]{2,1,0:T(8,128)}, f32[1,384,768]{2,1,0:T(8,128)}) custom-call(s32[3]{0:T(128)S(1)} %pad_add_fusion.ids, bf16[320,384]{1,0:T(8,128)(2,1)S(1)} %join.4.refs_0_, bf16[320,384]{1,0:T(8,128)(2,1)S(1)} %collective-permute-done.9.refs_1_, bf16[320,384]{1,0:T(8,128)(2,1)S(1)} %collective-permute-done.10.refs_2_, ...), custom_call_target="tpu_custom_call" | custom-call | bytes 14400000 | tf_op jit(solution)/shard_map/expert_grads/pallas_call | solution.py:53
  78.1 2.3 %collective-permute-start.27 = (bf16[160,384]{1,0:T(8,128)(2,1)S(1)}, bf16[160,384]{1,0:T(8,128)(2,1)S(1)}, u32[]{:S(2)}, u32[]{:S(2)}) collective-permute-start(bf16[160,384]{1,0:T(8,128)(2,1)S(1)} %get-tuple-element.146), channel_id=1, source_target_pairs={{0,16},{1,17},{2,18},{3,19},{4,20},{5,21},{6,22},{7,23},{8,24},{9,... | collective-permute-start | bytes 368648 | tf_op jit(solution)/shard_map/ppermute | solution.py:594
  81.6 4.3 %collective-permute-done.27.refs_1_ = bf16[160,384]{1,0:T(8,128)(2,1)S(1)} collective-permute-done((bf16[160,384]{1,0:T(8,128)(2,1)S(1)}, bf16[160,384]{1,0:T(8,128)(2,1)S(1)}, u32[]{:S(2)}, u32[]{:S(2)}) %collective-permute-start.27) | collective-permute-done | bytes 122912 | tf_op jit(solution)/shard_map/ppermute | solution.py:594
  93.5 1.9 %attend_back.1 = (bf16[128,384]{1,0:T(8,128)(2,1)S(1)}, bf16[128,384]{1,0:T(8,128)(2,1)S(1)}, bf16[128,384]{1,0:T(8,128)(2,1)S(1)}, bf16[128,384]{1,0:T(8,128)(2...) custom-call(s32[3]{0:T(128)S(1)} %pad_add_fusion.ids, bf16[128,768]{1,0:T(8,128)(2,1)S(1)} %get-tuple-element.153.att, ...), custom_call_target="tpu_custom_call" | custom-call | bytes 9000000 | tf_op jit(solution)/shard_map/attend_back/pallas_call | solution.py:53
  101.6 2.1 %collective-permute-done.34.refs_11_ = bf16[128,384]{1,0:T(8,128)(2,1)S(1)} collective-permute-done((bf16[128,384]{1,0:T(8,128)(2,1)S(1)}, bf16[128,384]{1,0:T(8,128)(2,1)S(1)}, u32[]{:S(2)}, u32[]{:S(2)}) %collective-permute-start.34) | collective-permute-done | bytes 98336 | tf_op jit(solution)/shard_map/ppermute | solution.py:594
  107.0 2.1 %collective-permute-start.39 = (bf16[224,384]{1,0:T(8,128)(2,1)S(1)}, bf16[224,384]{1,0:T(8,128)(2,1)S(1)}, u32[]{:S(2)}, u32[]{:S(2)}) collective-permute-start(bf16[224,384]{1,0:T(8,128)(2,1)S(1)} %get-tuple-element.174), channel_id=1, source_target_pairs={{0,16},{1,17},{2,18},{3,19},{4,20},{5,21},{6,22},{7,23},{8,24},{9,... | collective-permute-start | bytes 516104 | tf_op jit(solution)/shard_map/ppermute | solution.py:594
  110.5 11.6 %collective-permute-done.39.refs_1_ = bf16[224,384]{1,0:T(8,128)(2,1)S(1)} collective-permute-done((bf16[224,384]{1,0:T(8,128)(2,1)S(1)}, bf16[224,384]{1,0:T(8,128)(2,1)S(1)}, u32[]{:S(2)}, u32[]{:S(2)}) %collective-permute-start.39) | collective-permute-done | bytes 172064 | tf_op jit(solution)/shard_map/ppermute | solution.py:594
  125.6 4.2 %collective-permute-start.42 = (bf16[192,384]{1,0:T(8,128)(2,1)S(1)}, bf16[192,384]{1,0:T(8,128)(2,1)S(1)}, u32[]{:S(2)}, u32[]{:S(2)}) collective-permute-start(bf16[192,384]{1,0:T(8,128)(2,1)S(1)} %get-tuple-element.178), channel_id=1, source_target_pairs={{0,16},{1,17},{2,18},{3,19},{4,20},{5,21},{6,22},{7,23},{8,24},{9,... | collective-permute-start | bytes 442376 | tf_op jit(solution)/shard_map/ppermute | solution.py:594
  129.7 6.5 %collective-permute-done.42.refs_0_ = bf16[192,384]{1,0:T(8,128)(2,1)S(1)} collective-permute-done((bf16[192,384]{1,0:T(8,128)(2,1)S(1)}, bf16[192,384]{1,0:T(8,128)(2,1)S(1)}, u32[]{:S(2)}, u32[]{:S(2)}) %collective-permute-start.42) | collective-permute-done | bytes 147488 | tf_op jit(solution)/shard_map/ppermute | solution.py:594
  138.0 1.9 %collective-permute-start.47 = (bf16[224,384]{1,0:T(8,128)(2,1)S(1)}, bf16[224,384]{1,0:T(8,128)(2,1)S(1)}, u32[]{:S(2)}, u32[]{:S(2)}) collective-permute-start(bf16[224,384]{1,0:T(8,128)(2,1)S(1)} %collective-permute-done.44.refs_1_), channel_id=1, source_target_pairs={{0,4},{1,3},{2,6},{3,1},{4,0},{5,7},{6,2},{7,5},{8,12},{9,11},{10,... | collective-permute-start | bytes 516104 | tf_op jit(solution)/shard_map/ppermute | solution.py:594
  142.2 4.9 %collective-permute-done.48.refs_5_ = bf16[384,384]{1,0:T(8,128)(2,1)S(1)} collective-permute-done((bf16[384,384]{1,0:T(8,128)(2,1)S(1)}, bf16[384,384]{1,0:T(8,128)(2,1)S(1)}, u32[]{:S(2)}, u32[]{:S(2)}) %collective-permute-start.48) | collective-permute-done | bytes 294944 | tf_op jit(solution)/shard_map/ppermute | solution.py:594
  151.5 3.3 %collective-permute-done.51.refs_9_ = bf16[192,384]{1,0:T(8,128)(2,1)S(1)} collective-permute-done((bf16[192,384]{1,0:T(8,128)(2,1)S(1)}, bf16[192,384]{1,0:T(8,128)(2,1)S(1)}, u32[]{:S(2)}, u32[]{:S(2)}) %collective-permute-start.51) | collective-permute-done | bytes 147488 | tf_op jit(solution)/shard_map/ppermute | solution.py:594
  155.5 3.1 %collective-permute-done.53.refs_11_ = bf16[192,384]{1,0:T(8,128)(2,1)S(1)} collective-permute-done((bf16[192,384]{1,0:T(8,128)(2,1)S(1)}, bf16[192,384]{1,0:T(8,128)(2,1)S(1)}, u32[]{:S(2)}, u32[]{:S(2)}) %collective-permute-start.53) | collective-permute-done | bytes 147488 | tf_op jit(solution)/shard_map/ppermute | solution.py:594
  158.6 3.2 %final.1 = (f32[768,384]{1,0:T(8,128)}, f32[768,384]{1,0:T(8,128)}, f32[768,384]{1,0:T(8,128)}, f32[384,768]{1,0:T(8,128)}, f32[768]{0:T(1024)}, /*index=5*/f32[6,32]{1,0:T(8,128)}, f32[768]{0:T(1024)}, f32[4,768]{1,0:T(4,128)}) custom-call(s32[3]{0:T(128)S(1)} %pad_add_fusion.ids, bf16[224,384]{1,0:T(8,128)(2,1)S(1)} %get-tuple-element.177.refs_0_, ...), custom_call_target="tpu_custom_call" | custom-call | bytes 14040000 | tf_op jit(solution)/shard_map/final/pallas_call | solution.py:53
  (132 shorter events, 65.6 us)
Async XLA Ops:
  2.5 9.4 %collective-permute-start = (bf16[80,384]{1,0:T(8,128)(2,1)S(1)}, bf16[80,384]{1,0:T(8,128)(2,1)S(1)}, u32[]{:S(2)}, u32[]{:S(2)}) collective-permute-start(bf16[80,384]{1,0:T(8,128)(2,1)S(1)} %get-tuple-element.105), channel_id=1, source_target_pairs={{0,16},{1,17},{2,18},{3,19},{4,20},{5,21},{6,22},{7,23},{8,24},{9,... | collective-permute-start | bytes 184328 | tf_op jit(solution)/shard_map/ppermute | solution.py:594
  13.4 12.4 %collective-permute-start.7 = (bf16[576,384]{1,0:T(8,128)(2,1)S(1)}, bf16[576,384]{1,0:T(8,128)(2,1)S(1)}, u32[]{:S(2)}, u32[]{:S(2)}) collective-permute-start(bf16[576,384]{1,0:T(8,128)(2,1)S(1)} %join.3.refs_8_.refs_0_), channel_id=1, source_target_pairs={{0,2},{1,5},{2,0},{3,7},{4,6},{5,1},{6,4},{7,3},{8,10},{9,13},{10,... | collective-permute-start | bytes 1327112 | tf_op jit(solution)/shard_map/ppermute | solution.py:594
  15.0 11.1 %collective-permute-start.8 = (bf16[576,384]{1,0:T(8,128)(2,1)S(1)}, bf16[576,384]{1,0:T(8,128)(2,1)S(1)}, u32[]{:S(2)}, u32[]{:S(2)}) collective-permute-start(bf16[576,384]{1,0:T(8,128)(2,1)S(1)} %join.3.refs_8_.refs_0_), channel_id=1, source_target_pairs={{0,4},{1,3},{2,6},{3,1},{4,0},{5,7},{6,2},{7,5},{8,12},{9,11},{10,... | collective-permute-start | bytes 1327112 | tf_op jit(solution)/shard_map/ppermute | solution.py:594
  17.7 8.4 %collective-permute-start.4 = (bf16[80,384]{1,0:T(8,128)(2,1)S(1)}, bf16[80,384]{1,0:T(8,128)(2,1)S(1)}, u32[]{:S(2)}, u32[]{:S(2)}) collective-permute-start(bf16[80,384]{1,0:T(8,128)(2,1)S(1)} %get-tuple-element.111), channel_id=1, source_target_pairs={{0,16},{1,17},{2,18},{3,19},{4,20},{5,21},{6,22},{7,23},{8,24},{9,... | collective-permute-start | bytes 184328 | tf_op jit(solution)/shard_map/ppermute | solution.py:594
  26.8 8.7 %collective-permute-start.9 = (bf16[320,384]{1,0:T(8,128)(2,1)S(1)}, bf16[320,384]{1,0:T(8,128)(2,1)S(1)}, u32[]{:S(2)}, u32[]{:S(2)}) collective-permute-start(bf16[320,384]{1,0:T(8,128)(2,1)S(1)} %join.4.refs_0_), channel_id=1, source_target_pairs={{0,2},{1,5},{2,0},{3,7},{4,6},{5,1},{6,4},{7,3},{8,10},{9,13},{10,... | collective-permute-start | bytes 737288 | tf_op jit(solution)/shard_map/ppermute | solution.py:594
  28.2 9.1 %collective-permute-start.10 = (bf16[320,384]{1,0:T(8,128)(2,1)S(1)}, bf16[320,384]{1,0:T(8,128)(2,1)S(1)}, u32[]{:S(2)}, u32[]{:S(2)}) collective-permute-start(bf16[320,384]{1,0:T(8,128)(2,1)S(1)} %join.4.refs_0_), channel_id=1, source_target_pairs={{0,4},{1,3},{2,6},{3,1},{4,0},{5,7},{6,2},{7,5},{8,12},{9,11},{10,... | collective-permute-start | bytes 737288 | tf_op jit(solution)/shard_map/ppermute | solution.py:594
  30.0 9.6 %collective-permute-start.19 = (bf16[576,384]{1,0:T(8,128)(2,1)S(1)}, bf16[576,384]{1,0:T(8,128)(2,1)S(1)}, u32[]{:S(2)}, u32[]{:S(2)}) collective-permute-start(bf16[576,384]{1,0:T(8,128)(2,1)S(1)} %collective-permute-done.7.refs_9_.refs_1_), channel_id=1, source_target_pairs={{0,4},{1,3},{2,6},{3,1},{4,0},{5,7},{6,2},{7,5},{8,12},{9,11},{10,... | collective-permute-start | bytes 1327112 | tf_op jit(solution)/shard_map/ppermute | solution.py:594
  37.8 11.4 %collective-permute-start.20 = (bf16[576,384]{1,0:T(8,128)(2,1)S(1)}, bf16[576,384]{1,0:T(8,128)(2,1)S(1)}, u32[]{:S(2)}, u32[]{:S(2)}) collective-permute-start(bf16[576,384]{1,0:T(8,128)(2,1)S(1)} %join.3.refs_8_.refs_0_), channel_id=1, source_target_pairs={{0,1},{1,0},{2,3},{3,2},{4,5},{5,4},{6,7},{7,6},{8,9},{9,8},{10,11... | collective-permute-start | bytes 1327112 | tf_op jit(solution)/shard_map/ppermute | solution.py:594
  39.6 9.6 %collective-permute-start.22 = (bf16[576,384]{1,0:T(8,128)(2,1)S(1)}, bf16[576,384]{1,0:T(8,128)(2,1)S(1)}, u32[]{:S(2)}, u32[]{:S(2)}) collective-permute-start(bf16[576,384]{1,0:T(8,128)(2,1)S(1)} %collective-permute-done.7.refs_9_.refs_1_), channel_id=1, source_target_pairs={{0,1},{1,0},{2,3},{3,2},{4,5},{5,4},{6,7},{7,6},{8,9},{9,8},{10,11... | collective-permute-start | bytes 1327112 | tf_op jit(solution)/shard_map/ppermute | solution.py:594
  54.0 8.9 %collective-permute-start.17 = (bf16[640,384]{1,0:T(8,128)(2,1)S(1)}, bf16[640,384]{1,0:T(8,128)(2,1)S(1)}, u32[]{:S(2)}, u32[]{:S(2)}) collective-permute-start(bf16[640,384]{1,0:T(8,128)(2,1)S(1)} %get-tuple-element.126), channel_id=1, source_target_pairs={{0,2},{1,5},{2,0},{3,7},{4,6},{5,1},{6,4},{7,3},{8,10},{9,13},{10,... | collective-permute-start | bytes 1474568 | tf_op jit(solution)/shard_map/ppermute | solution.py:594
  56.4 14.1 %collective-permute-start.25 = (bf16[640,384]{1,0:T(8,128)(2,1)S(1)}, bf16[640,384]{1,0:T(8,128)(2,1)S(1)}, u32[]{:S(2)}, u32[]{:S(2)}) collective-permute-start(bf16[640,384]{1,0:T(8,128)(2,1)S(1)} %get-tuple-element.135), channel_id=1, source_target_pairs={{0,2},{1,5},{2,0},{3,7},{4,6},{5,1},{6,4},{7,3},{8,10},{9,13},{10,... | collective-permute-start | bytes 1474568 | tf_op jit(solution)/shard_map/ppermute | solution.py:594
  63.5 12.7 %collective-permute-start.18 = (bf16[320,384]{1,0:T(8,128)(2,1)S(1)}, bf16[320,384]{1,0:T(8,128)(2,1)S(1)}, u32[]{:S(2)}, u32[]{:S(2)}) collective-permute-start(bf16[320,384]{1,0:T(8,128)(2,1)S(1)} %get-tuple-element.128), channel_id=1, source_target_pairs={{0,4},{1,3},{2,6},{3,1},{4,0},{5,7},{6,2},{7,5},{8,12},{9,11},{10,... | collective-permute-start | bytes 737288 | tf_op jit(solution)/shard_map/ppermute | solution.py:594
  107.0 15.2 %collective-permute-start.39 = (bf16[224,384]{1,0:T(8,128)(2,1)S(1)}, bf16[224,384]{1,0:T(8,128)(2,1)S(1)}, u32[]{:S(2)}, u32[]{:S(2)}) collective-permute-start(bf16[224,384]{1,0:T(8,128)(2,1)S(1)} %get-tuple-element.174), channel_id=1, source_target_pairs={{0,16},{1,17},{2,18},{3,19},{4,20},{5,21},{6,22},{7,23},{8,24},{9,... | collective-permute-start | bytes 516104 | tf_op jit(solution)/shard_map/ppermute | solution.py:594
  109.1 13.1 %collective-permute-start.40 = (bf16[224,384]{1,0:T(8,128)(2,1)S(1)}, bf16[224,384]{1,0:T(8,128)(2,1)S(1)}, u32[]{:S(2)}, u32[]{:S(2)}) collective-permute-start(bf16[224,384]{1,0:T(8,128)(2,1)S(1)} %get-tuple-element.175), channel_id=1, source_target_pairs={{0,24},{1,25},{2,26},{3,27},{4,28},{5,29},{6,30},{7,31},{8,16},{9,... | collective-permute-start | bytes 516104 | tf_op jit(solution)/shard_map/ppermute | solution.py:594
  110.1 13.3 %collective-permute-start.41 = (bf16[224,384]{1,0:T(8,128)(2,1)S(1)}, bf16[224,384]{1,0:T(8,128)(2,1)S(1)}, u32[]{:S(2)}, u32[]{:S(2)}) collective-permute-start(bf16[224,384]{1,0:T(8,128)(2,1)S(1)} %get-tuple-element.176), channel_id=1, source_target_pairs={{0,8},{1,9},{2,10},{3,11},{4,12},{5,13},{6,14},{7,15},{8,0},{9,1},... | collective-permute-start | bytes 516104 | tf_op jit(solution)/shard_map/ppermute | solution.py:594
  124.1 12.5 %collective-permute-start.44 = (bf16[224,384]{1,0:T(8,128)(2,1)S(1)}, bf16[224,384]{1,0:T(8,128)(2,1)S(1)}, u32[]{:S(2)}, u32[]{:S(2)}) collective-permute-start(bf16[224,384]{1,0:T(8,128)(2,1)S(1)} %get-tuple-element.177.refs_0_), channel_id=1, source_target_pairs={{0,2},{1,5},{2,0},{3,7},{4,6},{5,1},{6,4},{7,3},{8,10},{9,13},{10,... | collective-permute-start | bytes 516104 | tf_op jit(solution)/shard_map/ppermute | solution.py:594
  125.6 10.7 %collective-permute-start.42 = (bf16[192,384]{1,0:T(8,128)(2,1)S(1)}, bf16[192,384]{1,0:T(8,128)(2,1)S(1)}, u32[]{:S(2)}, u32[]{:S(2)}) collective-permute-start(bf16[192,384]{1,0:T(8,128)(2,1)S(1)} %get-tuple-element.178), channel_id=1, source_target_pairs={{0,16},{1,17},{2,18},{3,19},{4,20},{5,21},{6,22},{7,23},{8,24},{9,... | collective-permute-start | bytes 442376 | tf_op jit(solution)/shard_map/ppermute | solution.py:594
  137.1 10.0 %collective-permute-start.48 = (bf16[384,384]{1,0:T(8,128)(2,1)S(1)}, bf16[384,384]{1,0:T(8,128)(2,1)S(1)}, u32[]{:S(2)}, u32[]{:S(2)}) collective-permute-start(bf16[384,384]{1,0:T(8,128)(2,1)S(1)} %join.5.refs_4_), channel_id=1, source_target_pairs={{0,2},{1,5},{2,0},{3,7},{4,6},{5,1},{6,4},{7,3},{8,10},{9,13},{10,... | collective-permute-start | bytes 884744 | tf_op jit(solution)/shard_map/ppermute | solution.py:594
  138.0 10.0 %collective-permute-start.47 = (bf16[224,384]{1,0:T(8,128)(2,1)S(1)}, bf16[224,384]{1,0:T(8,128)(2,1)S(1)}, u32[]{:S(2)}, u32[]{:S(2)}) collective-permute-start(bf16[224,384]{1,0:T(8,128)(2,1)S(1)} %collective-permute-done.44.refs_1_), channel_id=1, source_target_pairs={{0,4},{1,3},{2,6},{3,1},{4,0},{5,7},{6,2},{7,5},{8,12},{9,11},{10,... | collective-permute-start | bytes 516104 | tf_op jit(solution)/shard_map/ppermute | solution.py:594
  139.9 10.0 %collective-permute-start.45 = (bf16[224,384]{1,0:T(8,128)(2,1)S(1)}, bf16[224,384]{1,0:T(8,128)(2,1)S(1)}, u32[]{:S(2)}, u32[]{:S(2)}) collective-permute-start(bf16[224,384]{1,0:T(8,128)(2,1)S(1)} %get-tuple-element.177.refs_0_), channel_id=1, source_target_pairs={{0,4},{1,3},{2,6},{3,1},{4,0},{5,7},{6,2},{7,5},{8,12},{9,11},{10,... | collective-permute-start | bytes 516104 | tf_op jit(solution)/shard_map/ppermute | solution.py:594
  140.0 8.0 %collective-permute-start.46 = (bf16[192,384]{1,0:T(8,128)(2,1)S(1)}, bf16[192,384]{1,0:T(8,128)(2,1)S(1)}, u32[]{:S(2)}, u32[]{:S(2)}) collective-permute-start(bf16[192,384]{1,0:T(8,128)(2,1)S(1)} %get-tuple-element.178), channel_id=1, source_target_pairs={{0,24},{1,25},{2,26},{3,27},{4,28},{5,29},{6,30},{7,31},{8,16},{9,... | collective-permute-start | bytes 442376 | tf_op jit(solution)/shard_map/ppermute | solution.py:594
  141.4 10.2 %collective-permute-start.49 = (bf16[384,384]{1,0:T(8,128)(2,1)S(1)}, bf16[384,384]{1,0:T(8,128)(2,1)S(1)}, u32[]{:S(2)}, u32[]{:S(2)}) collective-permute-start(bf16[384,384]{1,0:T(8,128)(2,1)S(1)} %join.5.refs_4_), channel_id=1, source_target_pairs={{0,4},{1,3},{2,6},{3,1},{4,0},{5,7},{6,2},{7,5},{8,12},{9,11},{10,... | collective-permute-start | bytes 884744 | tf_op jit(solution)/shard_map/ppermute | solution.py:594
  147.1 11.4 %collective-permute-start.50 = (bf16[384,384]{1,0:T(8,128)(2,1)S(1)}, bf16[384,384]{1,0:T(8,128)(2,1)S(1)}, u32[]{:S(2)}, u32[]{:S(2)}) collective-permute-start(bf16[384,384]{1,0:T(8,128)(2,1)S(1)} %collective-permute-done.48.refs_5_), channel_id=1, source_target_pairs={{0,4},{1,3},{2,6},{3,1},{4,0},{5,7},{6,2},{7,5},{8,12},{9,11},{10,... | collective-permute-start | bytes 884744 | tf_op jit(solution)/shard_map/ppermute | solution.py:594
  149.9 8.6 %collective-permute-start.53 = (bf16[192,384]{1,0:T(8,128)(2,1)S(1)}, bf16[192,384]{1,0:T(8,128)(2,1)S(1)}, u32[]{:S(2)}, u32[]{:S(2)}) collective-permute-start(bf16[192,384]{1,0:T(8,128)(2,1)S(1)} %collective-permute-done.46.refs_8_), channel_id=1, source_target_pairs={{0,6},{1,7},{2,4},{3,5},{4,2},{5,3},{6,0},{7,1},{8,14},{9,15},{10,... | collective-permute-start | bytes 442376 | tf_op jit(solution)/shard_map/ppermute | solution.py:594
  (43 other events, 336.5 us)
